TPU v7x, 128 devices: a whole 4x4x4 slice. The times are simulated.
128 devices in a mesh: gx: 64 (over y, x, z_hi, core), gy: 2 (over z_lo).
Axes of the slice: x: 4, y: 4, z: 4 (z_hi: 2, z_lo: 2; z = z_hi * 2 + z_lo), core: 2. Of those that a mesh axis runs over, the one named last changes fastest.
Arguments:
- adjoint_in: float32 [3, 1024, 128, 256], P(None, 'gx', 'gy'), may hold values from -6 to 6
- checkpoints: bfloat16 [2, 16384, 3, 2048], P(None, ('gx', 'gy')), may hold values from -4 to 4
- send_owner: int32 [16384], P(('gx', 'gy')), may hold values from 0 to 127, as said below
- receive_rows: int32 [16384], P(('gx', 'gy')), may hold values from 0 to 255, as said below
- block_columns: int32 [4096, 8], P(('gx', 'gy')), may hold values from 0 to 35
- eddy_blocks: bfloat16 [8, 128, 128], replicated, may hold values from -0.1875 to 0.1875
- thrust: float32 [80], replicated, may hold values from 0.4 to 1
- yaw_angle: float32 [80], replicated, may hold values from -0.5 to 0.5
- turbine_place: float32 [3, 80], replicated, may hold values from 0 to 1
- turbine_tile: int32 [80], replicated, may hold values from 0 to 127
- fringe_rows: int32 [128], replicated, may hold values from 0 to 1023, as said below
Outputs:
- adjoint_out: float32 [3, 1024, 128, 256], P(None, 'gx', 'gy')
- control_gradient: float32 [2, 80], replicated
Inputs may be any that keep to these rules, and one draw needn't show every extreme that they name: `send_owner`: each storage tile holds 128 slots; at most 2 of its slots name one owner, exactly 2 for some owners; every owner is named by 128 slots in all. `receive_rows`: for each owner the 128 entries name each row storage*2+rank of a slot sent to it exactly once. `fringe_rows`: distinct rows.
All inputs are finite; a program needn't handle non-finite values.
Results may differ from a plain program's by a relative error of at most 0.00086.
Values may be sent and summed in bfloat16 or wider, within the bound.
A program may use at most 128 MiB of HBM per device.

v0:
```python
import functools

import jax
import jax.numpy as jnp
from jax import lax
from jax.experimental import pallas as pl
from jax.experimental.pallas import tpu as pltpu
from jax.sharding import PartitionSpec as P

MESH = pl.DeviceIdType.MESH

PB = 128
KB = 8
CAP = 2
NZB = 2


TIME_STEP = 0.25
BASE_VISC = 0.1
EDDY_COEF = 0.5
KERNEL_WIDTH = 1.5
FRINGE_KEEP = 0.5


def gather_sum_kernel(count_y, total, part_ref, out_ref, rows, send_sem, recv_sem):
    me = lax.axis_index("gx") * count_y + lax.axis_index("gy")

    def device(i):
        other = lax.rem(me + i, total)
        return (other // count_y, other % count_y)

    barrier = pltpu.get_barrier_semaphore()

    def greet(i, carry):
        pl.semaphore_signal(barrier, inc=1, device_id=device(i), device_id_type=MESH)
        return carry

    lax.fori_loop(1, total, greet, 0)
    pl.semaphore_wait(barrier, total - 1)
    rows[me] = part_ref[...]

    def send(i, carry):
        pltpu.make_async_remote_copy(
            src_ref=part_ref,
            dst_ref=rows.at[me],
            send_sem=send_sem,
            recv_sem=recv_sem,
            device_id=device(i),
            device_id_type=MESH,
        ).start()
        return carry

    lax.fori_loop(1, total, send, 0)
    everything = pltpu.make_async_remote_copy(
        src_ref=rows.at[pl.ds(0, total - 1)],
        dst_ref=rows.at[pl.ds(0, total - 1)],
        send_sem=send_sem,
        recv_sem=recv_sem,
        device_id=device(1),
        device_id_type=MESH,
    )
    everything.wait_send()
    everything.wait_recv()
    out_ref[...] = jnp.sum(rows[...], axis=0)


def gather_sum(part):
    count_y = lax.axis_size("gy")
    total = lax.axis_size("gx") * count_y
    width = part.shape[0]
    block = jnp.zeros((8, 128), jnp.float32).at[0, :width].set(part)
    summed = pl.pallas_call(
        functools.partial(gather_sum_kernel, count_y, total),
        out_shape=jax.ShapeDtypeStruct((8, 128), jnp.float32),
        in_specs=[pl.BlockSpec(memory_space=pltpu.VMEM)],
        out_specs=pl.BlockSpec(memory_space=pltpu.VMEM),
        scratch_shapes=[
            pltpu.VMEM((total, 8, 128), jnp.float32),
            pltpu.SemaphoreType.DMA(()),
            pltpu.SemaphoreType.DMA(()),
        ],
        compiler_params=pltpu.CompilerParams(collective_id=0, has_side_effects=True),
    )(block)
    return summed[0, :width]


def turbine_terms(
    tile_index, thrust, yaw_angle, turbine_place, turbine_tile, width_x, width_y, height
):
    owned_mask = (turbine_tile == tile_index).astype(jnp.float32)
    spread = 2.0 * KERNEL_WIDTH * KERNEL_WIDTH
    along_x = jnp.exp(
        -(
            (jnp.arange(width_x, dtype=jnp.float32)[None, :] - turbine_place[0][:, None] * width_x)
            ** 2
        )
        / spread
    )
    along_y = jnp.exp(
        -(
            (jnp.arange(width_y, dtype=jnp.float32)[None, :] - turbine_place[1][:, None] * width_y)
            ** 2
        )
        / spread
    )
    along_z = jnp.exp(
        -(
            (
                jnp.arange(height, dtype=jnp.float32)[None, :]
                - turbine_place[2][:, None] * (0.5 * height)
            )
            ** 2
        )
        / spread
    )
    plan_kernel = (along_x[:, :, None] * along_y[:, None, :]).reshape(
        along_x.shape[0], width_x * width_y
    )
    cosine = jnp.cos(yaw_angle)
    loading = owned_mask * thrust * cosine * cosine
    drag_field = jnp.dot(
        (plan_kernel * loading[:, None]).T, along_z, precision=lax.Precision.HIGHEST
    )
    return (owned_mask, plan_kernel, along_z, drag_field.reshape(width_x, width_y, height))


def advance_kernel(
    cols_ref, fringe_ref, a_ref, w_ref, e_ref, s_ref, n_ref, u_ref, drag_ref, eddy_ref,
    out_ref, xq, prod,
):
    components, width_x, width_y, height = a_ref.shape
    half = height // NZB
    def fill(px, src):
        for zb in range(NZB):
            for c in range(components):
                xq[2 * px + zb, c * width_y : (c + 1) * width_y, :] = src[c, :, zb * half : (zb + 1) * half].astype(jnp.bfloat16)

    def fill_plane(x, carry):
        for zb in range(NZB):
            for c in range(components):
                xq[2 * (x + 1) + zb, c * width_y : (c + 1) * width_y, :] = a_ref[c, x, :, zb * half : (zb + 1) * half].astype(jnp.bfloat16)
        return carry

    for zb in range(NZB):
        for c in range(components):
            xq[zb, c * width_y : (c + 1) * width_y, :] = w_ref[c, 0, :, zb * half : (zb + 1) * half].astype(jnp.bfloat16)
            xq[2 * (width_x + 1) + zb, c * width_y : (c + 1) * width_y, :] = e_ref[c, 0, :, zb * half : (zb + 1) * half].astype(jnp.bfloat16)
    lax.fori_loop(0, width_x, fill_plane, 0)

    def eddy_block(p, carry):
        acc = jnp.zeros((components * width_y, half), jnp.float32)
        for k in range(KB):
            acc = acc + jnp.dot(xq[cols_ref[p, k]], eddy_ref[k], preferred_element_type=jnp.float32)
        prod[p] = acc
        return carry

    lax.fori_loop(0, width_x * NZB, eddy_block, 0)

    row = lax.broadcasted_iota(jnp.int32, (width_y, height), 0)
    lane = lax.broadcasted_iota(jnp.int32, (width_y, height), 1)

    def plane(x, carry):
        u0 = u_ref[0, x].astype(jnp.float32)
        u1 = u_ref[1, x].astype(jnp.float32)
        u2 = u_ref[2, x].astype(jnp.float32)
        viscous = EDDY_COEF * jnp.sqrt(1.0 + (u0 * u0 + u1 * u1 + u2 * u2))
        west_index = jnp.maximum(x - 1, 0)
        east_index = jnp.minimum(x + 1, width_x - 1)
        scale = fringe_ref[x]
        for c in range(components):
            center = a_ref[c, x]
            west = jnp.where(x == 0, w_ref[c, 0], a_ref[c, west_index])
            east = jnp.where(x == width_x - 1, e_ref[c, 0], a_ref[c, east_index])
            north = jnp.where(row == width_y - 1, jnp.broadcast_to(n_ref[c, x], (width_y, height)), pltpu.roll(center, width_y - 1, 0))
            south = jnp.where(row == 0, jnp.broadcast_to(s_ref[c, x], (width_y, height)), pltpu.roll(center, 1, 0))
            upper = jnp.where(lane == height - 1, 0.0, pltpu.roll(center, height - 1, 1))
            lower = jnp.where(lane == 0, 0.0, pltpu.roll(center, 1, 1))
            laplace = east + west + north + south + upper + lower - 6.0 * center
            advect = 0.5 * (u0 * (east - west) + u1 * (north - south) + u2 * (upper - lower))
            product = jnp.concatenate(
                [prod[2 * x + zb, c * width_y : (c + 1) * width_y, :] for zb in range(NZB)], axis=1
            )
            update = center + TIME_STEP * (advect + BASE_VISC * laplace + viscous * product)
            if c == 0:
                update = update - TIME_STEP * drag_ref[x] * u0 * center
            out_ref[c, x] = update * scale
        return carry

    lax.fori_loop(0, width_x, plane, 0)


def advance(adjoint, west, east, south, north, forward, columns, eddy_blocks, drag_field, fringe_scale):
    components, width_x, width_y, height = adjoint.shape
    vmem = pl.BlockSpec(memory_space=pltpu.VMEM)
    smem = pl.BlockSpec(memory_space=pltpu.SMEM)
    return pl.pallas_call(
        advance_kernel,
        out_shape=jax.ShapeDtypeStruct(adjoint.shape, jnp.float32),
        in_specs=[smem, smem] + [vmem] * 8,
        out_specs=vmem,
        scratch_shapes=[
            pltpu.VMEM(((width_x + 2) * NZB, components * width_y, height // NZB), jnp.bfloat16),
            pltpu.VMEM((width_x * NZB, components * width_y, height // NZB), jnp.float32),
        ],
        compiler_params=pltpu.CompilerParams(vmem_limit_bytes=48 * 1024 * 1024),
    )(columns, fringe_scale, adjoint, west, east, south, north, forward, drag_field, eddy_blocks)


def halo(block, axis, dim):
    count = lax.axis_size(axis)
    forward = [(i, (i + 1) % count) for i in range(count)]
    backward = [(target, source) for source, target in forward]
    low = lax.ppermute(lax.slice_in_dim(block, block.shape[dim] - 1, None, axis=dim), axis, forward)
    high = lax.ppermute(lax.slice_in_dim(block, 0, 1, axis=dim), axis, backward)
    return low, high


def gradient_terms(adjoint, forward, owned_mask, plan_kernel, along_z):
    components, width_x, width_y, height = adjoint.shape
    velocity = forward[0].astype(jnp.float32)
    density = (velocity * velocity * adjoint[0]).reshape(width_x * width_y, height)
    projected = jnp.dot(density, along_z.T, precision=lax.Precision.HIGHEST)
    return owned_mask * jnp.sum(plan_kernel.T * projected, axis=0)


def shards(
    adjoint_in,
    checkpoints,
    send_owner,
    receive_rows,
    block_columns,
    eddy_blocks,
    thrust,
    yaw_angle,
    turbine_place,
    turbine_tile,
    fringe_rows,
):
    count_x = lax.axis_size("gx")
    count_y = lax.axis_size("gy")
    tile_count = count_x * count_y
    tile_index = lax.axis_index("gx") * count_y + lax.axis_index("gy")
    components, width_x, width_y, height = adjoint_in.shape
    steps_total = checkpoints.shape[0]
    block_shape = checkpoints.shape[2:]
    owner_ids = jnp.arange(tile_count, dtype=jnp.int32)
    onehot = (send_owner[:, None] == owner_ids[None, :]).astype(jnp.int32)
    slot_rank = jnp.sum(jnp.cumsum(onehot, axis=0) * onehot, axis=1) - 1
    position = send_owner * CAP + slot_rank
    slots = send_owner.shape[0]
    row_ids = jnp.arange(tile_count * CAP, dtype=jnp.int32)
    pack_table = (row_ids[:, None] == position[None, :]).astype(jnp.bfloat16)
    pack_table = pack_table.reshape(tile_count, CAP, slots)
    pick_table = (receive_rows[:, None] == row_ids[None, :]).astype(jnp.bfloat16)
    pick_table = pick_table.reshape(receive_rows.shape[0], tile_count, CAP)
    rows_x = lax.axis_index("gx") * width_x + jnp.arange(width_x, dtype=jnp.int32)
    fringe_hit = jnp.any(rows_x[:, None] == fringe_rows[None, :], axis=1)
    fringe_scale = jnp.where(fringe_hit, FRINGE_KEEP, 1.0).astype(jnp.float32)
    owned_mask, plan_kernel, along_z, drag_field = turbine_terms(
        tile_index, thrust, yaw_angle, turbine_place, turbine_tile, width_x, width_y, height
    )
    adjoint = adjoint_in
    gradient_sum = jnp.zeros((thrust.shape[0],), jnp.float32)
    for step_index in range(steps_total):
        stored = checkpoints[steps_total - 1 - step_index]
        packed = jnp.einsum(
            "drs,scb->dcrb", pack_table, stored, preferred_element_type=jnp.float32
        ).astype(jnp.bfloat16)
        arrived = lax.all_to_all(packed, ("gx", "gy"), split_axis=0, concat_axis=0, tiled=True)
        forward = jnp.einsum(
            "jsr,scrb->cjb", pick_table, arrived, preferred_element_type=jnp.float32
        ).astype(jnp.bfloat16)
        forward = forward.reshape(components, width_x, width_y, height)
        west, east = halo(adjoint, "gx", 1)
        south, north = halo(adjoint, "gy", 2)
        gradient_sum = gradient_sum + gradient_terms(adjoint, forward, owned_mask, plan_kernel, along_z)
        adjoint = advance(
            adjoint, west, east, south, north, forward, block_columns, eddy_blocks, drag_field, fringe_scale
        )
    gradient_sum = gather_sum(gradient_sum)
    cosine = jnp.cos(yaw_angle)
    sine = jnp.sin(yaw_angle)
    control_gradient = jnp.stack(
        [
            -0.5 * TIME_STEP * cosine * cosine * gradient_sum,
            TIME_STEP * thrust * sine * cosine * gradient_sum,
        ]
    )
    return (adjoint, control_gradient)


def solution(mesh):
    return jax.shard_map(
        shards,
        mesh=mesh,
        in_specs=(
            P(None, "gx", "gy", None),
            P(None, ("gx", "gy"), None, None),
            P(("gx", "gy")),
            P(("gx", "gy")),
            P(("gx", "gy"), None),
            P(),
            P(),
            P(),
            P(),
            P(),
            P(),
        ),
        out_specs=(P(None, "gx", "gy", None), P()),
        check_vma=False,
    )
```

profile of v0, /device:TPU:1, one launch (start us, length us, event | category | flops | bytes accessed | tf_op | source)
XLA Modules:
  0.0 175.8 jit_solution(16924993471089558468)
XLA Ops:
  3.1 2.4 %fusion.4 = bf16[128,3,2,2048]{3,0,2,1:T(8,128)(2,1)S(1)} fusion(bf16[2,128,3,2048]{3,1,2,0:T(8,128)(2,1)} %param.14, s32[128]{0:T(128)S(1)} %add_add_fusion, s32[128,2]{0,1:T(2,128)S(1)} %multiply_add_fusion), kind=kOutput, calls=%fused_computation.8 | convolution fusion | flops 404258816 | bytes 4720128 | tf_op jit(solution)/shard_map/drs,scb->dcrb/dot_general | solution.py:266
  5.5 4.9 %copy.49 = bf16[128,3,2,2048]{3,2,1,0:T(2,128)(2,1)} copy(bf16[128,3,2,2048]{3,0,2,1:T(8,128)(2,1)S(1)} %fusion.4) | data formatting | bytes 6291456 | tf_op jit(solution)/shard_map/convert_element_type | solution.py:268
  10.4 11.9 %all-to-all-start = ((bf16[128,3,2,2048]{3,2,1,0:T(2,128)(2,1)}), bf16[128,3,2,2048]{3,2,1,0:T(2,128)(2,1)}, u32[]{:S(2)}, u32[]{:S(2)}) async-start(bf16[128,3,2,2048]{3,2,1,0:T(2,128)(2,1)} %copy.49), calls=%async_computation | async-start | bytes 6291456 | tf_op jit(solution)/shard_map/all_to_all | solution.py:269
  25.2 1.8 %fusion.56 = (f32[3,1,64,256]{3,2,1,0:T(8,128)}, f32[3,1,64,256]{3,2,1,0:T(8,128)}) fusion(f32[3,16,64,256]{3,2,1,0:T(8,128)} %a_ref.1), kind=kLoop, calls=%fused_computation.79 | loop fusion | bytes 786432 | tf_op jit(solution)/shard_map/slice | solution.py:214
  28.5 2.4 %collective-permute-start = (f32[3,1,64,256]{3,2,1,0:T(8,128)}, f32[3,1,64,256]{3,2,1,0:T(8,128)S(1)}, u32[]{:S(2)}, u32[]{:S(2)}) collective-permute-start(f32[3,1,64,256]{3,2,1,0:T(8,128)} %get-tuple-element.21), channel_id=1, source_target_pairs={{0,2},{2,4},{4,6},{6,8},{8,10},{10,12},{12,14},{14,16},{16,18},{18... | collective-permute-start | bytes 589832 | tf_op jit(solution)/shard_map/ppermute | solution.py:213
  30.9 2.3 %slice.86 = f32[1,16,64,256]{3,2,1,0:T(8,128)} slice(f32[3,16,64,256]{3,2,1,0:T(8,128)} %a_ref.1), slice={[0:1], [0:16], [0:64], [0:256]} | slice | bytes 2097152 | tf_op jit(solution)/shard_map/slice | solution.py:221
  33.4 2.4 %fusion.5 = bf16[128,3,2,2048]{3,0,2,1:T(8,128)(2,1)S(1)} fusion(bf16[2,128,3,2048]{3,1,2,0:T(8,128)(2,1)} %param.14, s32[128]{0:T(128)S(1)} %add_add_fusion, s32[128,2]{0,1:T(2,128)S(1)} %multiply_add_fusion), kind=kOutput, calls=%fused_computation.9 | convolution fusion | flops 404258816 | bytes 4720128 | tf_op jit(solution)/shard_map/drs,scb->dcrb/dot_general | solution.py:266
  35.8 4.9 %copy.55 = bf16[128,3,2,2048]{3,2,1,0:T(2,128)(2,1)} copy(bf16[128,3,2,2048]{3,0,2,1:T(8,128)(2,1)S(1)} %fusion.5) | data formatting | bytes 6291456 | tf_op jit(solution)/shard_map/convert_element_type | solution.py:268
  40.8 22.8 %all-to-all-done = bf16[128,3,2,2048]{3,2,1,0:T(2,128)(2,1)} async-done(((bf16[128,3,2,2048]{3,2,1,0:T(2,128)(2,1)}), bf16[128,3,2,2048]{3,2,1,0:T(2,128)(2,1)}, u32[]{:S(2)}, u32[]{:S(2)}) %all-to-all-start) | async-done | bytes 3145760 | tf_op jit(solution)/shard_map/all_to_all | solution.py:269
  63.5 6.3 %all-to-all-start.1 = ((bf16[128,3,2,2048]{3,2,1,0:T(2,128)(2,1)}), bf16[128,3,2,2048]{3,2,1,0:T(2,128)(2,1)}, u32[]{:S(2)}, u32[]{:S(2)}) async-start(bf16[128,3,2,2048]{3,2,1,0:T(2,128)(2,1)} %copy.55), calls=%async_computation.1 | async-start | bytes 6291456 | tf_op jit(solution)/shard_map/all_to_all | solution.py:269
  72.3 3.3 %fusion.10 = bf16[3,128,2048]{1,2,0:T(8,128)(2,1)S(1)} fusion(bf16[128,3,2,2048]{3,2,1,0:T(2,128)(2,1)} %all-to-all-done, s32[128,2]{0,1:T(2,128)S(1)} %multiply_add_fusion, s32[128]{0:T(128)S(1)} %copy-done.12), kind=kOutput, calls=%fused_computation.10 | convolution fusion | flops 403472384 | bytes 4720128 | tf_op jit(solution)/shard_map/jsr,scrb->cjb/dot_general | solution.py:270
  78.3 2.6 %reshape.175.u_ref = bf16[3,16,64,256]{3,2,1,0:T(8,128)(2,1)S(1)} reshape(bf16[3,128,2048]{2,1,0:T(8,128)(2,1)} %copy.51) | data formatting | bytes 3145728 | tf_op jit(solution)/shard_map/reshape | solution.py:273
  81.0 16.6 %shard_map.122.a_ref = f32[3,16,64,256]{3,2,1,0:T(8,128)} custom-call(s32[32,8]{1,0:T(8,128)S(1)} %copy.58.cols_ref, f32[16]{0:T(128)S(1)} %broadcast_select_fusion.fringe_ref, f32[3,16,64,256]{3,2,1,0:T(8,128)} %a_ref.1, f32[3,1,64,256]{3,2,1,0:T(8,128)S(1)} %collective-permute-done.w_ref, f32[3,1,64,256]{3,2,1,0:T(8,128)S(1)} %collective-permute-done.1.e_ref, ...), custom_call_target="tpu_custom_call" | custom-call | tf_op jit(solution)/shard_map/pallas_call | solution.py:196
  98.8 1.8 %fusion.54 = (f32[3,1,64,256]{3,2,1,0:T(8,128)}, f32[3,1,64,256]{3,2,1,0:T(8,128)}) fusion(f32[3,16,64,256]{3,2,1,0:T(8,128)} %shard_map.122.a_ref), kind=kLoop, calls=%fused_computation.77 | loop fusion | bytes 786432 | tf_op jit(solution)/shard_map/slice | solution.py:214
  101.7 9.4 %all-to-all-done.1 = bf16[128,3,2,2048]{3,2,1,0:T(2,128)(2,1)} async-done(((bf16[128,3,2,2048]{3,2,1,0:T(2,128)(2,1)}), bf16[128,3,2,2048]{3,2,1,0:T(2,128)(2,1)}, u32[]{:S(2)}, u32[]{:S(2)}) %all-to-all-start.1) | async-done | bytes 3145760 | tf_op jit(solution)/shard_map/all_to_all | solution.py:269
  111.1 3.3 %fusion.13 = bf16[3,128,2048]{1,2,0:T(8,128)(2,1)S(1)} fusion(bf16[128,3,2,2048]{3,2,1,0:T(2,128)(2,1)} %all-to-all-done.1, s32[128,2]{0,1:T(2,128)S(1)} %multiply_add_fusion, s32[128]{0:T(128)S(1)} %copy-done.12), kind=kOutput, calls=%fused_computation.11 | convolution fusion | flops 403472384 | bytes 4720128 | tf_op jit(solution)/shard_map/jsr,scrb->cjb/dot_general | solution.py:270
  116.6 2.5 %copy.60 = f32[1,128,2048]{2,1,0:T(8,128)} copy(f32[1,128,2048]{1,2,0:T(8,128)} %convert_multiply_fusion) | data formatting | bytes 2097152 | tf_op jit(solution)/shard_map/mul | solution.py:221
  119.1 2.4 %mul.184 = f32[1024,256]{1,0:T(8,128)} reshape(f32[1,128,2048]{2,1,0:T(8,128)} %copy.60) | data formatting | bytes 2097152 | tf_op jit(solution)/shard_map/mul | solution.py:221
  122.9 2.5 %mul.179 = f32[1024,256]{1,0:T(8,128)} reshape(f32[1,128,2048]{2,1,0:T(8,128)} %copy.59) | data formatting | bytes 2097152 | tf_op jit(solution)/shard_map/mul | solution.py:221
  125.3 1.8 %bitcast_multiply_fusion.1 = f32[1024,256]{1,0:T(8,128)S(1)} fusion(f32[1024,256]{1,0:T(8,128)} %mul.179, f32[1,16,64,256]{3,2,1,0:T(8,128)} %slice.86), kind=kLoop, calls=%fused_computation.21 | loop fusion | flops 262144 | bytes 3145728 | tf_op jit(solution)/shard_map/mul | solution.py:221
  135.2 17.4 %shard_map.124 = f32[8,128]{1,0:T(8,128)} custom-call(f32[8,128]{1,0:T(8,128)} %scatter.4.part_ref), custom_call_target="tpu_custom_call" | custom-call | tf_op jit(solution)/shard_map/pallas_call | solution.py:72
  153.9 2.6 %copy.57 = bf16[3,128,2048]{2,1,0:T(8,128)(2,1)} copy(bf16[3,128,2048]{1,2,0:T(8,128)(2,1)} %copy-done.4) | data formatting | bytes 3145728 | tf_op jit(solution)/shard_map/convert_element_type | solution.py:272
  156.5 2.6 %reshape.176.u_ref = bf16[3,16,64,256]{3,2,1,0:T(8,128)(2,1)S(1)} reshape(bf16[3,128,2048]{2,1,0:T(8,128)(2,1)} %copy.57) | data formatting | bytes 3145728 | tf_op jit(solution)/shard_map/reshape | solution.py:273
  159.2 16.6 %shard_map.123 = f32[3,16,64,256]{3,2,1,0:T(8,128)} custom-call(s32[32,8]{1,0:T(8,128)S(1)} %copy.58.cols_ref, f32[16]{0:T(128)S(1)} %broadcast_select_fusion.fringe_ref, f32[3,16,64,256]{3,2,1,0:T(8,128)} %shard_map.122.a_ref, f32[3,1,64,256]{3,2,1,0:T(8,128)S(1)} %collective-permute-done.4.w_ref, f32[3,1,64,256]{3,2,1,0:T(8,128)S(1)} %collective-permute-done.5.e_ref, ...), custom_call_target="tpu_custom_call" | custom-call | tf_op jit(solution)/shard_map/pallas_call | solution.py:196
  (76 shorter events, 27.3 us)
Async XLA Ops:
  10.4 22.9 %copy-start.10 = (f32[80]{0:T(128)S(1)}, f32[80]{0:T(128)}, u32[]{:S(2)}) copy-start(f32[80]{0:T(128)} %param.20) | copy-start | bytes 964
  10.4 22.9 %copy-start.6 = (s32[32,8]{0,1:T(8,128)S(1)}, s32[32,8]{0,1:T(8,128)}, u32[]{:S(2)}) copy-start(s32[32,8]{0,1:T(8,128)} %param.17) | copy-start | bytes 3076
  10.4 53.2 %all-to-all-start = ((bf16[128,3,2,2048]{3,2,1,0:T(2,128)(2,1)}), bf16[128,3,2,2048]{3,2,1,0:T(2,128)(2,1)}, u32[]{:S(2)}, u32[]{:S(2)}) async-start(bf16[128,3,2,2048]{3,2,1,0:T(2,128)(2,1)} %copy.49), calls=%async_computation | async-start | bytes 6291456 | tf_op jit(solution)/shard_map/all_to_all | solution.py:269
  23.5 57.5 %collective-permute-start.3 = (f32[3,16,1,256]{3,2,1,0:T(1,128)S(1)}, f32[3,16,1,256]{3,2,1,0:T(1,128)S(1)}, u32[]{:S(2)}, u32[]{:S(2)}) collective-permute-start(f32[3,16,1,256]{3,2,1,0:T(1,128)S(1)} %get-tuple-element.18), channel_id=1, source_target_pairs={{1,0},{0,1},{3,2},{2,3},{5,4},{4,5},{7,6},{6,7},{9,8},{8,9},{11,10... | collective-permute-start | bytes 147464 | tf_op jit(solution)/shard_map/ppermute | solution.py:214
  25.1 55.9 %collective-permute-start.2 = (f32[3,16,1,256]{3,2,1,0:T(1,128)S(1)}, f32[3,16,1,256]{3,2,1,0:T(1,128)S(1)}, u32[]{:S(2)}, u32[]{:S(2)}) collective-permute-start(f32[3,16,1,256]{3,2,1,0:T(1,128)S(1)} %get-tuple-element.19), channel_id=1, source_target_pairs={{0,1},{1,0},{2,3},{3,2},{4,5},{5,4},{6,7},{7,6},{8,9},{9,8},{10,11... | collective-permute-start | bytes 147464 | tf_op jit(solution)/shard_map/ppermute | solution.py:213
  27.0 54.0 %collective-permute-start.1 = (f32[3,1,64,256]{3,2,1,0:T(8,128)}, f32[3,1,64,256]{3,2,1,0:T(8,128)S(1)}, u32[]{:S(2)}, u32[]{:S(2)}) collective-permute-start(f32[3,1,64,256]{3,2,1,0:T(8,128)} %get-tuple-element.20), channel_id=1, source_target_pairs={{2,0},{4,2},{6,4},{8,6},{10,8},{12,10},{14,12},{16,14},{18,16},{20... | collective-permute-start | bytes 589832 | tf_op jit(solution)/shard_map/ppermute | solution.py:214
  28.5 52.4 %collective-permute-start = (f32[3,1,64,256]{3,2,1,0:T(8,128)}, f32[3,1,64,256]{3,2,1,0:T(8,128)S(1)}, u32[]{:S(2)}, u32[]{:S(2)}) collective-permute-start(f32[3,1,64,256]{3,2,1,0:T(8,128)} %get-tuple-element.21), channel_id=1, source_target_pairs={{0,2},{2,4},{4,6},{6,8},{8,10},{10,12},{12,14},{14,16},{16,18},{18... | collective-permute-start | bytes 589832 | tf_op jit(solution)/shard_map/ppermute | solution.py:213
  35.8 4.9 %copy-start.9 = (f32[3,80]{1,0:T(4,128)S(1)}, f32[3,80]{1,0:T(4,128)}, u32[]{:S(2)}) copy-start(f32[3,80]{1,0:T(4,128)} %param.21) | copy-start | bytes 2884
  40.7 29.8 %copy-start.7 = (s32[80]{0:T(128)S(1)}, s32[80]{0:T(128)}, u32[]{:S(2)}) copy-start(s32[80]{0:T(128)} %param.22) | copy-start | bytes 964
  40.7 29.8 %copy-start.8 = (f32[80]{0:T(128)S(1)}, f32[80]{0:T(128)}, u32[]{:S(2)}) copy-start(f32[80]{0:T(128)} %param.19) | copy-start | bytes 964
  63.5 47.5 %all-to-all-start.1 = ((bf16[128,3,2,2048]{3,2,1,0:T(2,128)(2,1)}), bf16[128,3,2,2048]{3,2,1,0:T(2,128)(2,1)}, u32[]{:S(2)}, u32[]{:S(2)}) async-start(bf16[128,3,2,2048]{3,2,1,0:T(2,128)(2,1)} %copy.55), calls=%async_computation.1 | async-start | bytes 6291456 | tf_op jit(solution)/shard_map/all_to_all | solution.py:269
  69.8 1.0 copy-start.11
  69.8 2.5 %copy-start.12 = (s32[128]{0:T(128)S(1)}, s32[128]{0:T(128)}, u32[]{:S(2)}) copy-start(s32[128]{0:T(128)} %param.16) | copy-start | bytes 1540
  70.5 0.7 copy-start.1
  75.6 1.1 copy-start.5
  76.8 4.2 %copy-start = (bf16[8,128,128]{2,1,0:T(8,128)(2,1)S(1)}, bf16[8,128,128]{2,1,0:T(8,128)(2,1)}, u32[]{:S(2)}) copy-start(bf16[8,128,128]{2,1,0:T(8,128)(2,1)} %eddy_ref.3) | copy-start | bytes 786436
  114.4 1.1 copy-start.4
  122.9 4.2 %copy-start.2 = (f32[80,1024]{1,0:T(8,128)S(1)}, f32[80,1024]{1,0:T(8,128)}, u32[]{:S(2)}) copy-start(f32[80,1024]{1,0:T(8,128)} %copy-done.1) | copy-start | bytes 983044
  122.9 10.3 %slice-start = ((f32[3,16,64,256]{3,2,1,0:T(8,128)}), f32[1,16,64,256]{3,2,1,0:T(8,128)S(1)}, s32[]{:S(2)}) async-start(f32[3,16,64,256]{3,2,1,0:T(8,128)} %shard_map.122.a_ref), calls=%async_computation.2 | async-start | bytes 2097152 | tf_op jit(solution)/shard_map/slice | solution.py:221
  125.3 7.9 %copy-start.3 = (f32[1024,256]{1,0:T(8,128)S(1)}, f32[1024,256]{1,0:T(8,128)}, u32[]{:S(2)}) copy-start(f32[1024,256]{1,0:T(8,128)} %mul.184) | copy-start | bytes 3145732
  128.4 30.7 %collective-permute-start.7 = (f32[3,16,1,256]{3,2,1,0:T(1,128)S(1)}, f32[3,16,1,256]{3,2,1,0:T(1,128)S(1)}, u32[]{:S(2)}, u32[]{:S(2)}) collective-permute-start(f32[3,16,1,256]{3,2,1,0:T(1,128)S(1)} %get-tuple-element.14), channel_id=1, source_target_pairs={{1,0},{0,1},{3,2},{2,3},{5,4},{4,5},{7,6},{6,7},{9,8},{8,9},{11,10... | collective-permute-start | bytes 147464 | tf_op jit(solution)/shard_map/ppermute | solution.py:214
  129.0 30.1 %collective-permute-start.6 = (f32[3,16,1,256]{3,2,1,0:T(1,128)S(1)}, f32[3,16,1,256]{3,2,1,0:T(1,128)S(1)}, u32[]{:S(2)}, u32[]{:S(2)}) collective-permute-start(f32[3,16,1,256]{3,2,1,0:T(1,128)S(1)} %get-tuple-element.15), channel_id=1, source_target_pairs={{0,1},{1,0},{2,3},{3,2},{4,5},{5,4},{6,7},{7,6},{8,9},{9,8},{10,11... | collective-permute-start | bytes 147464 | tf_op jit(solution)/shard_map/ppermute | solution.py:213
  129.9 29.2 %collective-permute-start.5 = (f32[3,1,64,256]{3,2,1,0:T(8,128)}, f32[3,1,64,256]{3,2,1,0:T(8,128)S(1)}, u32[]{:S(2)}, u32[]{:S(2)}) collective-permute-start(f32[3,1,64,256]{3,2,1,0:T(8,128)} %get-tuple-element.16), channel_id=1, source_target_pairs={{2,0},{4,2},{6,4},{8,6},{10,8},{12,10},{14,12},{16,14},{18,16},{20... | collective-permute-start | bytes 589832 | tf_op jit(solution)/shard_map/ppermute | solution.py:214
  131.5 27.7 %collective-permute-start.4 = (f32[3,1,64,256]{3,2,1,0:T(8,128)}, f32[3,1,64,256]{3,2,1,0:T(8,128)S(1)}, u32[]{:S(2)}, u32[]{:S(2)}) collective-permute-start(f32[3,1,64,256]{3,2,1,0:T(8,128)} %get-tuple-element.17), channel_id=1, source_target_pairs={{0,2},{2,4},{4,6},{6,8},{8,10},{10,12},{12,14},{14,16},{16,18},{18... | collective-permute-start | bytes 589832 | tf_op jit(solution)/shard_map/ppermute | solution.py:213
where the time goes:
time: 177 us; the launch traced here: 176 us
  Pallas kernels  50.5 us (29%)
  local copies, waits for them, and re-layouts  40 us (23%)
  waiting for transfers between devices  32.2 us (18%)
  starting transfers between devices  28.6 us (16%)
  matrix products  15.1 us (9%)
  other arithmetic  8.42 us (5%)
    pallas_call x2, Pallas kernels, advance(): pl.pallas_call(advance_kernel, out_shape=jax.ShapeDtypeStruct(adjoint.sha...  33.2 us
    all_to_all x2, waiting for transfers between devices, shards(): lax.all_to_all(packed, ('gx', 'gy'), split_axis=0, concat_axis=0, tiled=T...  32.1 us
    all_to_all x2, starting transfers between devices, shards(): lax.all_to_all(packed, ('gx', 'gy'), split_axis=0, concat_axis=0, tiled=T...  18.2 us
    pallas_call x1, Pallas kernels, gather_sum(): pl.pallas_call(functools.partial(gather_sum_kernel, count_y, total), out_...  17.4 us
    convert_element_type x2, local copies, waits for them, and re-layouts, shards(): packed = jnp.einsum('drs,scb->dcrb', pack_table, stored, preferred_elemen...  9.83 us
    mul x4, local copies, waits for them, and re-layouts, gradient_terms(): velocity * velocity * adjoint[0]  8.73 us
    dot_general x2, matrix products, shards(): jnp.einsum('jsr,scrb->cjb', pick_table, arrived, preferred_element_type=j...  6.65 us
    slice x4, local copies, waits for them, and re-layouts, halo(): high = lax.ppermute(lax.slice_in_dim(block, 0, 1, axis=dim), axis, backward)  6.03 us
  transfers between devices with their start and end apart: 10, of which 2 were waited for; matrix products, arithmetic and copies ran while one was open for 20% of the time, Pallas kernels for 19%

commit v1 on v0

--- a/solution.py
+++ b/solution.py
@@ -22,62 +22,84 @@
 FRINGE_KEEP = 0.5
 
 
-def gather_sum_kernel(count_y, total, part_ref, out_ref, rows, send_sem, recv_sem):
+def gather_sum_kernel(count_y, group, part_ref, out_ref, near, far, sems):
+    total = lax.axis_size("gx") * count_y
+    groups = total // group
     me = lax.axis_index("gx") * count_y + lax.axis_index("gy")
-
-    def device(i):
-        other = lax.rem(me + i, total)
+    mine, base = me % group, me - me % group
+
+    def near_device(i):
+        other = base + lax.rem(mine + i, group)
         return (other // count_y, other % count_y)
 
+    def far_device(i):
+        other = lax.rem(me + i * group, total)
+        return (other // count_y, other % count_y)
+
     barrier = pltpu.get_barrier_semaphore()
 
-    def greet(i, carry):
-        pl.semaphore_signal(barrier, inc=1, device_id=device(i), device_id_type=MESH)
-        return carry
-
-    lax.fori_loop(1, total, greet, 0)
-    pl.semaphore_wait(barrier, total - 1)
-    rows[me] = part_ref[...]
-
-    def send(i, carry):
+    def greet_near(i, carry):
+        pl.semaphore_signal(barrier, inc=1, device_id=near_device(i), device_id_type=MESH)
+        return carry
+
+    def greet_far(i, carry):
+        pl.semaphore_signal(barrier, inc=1, device_id=far_device(i), device_id_type=MESH)
+        return carry
+
+    lax.fori_loop(1, group, greet_near, 0)
+    lax.fori_loop(1, groups, greet_far, 0)
+    pl.semaphore_wait(barrier, group + groups - 2)
+
+    near[mine] = part_ref[...]
+
+    def send_near(i, carry):
         pltpu.make_async_remote_copy(
-            src_ref=part_ref,
-            dst_ref=rows.at[me],
-            send_sem=send_sem,
-            recv_sem=recv_sem,
-            device_id=device(i),
-            device_id_type=MESH,
+            src_ref=part_ref, dst_ref=near.at[mine], send_sem=sems.at[0], recv_sem=sems.at[1],
+            device_id=near_device(i), device_id_type=MESH,
         ).start()
         return carry
 
-    lax.fori_loop(1, total, send, 0)
-    everything = pltpu.make_async_remote_copy(
-        src_ref=rows.at[pl.ds(0, total - 1)],
-        dst_ref=rows.at[pl.ds(0, total - 1)],
-        send_sem=send_sem,
-        recv_sem=recv_sem,
-        device_id=device(1),
-        device_id_type=MESH,
-    )
-    everything.wait_send()
-    everything.wait_recv()
-    out_ref[...] = jnp.sum(rows[...], axis=0)
+    lax.fori_loop(1, group, send_near, 0)
+    first = pltpu.make_async_remote_copy(
+        src_ref=near.at[pl.ds(0, group - 1)], dst_ref=near.at[pl.ds(0, group - 1)],
+        send_sem=sems.at[0], recv_sem=sems.at[1], device_id=near_device(1), device_id_type=MESH,
+    )
+    first.wait_send()
+    first.wait_recv()
+    far[me // group] = jnp.sum(near[...], axis=0)
+
+    def send_far(i, carry):
+        pltpu.make_async_remote_copy(
+            src_ref=far.at[me // group], dst_ref=far.at[me // group], send_sem=sems.at[2], recv_sem=sems.at[3],
+            device_id=far_device(i), device_id_type=MESH,
+        ).start()
+        return carry
+
+    lax.fori_loop(1, groups, send_far, 0)
+    second = pltpu.make_async_remote_copy(
+        src_ref=far.at[pl.ds(0, groups - 1)], dst_ref=far.at[pl.ds(0, groups - 1)],
+        send_sem=sems.at[2], recv_sem=sems.at[3], device_id=far_device(1), device_id_type=MESH,
+    )
+    second.wait_send()
+    second.wait_recv()
+    out_ref[...] = jnp.sum(far[...], axis=0)
 
 
 def gather_sum(part):
     count_y = lax.axis_size("gy")
     total = lax.axis_size("gx") * count_y
+    group = 8 if total % 8 == 0 and total > 8 else total // 2
     width = part.shape[0]
     block = jnp.zeros((8, 128), jnp.float32).at[0, :width].set(part)
     summed = pl.pallas_call(
-        functools.partial(gather_sum_kernel, count_y, total),
+        functools.partial(gather_sum_kernel, count_y, group),
         out_shape=jax.ShapeDtypeStruct((8, 128), jnp.float32),
         in_specs=[pl.BlockSpec(memory_space=pltpu.VMEM)],
         out_specs=pl.BlockSpec(memory_space=pltpu.VMEM),
         scratch_shapes=[
-            pltpu.VMEM((total, 8, 128), jnp.float32),
-            pltpu.SemaphoreType.DMA(()),
-            pltpu.SemaphoreType.DMA(()),
+            pltpu.VMEM((group, 8, 128), jnp.float32),
+            pltpu.VMEM((total // group, 8, 128), jnp.float32),
+            pltpu.SemaphoreType.DMA((4,)),
         ],
         compiler_params=pltpu.CompilerParams(collective_id=0, has_side_effects=True),
     )(block)

time: 177 us -> 171 us (0.966)
  Pallas kernels: 50.5 us -> 45.1 us
    pallas_call x1, Pallas kernels: 17.4 us -> 11.9 us  [gather_sum(): pl.pallas_call(functools.partial(gather_sum_kernel, count_y, group), out_...]
  transfers between devices with their start and end apart: 10 -> 10, of which waited for: 2 -> 2; matrix products, arithmetic and copies ran while one was open for 20% -> 21% of each run, Pallas kernels for 19% -> 17%
where the time goes in v1:
time: 171 us; the launch traced here: 170 us
  Pallas kernels  45.1 us (26%)
  local copies, waits for them, and re-layouts  40 us (23%)
  waiting for transfers between devices  32.2 us (19%)
  starting transfers between devices  28.6 us (17%)
  matrix products  15.1 us (9%)
  other arithmetic  8.42 us (5%)
    pallas_call x2, Pallas kernels, advance(): pl.pallas_call(advance_kernel, out_shape=jax.ShapeDtypeStruct(adjoint.sha...  33.2 us
    all_to_all x2, waiting for transfers between devices, shards(): lax.all_to_all(packed, ('gx', 'gy'), split_axis=0, concat_axis=0, tiled=T...  32.1 us
    all_to_all x2, starting transfers between devices, shards(): lax.all_to_all(packed, ('gx', 'gy'), split_axis=0, concat_axis=0, tiled=T...  18.2 us
    pallas_call x1, Pallas kernels, gather_sum(): pl.pallas_call(functools.partial(gather_sum_kernel, count_y, group), out_...  11.9 us
    convert_element_type x2, local copies, waits for them, and re-layouts, shards(): packed = jnp.einsum('drs,scb->dcrb', pack_table, stored, preferred_elemen...  9.83 us
    mul x4, local copies, waits for them, and re-layouts, gradient_terms(): velocity * velocity * adjoint[0]  8.73 us
    dot_general x2, matrix products, shards(): jnp.einsum('jsr,scrb->cjb', pick_table, arrived, preferred_element_type=j...  6.65 us
    slice x4, local copies, waits for them, and re-layouts, halo(): high = lax.ppermute(lax.slice_in_dim(block, 0, 1, axis=dim), axis, backward)  6.03 us
  transfers between devices with their start and end apart: 10, of which 2 were waited for; matrix products, arithmetic and copies ran while one was open for 21% of the time, Pallas kernels for 17%

profile of v1, /device:TPU:1, one launch (start us, length us, event | category | flops | bytes accessed | tf_op | source)
XLA Modules:
  0.0 170.4 jit_solution(4720486282377066230)
XLA Ops:
  3.1 2.4 %fusion.4 = bf16[128,3,2,2048]{3,0,2,1:T(8,128)(2,1)S(1)} fusion(bf16[2,128,3,2048]{3,1,2,0:T(8,128)(2,1)} %param.14, s32[128]{0:T(128)S(1)} %add_add_fusion, s32[128,2]{0,1:T(2,128)S(1)} %multiply_add_fusion), kind=kOutput, calls=%fused_computation.8 | convolution fusion | flops 404258816 | bytes 4720128 | tf_op jit(solution)/shard_map/drs,scb->dcrb/dot_general | solution.py:288
  5.5 4.9 %copy.49 = bf16[128,3,2,2048]{3,2,1,0:T(2,128)(2,1)} copy(bf16[128,3,2,2048]{3,0,2,1:T(8,128)(2,1)S(1)} %fusion.4) | data formatting | bytes 6291456 | tf_op jit(solution)/shard_map/convert_element_type | solution.py:290
  10.4 11.9 %all-to-all-start = ((bf16[128,3,2,2048]{3,2,1,0:T(2,128)(2,1)}), bf16[128,3,2,2048]{3,2,1,0:T(2,128)(2,1)}, u32[]{:S(2)}, u32[]{:S(2)}) async-start(bf16[128,3,2,2048]{3,2,1,0:T(2,128)(2,1)} %copy.49), calls=%async_computation | async-start | bytes 6291456 | tf_op jit(solution)/shard_map/all_to_all | solution.py:291
  25.2 1.8 %fusion.56 = (f32[3,1,64,256]{3,2,1,0:T(8,128)}, f32[3,1,64,256]{3,2,1,0:T(8,128)}) fusion(f32[3,16,64,256]{3,2,1,0:T(8,128)} %a_ref.1), kind=kLoop, calls=%fused_computation.79 | loop fusion | bytes 786432 | tf_op jit(solution)/shard_map/slice | solution.py:236
  28.5 2.4 %collective-permute-start = (f32[3,1,64,256]{3,2,1,0:T(8,128)}, f32[3,1,64,256]{3,2,1,0:T(8,128)S(1)}, u32[]{:S(2)}, u32[]{:S(2)}) collective-permute-start(f32[3,1,64,256]{3,2,1,0:T(8,128)} %get-tuple-element.21), channel_id=1, source_target_pairs={{0,2},{2,4},{4,6},{6,8},{8,10},{10,12},{12,14},{14,16},{16,18},{18... | collective-permute-start | bytes 589832 | tf_op jit(solution)/shard_map/ppermute | solution.py:235
  30.9 2.3 %slice.86 = f32[1,16,64,256]{3,2,1,0:T(8,128)} slice(f32[3,16,64,256]{3,2,1,0:T(8,128)} %a_ref.1), slice={[0:1], [0:16], [0:64], [0:256]} | slice | bytes 2097152 | tf_op jit(solution)/shard_map/slice | solution.py:243
  33.4 2.4 %fusion.5 = bf16[128,3,2,2048]{3,0,2,1:T(8,128)(2,1)S(1)} fusion(bf16[2,128,3,2048]{3,1,2,0:T(8,128)(2,1)} %param.14, s32[128]{0:T(128)S(1)} %add_add_fusion, s32[128,2]{0,1:T(2,128)S(1)} %multiply_add_fusion), kind=kOutput, calls=%fused_computation.9 | convolution fusion | flops 404258816 | bytes 4720128 | tf_op jit(solution)/shard_map/drs,scb->dcrb/dot_general | solution.py:288
  35.8 4.9 %copy.55 = bf16[128,3,2,2048]{3,2,1,0:T(2,128)(2,1)} copy(bf16[128,3,2,2048]{3,0,2,1:T(8,128)(2,1)S(1)} %fusion.5) | data formatting | bytes 6291456 | tf_op jit(solution)/shard_map/convert_element_type | solution.py:290
  40.8 22.8 %all-to-all-done = bf16[128,3,2,2048]{3,2,1,0:T(2,128)(2,1)} async-done(((bf16[128,3,2,2048]{3,2,1,0:T(2,128)(2,1)}), bf16[128,3,2,2048]{3,2,1,0:T(2,128)(2,1)}, u32[]{:S(2)}, u32[]{:S(2)}) %all-to-all-start) | async-done | bytes 3145760 | tf_op jit(solution)/shard_map/all_to_all | solution.py:291
  63.5 6.3 %all-to-all-start.1 = ((bf16[128,3,2,2048]{3,2,1,0:T(2,128)(2,1)}), bf16[128,3,2,2048]{3,2,1,0:T(2,128)(2,1)}, u32[]{:S(2)}, u32[]{:S(2)}) async-start(bf16[128,3,2,2048]{3,2,1,0:T(2,128)(2,1)} %copy.55), calls=%async_computation.1 | async-start | bytes 6291456 | tf_op jit(solution)/shard_map/all_to_all | solution.py:291
  72.3 3.3 %fusion.10 = bf16[3,128,2048]{1,2,0:T(8,128)(2,1)S(1)} fusion(bf16[128,3,2,2048]{3,2,1,0:T(2,128)(2,1)} %all-to-all-done, s32[128,2]{0,1:T(2,128)S(1)} %multiply_add_fusion, s32[128]{0:T(128)S(1)} %copy-done.12), kind=kOutput, calls=%fused_computation.10 | convolution fusion | flops 403472384 | bytes 4720128 | tf_op jit(solution)/shard_map/jsr,scrb->cjb/dot_general | solution.py:292
  78.3 2.6 %reshape.175.u_ref = bf16[3,16,64,256]{3,2,1,0:T(8,128)(2,1)S(1)} reshape(bf16[3,128,2048]{2,1,0:T(8,128)(2,1)} %copy.51) | data formatting | bytes 3145728 | tf_op jit(solution)/shard_map/reshape | solution.py:295
  81.0 16.6 %shard_map.122.a_ref = f32[3,16,64,256]{3,2,1,0:T(8,128)} custom-call(s32[32,8]{1,0:T(8,128)S(1)} %copy.58.cols_ref, f32[16]{0:T(128)S(1)} %broadcast_select_fusion.fringe_ref, f32[3,16,64,256]{3,2,1,0:T(8,128)} %a_ref.1, f32[3,1,64,256]{3,2,1,0:T(8,128)S(1)} %collective-permute-done.w_ref, f32[3,1,64,256]{3,2,1,0:T(8,128)S(1)} %collective-permute-done.1.e_ref, ...), custom_call_target="tpu_custom_call" | custom-call | tf_op jit(solution)/shard_map/pallas_call | solution.py:218
  98.8 1.8 %fusion.54 = (f32[3,1,64,256]{3,2,1,0:T(8,128)}, f32[3,1,64,256]{3,2,1,0:T(8,128)}) fusion(f32[3,16,64,256]{3,2,1,0:T(8,128)} %shard_map.122.a_ref), kind=kLoop, calls=%fused_computation.77 | loop fusion | bytes 786432 | tf_op jit(solution)/shard_map/slice | solution.py:236
  101.7 9.4 %all-to-all-done.1 = bf16[128,3,2,2048]{3,2,1,0:T(2,128)(2,1)} async-done(((bf16[128,3,2,2048]{3,2,1,0:T(2,128)(2,1)}), bf16[128,3,2,2048]{3,2,1,0:T(2,128)(2,1)}, u32[]{:S(2)}, u32[]{:S(2)}) %all-to-all-start.1) | async-done | bytes 3145760 | tf_op jit(solution)/shard_map/all_to_all | solution.py:291
  111.1 3.3 %fusion.13 = bf16[3,128,2048]{1,2,0:T(8,128)(2,1)S(1)} fusion(bf16[128,3,2,2048]{3,2,1,0:T(2,128)(2,1)} %all-to-all-done.1, s32[128,2]{0,1:T(2,128)S(1)} %multiply_add_fusion, s32[128]{0:T(128)S(1)} %copy-done.12), kind=kOutput, calls=%fused_computation.11 | convolution fusion | flops 403472384 | bytes 4720128 | tf_op jit(solution)/shard_map/jsr,scrb->cjb/dot_general | solution.py:292
  116.6 2.5 %copy.60 = f32[1,128,2048]{2,1,0:T(8,128)} copy(f32[1,128,2048]{1,2,0:T(8,128)} %convert_multiply_fusion) | data formatting | bytes 2097152 | tf_op jit(solution)/shard_map/mul | solution.py:243
  119.1 2.4 %mul.184 = f32[1024,256]{1,0:T(8,128)} reshape(f32[1,128,2048]{2,1,0:T(8,128)} %copy.60) | data formatting | bytes 2097152 | tf_op jit(solution)/shard_map/mul | solution.py:243
  122.9 2.5 %mul.179 = f32[1024,256]{1,0:T(8,128)} reshape(f32[1,128,2048]{2,1,0:T(8,128)} %copy.59) | data formatting | bytes 2097152 | tf_op jit(solution)/shard_map/mul | solution.py:243
  125.3 1.8 %bitcast_multiply_fusion.1 = f32[1024,256]{1,0:T(8,128)S(1)} fusion(f32[1024,256]{1,0:T(8,128)} %mul.179, f32[1,16,64,256]{3,2,1,0:T(8,128)} %slice.86), kind=kLoop, calls=%fused_computation.21 | loop fusion | flops 262144 | bytes 3145728 | tf_op jit(solution)/shard_map/mul | solution.py:243
  135.2 11.9 %shard_map.124 = f32[8,128]{1,0:T(8,128)} custom-call(f32[8,128]{1,0:T(8,128)} %scatter.4.part_ref), custom_call_target="tpu_custom_call" | custom-call | tf_op jit(solution)/shard_map/pallas_call | solution.py:94
  148.5 2.6 %copy.57 = bf16[3,128,2048]{2,1,0:T(8,128)(2,1)} copy(bf16[3,128,2048]{1,2,0:T(8,128)(2,1)} %copy-done.4) | data formatting | bytes 3145728 | tf_op jit(solution)/shard_map/convert_element_type | solution.py:294
  151.1 2.6 %reshape.176.u_ref = bf16[3,16,64,256]{3,2,1,0:T(8,128)(2,1)S(1)} reshape(bf16[3,128,2048]{2,1,0:T(8,128)(2,1)} %copy.57) | data formatting | bytes 3145728 | tf_op jit(solution)/shard_map/reshape | solution.py:295
  153.8 16.6 %shard_map.123 = f32[3,16,64,256]{3,2,1,0:T(8,128)} custom-call(s32[32,8]{1,0:T(8,128)S(1)} %copy.58.cols_ref, f32[16]{0:T(128)S(1)} %broadcast_select_fusion.fringe_ref, f32[3,16,64,256]{3,2,1,0:T(8,128)} %shard_map.122.a_ref, f32[3,1,64,256]{3,2,1,0:T(8,128)S(1)} %collective-permute-done.4.w_ref, f32[3,1,64,256]{3,2,1,0:T(8,128)S(1)} %collective-permute-done.5.e_ref, ...), custom_call_target="tpu_custom_call" | custom-call | tf_op jit(solution)/shard_map/pallas_call | solution.py:218
  (76 shorter events, 27.3 us)
Async XLA Ops:
  10.4 22.9 %copy-start.10 = (f32[80]{0:T(128)S(1)}, f32[80]{0:T(128)}, u32[]{:S(2)}) copy-start(f32[80]{0:T(128)} %param.20) | copy-start | bytes 964
  10.4 22.9 %copy-start.6 = (s32[32,8]{0,1:T(8,128)S(1)}, s32[32,8]{0,1:T(8,128)}, u32[]{:S(2)}) copy-start(s32[32,8]{0,1:T(8,128)} %param.17) | copy-start | bytes 3076
  10.4 53.2 %all-to-all-start = ((bf16[128,3,2,2048]{3,2,1,0:T(2,128)(2,1)}), bf16[128,3,2,2048]{3,2,1,0:T(2,128)(2,1)}, u32[]{:S(2)}, u32[]{:S(2)}) async-start(bf16[128,3,2,2048]{3,2,1,0:T(2,128)(2,1)} %copy.49), calls=%async_computation | async-start | bytes 6291456 | tf_op jit(solution)/shard_map/all_to_all | solution.py:291
  23.5 57.5 %collective-permute-start.3 = (f32[3,16,1,256]{3,2,1,0:T(1,128)S(1)}, f32[3,16,1,256]{3,2,1,0:T(1,128)S(1)}, u32[]{:S(2)}, u32[]{:S(2)}) collective-permute-start(f32[3,16,1,256]{3,2,1,0:T(1,128)S(1)} %get-tuple-element.18), channel_id=1, source_target_pairs={{1,0},{0,1},{3,2},{2,3},{5,4},{4,5},{7,6},{6,7},{9,8},{8,9},{11,10... | collective-permute-start | bytes 147464 | tf_op jit(solution)/shard_map/ppermute | solution.py:236
  25.1 55.9 %collective-permute-start.2 = (f32[3,16,1,256]{3,2,1,0:T(1,128)S(1)}, f32[3,16,1,256]{3,2,1,0:T(1,128)S(1)}, u32[]{:S(2)}, u32[]{:S(2)}) collective-permute-start(f32[3,16,1,256]{3,2,1,0:T(1,128)S(1)} %get-tuple-element.19), channel_id=1, source_target_pairs={{0,1},{1,0},{2,3},{3,2},{4,5},{5,4},{6,7},{7,6},{8,9},{9,8},{10,11... | collective-permute-start | bytes 147464 | tf_op jit(solution)/shard_map/ppermute | solution.py:235
  27.0 54.0 %collective-permute-start.1 = (f32[3,1,64,256]{3,2,1,0:T(8,128)}, f32[3,1,64,256]{3,2,1,0:T(8,128)S(1)}, u32[]{:S(2)}, u32[]{:S(2)}) collective-permute-start(f32[3,1,64,256]{3,2,1,0:T(8,128)} %get-tuple-element.20), channel_id=1, source_target_pairs={{2,0},{4,2},{6,4},{8,6},{10,8},{12,10},{14,12},{16,14},{18,16},{20... | collective-permute-start | bytes 589832 | tf_op jit(solution)/shard_map/ppermute | solution.py:236
  28.5 52.4 %collective-permute-start = (f32[3,1,64,256]{3,2,1,0:T(8,128)}, f32[3,1,64,256]{3,2,1,0:T(8,128)S(1)}, u32[]{:S(2)}, u32[]{:S(2)}) collective-permute-start(f32[3,1,64,256]{3,2,1,0:T(8,128)} %get-tuple-element.21), channel_id=1, source_target_pairs={{0,2},{2,4},{4,6},{6,8},{8,10},{10,12},{12,14},{14,16},{16,18},{18... | collective-permute-start | bytes 589832 | tf_op jit(solution)/shard_map/ppermute | solution.py:235
  35.8 4.9 %copy-start.9 = (f32[3,80]{1,0:T(4,128)S(1)}, f32[3,80]{1,0:T(4,128)}, u32[]{:S(2)}) copy-start(f32[3,80]{1,0:T(4,128)} %param.21) | copy-start | bytes 2884
  40.7 29.8 %copy-start.7 = (s32[80]{0:T(128)S(1)}, s32[80]{0:T(128)}, u32[]{:S(2)}) copy-start(s32[80]{0:T(128)} %param.22) | copy-start | bytes 964
  40.7 29.8 %copy-start.8 = (f32[80]{0:T(128)S(1)}, f32[80]{0:T(128)}, u32[]{:S(2)}) copy-start(f32[80]{0:T(128)} %param.19) | copy-start | bytes 964
  63.5 47.5 %all-to-all-start.1 = ((bf16[128,3,2,2048]{3,2,1,0:T(2,128)(2,1)}), bf16[128,3,2,2048]{3,2,1,0:T(2,128)(2,1)}, u32[]{:S(2)}, u32[]{:S(2)}) async-start(bf16[128,3,2,2048]{3,2,1,0:T(2,128)(2,1)} %copy.55), calls=%async_computation.1 | async-start | bytes 6291456 | tf_op jit(solution)/shard_map/all_to_all | solution.py:291
  69.8 1.0 copy-start.11
  69.8 2.5 %copy-start.12 = (s32[128]{0:T(128)S(1)}, s32[128]{0:T(128)}, u32[]{:S(2)}) copy-start(s32[128]{0:T(128)} %param.16) | copy-start | bytes 1540
  70.5 0.7 copy-start.1
  75.6 1.1 copy-start.5
  76.8 4.2 %copy-start = (bf16[8,128,128]{2,1,0:T(8,128)(2,1)S(1)}, bf16[8,128,128]{2,1,0:T(8,128)(2,1)}, u32[]{:S(2)}) copy-start(bf16[8,128,128]{2,1,0:T(8,128)(2,1)} %eddy_ref.3) | copy-start | bytes 786436
  114.4 1.1 copy-start.4
  122.9 4.2 %copy-start.2 = (f32[80,1024]{1,0:T(8,128)S(1)}, f32[80,1024]{1,0:T(8,128)}, u32[]{:S(2)}) copy-start(f32[80,1024]{1,0:T(8,128)} %copy-done.1) | copy-start | bytes 983044
  122.9 10.3 %slice-start = ((f32[3,16,64,256]{3,2,1,0:T(8,128)}), f32[1,16,64,256]{3,2,1,0:T(8,128)S(1)}, s32[]{:S(2)}) async-start(f32[3,16,64,256]{3,2,1,0:T(8,128)} %shard_map.122.a_ref), calls=%async_computation.2 | async-start | bytes 2097152 | tf_op jit(solution)/shard_map/slice | solution.py:243
  125.3 7.9 %copy-start.3 = (f32[1024,256]{1,0:T(8,128)S(1)}, f32[1024,256]{1,0:T(8,128)}, u32[]{:S(2)}) copy-start(f32[1024,256]{1,0:T(8,128)} %mul.184) | copy-start | bytes 3145732
  128.4 25.3 %collective-permute-start.7 = (f32[3,16,1,256]{3,2,1,0:T(1,128)S(1)}, f32[3,16,1,256]{3,2,1,0:T(1,128)S(1)}, u32[]{:S(2)}, u32[]{:S(2)}) collective-permute-start(f32[3,16,1,256]{3,2,1,0:T(1,128)S(1)} %get-tuple-element.14), channel_id=1, source_target_pairs={{1,0},{0,1},{3,2},{2,3},{5,4},{4,5},{7,6},{6,7},{9,8},{8,9},{11,10... | collective-permute-start | bytes 147464 | tf_op jit(solution)/shard_map/ppermute | solution.py:236
  129.0 24.7 %collective-permute-start.6 = (f32[3,16,1,256]{3,2,1,0:T(1,128)S(1)}, f32[3,16,1,256]{3,2,1,0:T(1,128)S(1)}, u32[]{:S(2)}, u32[]{:S(2)}) collective-permute-start(f32[3,16,1,256]{3,2,1,0:T(1,128)S(1)} %get-tuple-element.15), channel_id=1, source_target_pairs={{0,1},{1,0},{2,3},{3,2},{4,5},{5,4},{6,7},{7,6},{8,9},{9,8},{10,11... | collective-permute-start | bytes 147464 | tf_op jit(solution)/shard_map/ppermute | solution.py:235
  129.9 23.8 %collective-permute-start.5 = (f32[3,1,64,256]{3,2,1,0:T(8,128)}, f32[3,1,64,256]{3,2,1,0:T(8,128)S(1)}, u32[]{:S(2)}, u32[]{:S(2)}) collective-permute-start(f32[3,1,64,256]{3,2,1,0:T(8,128)} %get-tuple-element.16), channel_id=1, source_target_pairs={{2,0},{4,2},{6,4},{8,6},{10,8},{12,10},{14,12},{16,14},{18,16},{20... | collective-permute-start | bytes 589832 | tf_op jit(solution)/shard_map/ppermute | solution.py:236
  131.5 22.3 %collective-permute-start.4 = (f32[3,1,64,256]{3,2,1,0:T(8,128)}, f32[3,1,64,256]{3,2,1,0:T(8,128)S(1)}, u32[]{:S(2)}, u32[]{:S(2)}) collective-permute-start(f32[3,1,64,256]{3,2,1,0:T(8,128)} %get-tuple-element.17), channel_id=1, source_target_pairs={{0,2},{2,4},{4,6},{6,8},{8,10},{10,12},{12,14},{14,16},{16,18},{18... | collective-permute-start | bytes 589832 | tf_op jit(solution)/shard_map/ppermute | solution.py:235

commit v2 on v0

--- a/solution.py
+++ b/solution.py
@@ -20,68 +20,6 @@
 EDDY_COEF = 0.5
 KERNEL_WIDTH = 1.5
 FRINGE_KEEP = 0.5
-
-
-def gather_sum_kernel(count_y, total, part_ref, out_ref, rows, send_sem, recv_sem):
-    me = lax.axis_index("gx") * count_y + lax.axis_index("gy")
-
-    def device(i):
-        other = lax.rem(me + i, total)
-        return (other // count_y, other % count_y)
-
-    barrier = pltpu.get_barrier_semaphore()
-
-    def greet(i, carry):
-        pl.semaphore_signal(barrier, inc=1, device_id=device(i), device_id_type=MESH)
-        return carry
-
-    lax.fori_loop(1, total, greet, 0)
-    pl.semaphore_wait(barrier, total - 1)
-    rows[me] = part_ref[...]
-
-    def send(i, carry):
-        pltpu.make_async_remote_copy(
-            src_ref=part_ref,
-            dst_ref=rows.at[me],
-            send_sem=send_sem,
-            recv_sem=recv_sem,
-            device_id=device(i),
-            device_id_type=MESH,
-        ).start()
-        return carry
-
-    lax.fori_loop(1, total, send, 0)
-    everything = pltpu.make_async_remote_copy(
-        src_ref=rows.at[pl.ds(0, total - 1)],
-        dst_ref=rows.at[pl.ds(0, total - 1)],
-        send_sem=send_sem,
-        recv_sem=recv_sem,
-        device_id=device(1),
-        device_id_type=MESH,
-    )
-    everything.wait_send()
-    everything.wait_recv()
-    out_ref[...] = jnp.sum(rows[...], axis=0)
-
-
-def gather_sum(part):
-    count_y = lax.axis_size("gy")
-    total = lax.axis_size("gx") * count_y
-    width = part.shape[0]
-    block = jnp.zeros((8, 128), jnp.float32).at[0, :width].set(part)
-    summed = pl.pallas_call(
-        functools.partial(gather_sum_kernel, count_y, total),
-        out_shape=jax.ShapeDtypeStruct((8, 128), jnp.float32),
-        in_specs=[pl.BlockSpec(memory_space=pltpu.VMEM)],
-        out_specs=pl.BlockSpec(memory_space=pltpu.VMEM),
-        scratch_shapes=[
-            pltpu.VMEM((total, 8, 128), jnp.float32),
-            pltpu.SemaphoreType.DMA(()),
-            pltpu.SemaphoreType.DMA(()),
-        ],
-        compiler_params=pltpu.CompilerParams(collective_id=0, has_side_effects=True),
-    )(block)
-    return summed[0, :width]
 
 
 def turbine_terms(
@@ -124,11 +62,51 @@
     return (owned_mask, plan_kernel, along_z, drag_field.reshape(width_x, width_y, height))
 
 
-def advance_kernel(
-    cols_ref, fringe_ref, a_ref, w_ref, e_ref, s_ref, n_ref, u_ref, drag_ref, eddy_ref,
-    out_ref, xq, prod,
-):
+def advance_kernel(count_y, group, exchange, *refs):
+    if exchange:
+        (cols_ref, fringe_ref, a_ref, w_ref, e_ref, s_ref, n_ref, u_ref, drag_ref, eddy_ref, part_ref,
+         out_ref, sum_ref, xq, prod, near, far, sems) = refs
+    else:
+        (cols_ref, fringe_ref, a_ref, w_ref, e_ref, s_ref, n_ref, u_ref, drag_ref, eddy_ref,
+         out_ref, xq, prod) = refs
     components, width_x, width_y, height = a_ref.shape
+    if exchange:
+        total = lax.axis_size("gx") * count_y
+        groups = total // group
+        me = lax.axis_index("gx") * count_y + lax.axis_index("gy")
+        mine, base = me % group, me - me % group
+
+        def near_device(i):
+            other = base + lax.rem(mine + i, group)
+            return (other // count_y, other % count_y)
+
+        def far_device(i):
+            other = lax.rem(me + i * group, total)
+            return (other // count_y, other % count_y)
+
+        barrier = pltpu.get_barrier_semaphore()
+
+        def greet_near(i, carry):
+            pl.semaphore_signal(barrier, inc=1, device_id=near_device(i), device_id_type=MESH)
+            return carry
+
+        def greet_far(i, carry):
+            pl.semaphore_signal(barrier, inc=1, device_id=far_device(i), device_id_type=MESH)
+            return carry
+
+        lax.fori_loop(1, group, greet_near, 0)
+        lax.fori_loop(1, groups, greet_far, 0)
+        pl.semaphore_wait(barrier, group + groups - 2)
+        near[mine] = part_ref[...]
+
+        def send_near(i, carry):
+            pltpu.make_async_remote_copy(
+                src_ref=part_ref, dst_ref=near.at[mine], send_sem=sems.at[0], recv_sem=sems.at[1],
+                device_id=near_device(i), device_id_type=MESH,
+            ).start()
+            return carry
+
+        lax.fori_loop(1, group, send_near, 0)
     half = height // NZB
     def fill(px, src):
         for zb in range(NZB):
@@ -155,6 +133,23 @@
         return carry
 
     lax.fori_loop(0, width_x * NZB, eddy_block, 0)
+    if exchange:
+        first = pltpu.make_async_remote_copy(
+            src_ref=near.at[pl.ds(0, group - 1)], dst_ref=near.at[pl.ds(0, group - 1)],
+            send_sem=sems.at[0], recv_sem=sems.at[1], device_id=near_device(1), device_id_type=MESH,
+        )
+        first.wait_send()
+        first.wait_recv()
+        far[me // group] = jnp.sum(near[...], axis=0)
+
+        def send_far(i, carry):
+            pltpu.make_async_remote_copy(
+                src_ref=far.at[me // group], dst_ref=far.at[me // group], send_sem=sems.at[2],
+                recv_sem=sems.at[3], device_id=far_device(i), device_id_type=MESH,
+            ).start()
+            return carry
+
+        lax.fori_loop(1, groups, send_far, 0)
 
     row = lax.broadcasted_iota(jnp.int32, (width_y, height), 0)
     lane = lax.broadcasted_iota(jnp.int32, (width_y, height), 1)
@@ -187,23 +182,52 @@
         return carry
 
     lax.fori_loop(0, width_x, plane, 0)
-
-
-def advance(adjoint, west, east, south, north, forward, columns, eddy_blocks, drag_field, fringe_scale):
+    if exchange:
+        second = pltpu.make_async_remote_copy(
+            src_ref=far.at[pl.ds(0, groups - 1)], dst_ref=far.at[pl.ds(0, groups - 1)],
+            send_sem=sems.at[2], recv_sem=sems.at[3], device_id=far_device(1), device_id_type=MESH,
+        )
+        second.wait_send()
+        second.wait_recv()
+        sum_ref[...] = jnp.sum(far[...], axis=0)
+
+
+def advance(adjoint, west, east, south, north, forward, columns, eddy_blocks, drag_field, fringe_scale, part=None):
     components, width_x, width_y, height = adjoint.shape
     vmem = pl.BlockSpec(memory_space=pltpu.VMEM)
     smem = pl.BlockSpec(memory_space=pltpu.SMEM)
-    return pl.pallas_call(
-        advance_kernel,
-        out_shape=jax.ShapeDtypeStruct(adjoint.shape, jnp.float32),
-        in_specs=[smem, smem] + [vmem] * 8,
-        out_specs=vmem,
-        scratch_shapes=[
-            pltpu.VMEM(((width_x + 2) * NZB, components * width_y, height // NZB), jnp.bfloat16),
-            pltpu.VMEM((width_x * NZB, components * width_y, height // NZB), jnp.float32),
-        ],
-        compiler_params=pltpu.CompilerParams(vmem_limit_bytes=48 * 1024 * 1024),
-    )(columns, fringe_scale, adjoint, west, east, south, north, forward, drag_field, eddy_blocks)
+    count_y = lax.axis_size("gy")
+    total = lax.axis_size("gx") * count_y
+    group = 8 if total % 8 == 0 and total > 8 else total // 2
+    exchange = part is not None
+    operands = [columns, fringe_scale, adjoint, west, east, south, north, forward, drag_field, eddy_blocks]
+    out_shape = [jax.ShapeDtypeStruct(adjoint.shape, jnp.float32)]
+    scratch = [
+        pltpu.VMEM(((width_x + 2) * NZB, components * width_y, height // NZB), jnp.bfloat16),
+        pltpu.VMEM((width_x * NZB, components * width_y, height // NZB), jnp.float32),
+    ]
+    params = dict(vmem_limit_bytes=48 * 1024 * 1024)
+    if exchange:
+        width = part.shape[0]
+        operands.append(jnp.zeros((8, 128), jnp.float32).at[0, :width].set(part))
+        out_shape.append(jax.ShapeDtypeStruct((8, 128), jnp.float32))
+        scratch += [
+            pltpu.VMEM((group, 8, 128), jnp.float32),
+            pltpu.VMEM((total // group, 8, 128), jnp.float32),
+            pltpu.SemaphoreType.DMA((4,)),
+        ]
+        params.update(collective_id=0, has_side_effects=True)
+    results = pl.pallas_call(
+        functools.partial(advance_kernel, count_y, group, exchange),
+        out_shape=tuple(out_shape),
+        in_specs=[smem, smem] + [vmem] * (len(operands) - 2),
+        out_specs=tuple([vmem] * len(out_shape)),
+        scratch_shapes=scratch,
+        compiler_params=pltpu.CompilerParams(**params),
+    )(*operands)
+    if exchange:
+        return results[0], results[1][0, :width]
+    return results[0]
 
 
 def halo(block, axis, dim):
@@ -274,10 +298,15 @@
         west, east = halo(adjoint, "gx", 1)
         south, north = halo(adjoint, "gy", 2)
         gradient_sum = gradient_sum + gradient_terms(adjoint, forward, owned_mask, plan_kernel, along_z)
-        adjoint = advance(
-            adjoint, west, east, south, north, forward, block_columns, eddy_blocks, drag_field, fringe_scale
-        )
-    gradient_sum = gather_sum(gradient_sum)
+        last = step_index == steps_total - 1
+        stepped = advance(
+            adjoint, west, east, south, north, forward, block_columns, eddy_blocks, drag_field, fringe_scale,
+            gradient_sum if last else None,
+        )
+        if last:
+            adjoint, gradient_sum = stepped
+        else:
+            adjoint = stepped
     cosine = jnp.cos(yaw_angle)
     sine = jnp.sin(yaw_angle)
     control_gradient = jnp.stack(

time: 177 us -> 167 us (0.944)
  Pallas kernels: 50.5 us -> 37 us
  local copies, waits for them, and re-layouts: 40 us -> 43.3 us
    pallas_call x3 -> x2, Pallas kernels: 50.5 us -> 37 us  [advance(): pl.pallas_call(functools.partial(advance_kernel, count_y, group, exchange...]
    unnamed x27 -> x28, local copies, waits for them, and re-layouts: 2.58 us -> 6.53 us
  transfers between devices with their start and end apart: 10 -> 10, of which waited for: 2 -> 2; matrix products, arithmetic and copies ran while one was open for 20% -> 20% of each run, Pallas kernels for 19% -> 10%
where the time goes in v2:
time: 167 us; the launch traced here: 165 us
  local copies, waits for them, and re-layouts  43.3 us (26%)
  Pallas kernels  37 us (22%)
  waiting for transfers between devices  32.1 us (19%)
  starting transfers between devices  28.6 us (17%)
  matrix products  15.1 us (9%)
  other arithmetic  7.73 us (5%)
    pallas_call x2, Pallas kernels, advance(): pl.pallas_call(functools.partial(advance_kernel, count_y, group, exchange...  37 us
    all_to_all x2, waiting for transfers between devices, shards(): lax.all_to_all(packed, ('gx', 'gy'), split_axis=0, concat_axis=0, tiled=T...  32.1 us
    all_to_all x2, starting transfers between devices, shards(): lax.all_to_all(packed, ('gx', 'gy'), split_axis=0, concat_axis=0, tiled=T...  18.2 us
    convert_element_type x2, local copies, waits for them, and re-layouts, shards(): packed = jnp.einsum('drs,scb->dcrb', pack_table, stored, preferred_elemen...  9.83 us
    mul x4, local copies, waits for them, and re-layouts, gradient_terms(): velocity * velocity * adjoint[0]  8.65 us
    dot_general x2, matrix products, shards(): jnp.einsum('jsr,scrb->cjb', pick_table, arrived, preferred_element_type=j...  6.65 us
    unnamed x28, local copies, waits for them, and re-layouts  6.53 us
    slice x4, local copies, waits for them, and re-layouts, halo(): high = lax.ppermute(lax.slice_in_dim(block, 0, 1, axis=dim), axis, backward)  6.06 us
  transfers between devices with their start and end apart: 10, of which 2 were waited for; matrix products, arithmetic and copies ran while one was open for 20% of the time, Pallas kernels for 10%

profile of v2, /device:TPU:1, one launch (start us, length us, event | category | flops | bytes accessed | tf_op | source)
XLA Modules:
  0.0 164.8 jit_solution(5460602004238420659)
XLA Ops:
  3.1 2.4 %fusion.4 = bf16[128,3,2,2048]{3,0,2,1:T(8,128)(2,1)S(1)} fusion(bf16[2,128,3,2048]{3,1,2,0:T(8,128)(2,1)} %param.14, s32[128]{0:T(128)S(1)} %add_add_fusion, s32[128,2]{0,1:T(2,128)S(1)} %multiply_add_fusion), kind=kOutput, calls=%fused_computation.8 | convolution fusion | flops 404258816 | bytes 4720128 | tf_op jit(solution)/shard_map/drs,scb->dcrb/dot_general | solution.py:290
  5.5 4.9 %copy.49 = bf16[128,3,2,2048]{3,2,1,0:T(2,128)(2,1)} copy(bf16[128,3,2,2048]{3,0,2,1:T(8,128)(2,1)S(1)} %fusion.4) | data formatting | bytes 6291456 | tf_op jit(solution)/shard_map/convert_element_type | solution.py:292
  10.4 11.9 %all-to-all-start = ((bf16[128,3,2,2048]{3,2,1,0:T(2,128)(2,1)}), bf16[128,3,2,2048]{3,2,1,0:T(2,128)(2,1)}, u32[]{:S(2)}, u32[]{:S(2)}) async-start(bf16[128,3,2,2048]{3,2,1,0:T(2,128)(2,1)} %copy.49), calls=%async_computation | async-start | bytes 6291456 | tf_op jit(solution)/shard_map/all_to_all | solution.py:293
  25.2 1.8 %fusion.56 = (f32[3,1,64,256]{3,2,1,0:T(8,128)}, f32[3,1,64,256]{3,2,1,0:T(8,128)}) fusion(f32[3,16,64,256]{3,2,1,0:T(8,128)} %refs_2_.1), kind=kLoop, calls=%fused_computation.79 | loop fusion | bytes 786432 | tf_op jit(solution)/shard_map/slice | solution.py:238
  28.5 2.4 %collective-permute-start = (f32[3,1,64,256]{3,2,1,0:T(8,128)}, f32[3,1,64,256]{3,2,1,0:T(8,128)S(1)}, u32[]{:S(2)}, u32[]{:S(2)}) collective-permute-start(f32[3,1,64,256]{3,2,1,0:T(8,128)} %get-tuple-element.25), channel_id=1, source_target_pairs={{0,2},{2,4},{4,6},{6,8},{8,10},{10,12},{12,14},{14,16},{16,18},{18... | collective-permute-start | bytes 589832 | tf_op jit(solution)/shard_map/ppermute | solution.py:237
  30.9 2.3 %slice.86 = f32[1,16,64,256]{3,2,1,0:T(8,128)} slice(f32[3,16,64,256]{3,2,1,0:T(8,128)} %refs_2_.1), slice={[0:1], [0:16], [0:64], [0:256]} | slice | bytes 2097152 | tf_op jit(solution)/shard_map/slice | solution.py:245
  33.4 2.4 %fusion.5 = bf16[128,3,2,2048]{3,0,2,1:T(8,128)(2,1)S(1)} fusion(bf16[2,128,3,2048]{3,1,2,0:T(8,128)(2,1)} %param.14, s32[128]{0:T(128)S(1)} %add_add_fusion, s32[128,2]{0,1:T(2,128)S(1)} %multiply_add_fusion), kind=kOutput, calls=%fused_computation.9 | convolution fusion | flops 404258816 | bytes 4720128 | tf_op jit(solution)/shard_map/drs,scb->dcrb/dot_general | solution.py:290
  35.8 4.9 %copy.55 = bf16[128,3,2,2048]{3,2,1,0:T(2,128)(2,1)} copy(bf16[128,3,2,2048]{3,0,2,1:T(8,128)(2,1)S(1)} %fusion.5) | data formatting | bytes 6291456 | tf_op jit(solution)/shard_map/convert_element_type | solution.py:292
  40.8 22.8 %all-to-all-done = bf16[128,3,2,2048]{3,2,1,0:T(2,128)(2,1)} async-done(((bf16[128,3,2,2048]{3,2,1,0:T(2,128)(2,1)}), bf16[128,3,2,2048]{3,2,1,0:T(2,128)(2,1)}, u32[]{:S(2)}, u32[]{:S(2)}) %all-to-all-start) | async-done | bytes 3145760 | tf_op jit(solution)/shard_map/all_to_all | solution.py:293
  63.5 6.3 %all-to-all-start.1 = ((bf16[128,3,2,2048]{3,2,1,0:T(2,128)(2,1)}), bf16[128,3,2,2048]{3,2,1,0:T(2,128)(2,1)}, u32[]{:S(2)}, u32[]{:S(2)}) async-start(bf16[128,3,2,2048]{3,2,1,0:T(2,128)(2,1)} %copy.55), calls=%async_computation.1 | async-start | bytes 6291456 | tf_op jit(solution)/shard_map/all_to_all | solution.py:293
  72.3 3.3 %fusion.10 = bf16[3,128,2048]{1,2,0:T(8,128)(2,1)S(1)} fusion(bf16[128,3,2,2048]{3,2,1,0:T(2,128)(2,1)} %all-to-all-done, s32[128,2]{0,1:T(2,128)S(1)} %multiply_add_fusion, s32[128]{0:T(128)S(1)} %copy-done.12), kind=kOutput, calls=%fused_computation.10 | convolution fusion | flops 403472384 | bytes 4720128 | tf_op jit(solution)/shard_map/jsr,scrb->cjb/dot_general | solution.py:294
  78.3 2.6 %reshape.175.refs_7_ = bf16[3,16,64,256]{3,2,1,0:T(8,128)(2,1)S(1)} reshape(bf16[3,128,2048]{2,1,0:T(8,128)(2,1)} %copy.51) | data formatting | bytes 3145728 | tf_op jit(solution)/shard_map/reshape | solution.py:297
  81.0 16.6 %shard_map.122.refs_2_ = f32[3,16,64,256]{3,2,1,0:T(8,128)} custom-call(s32[32,8]{1,0:T(8,128)S(1)} %copy.60.refs_0_, f32[16]{0:T(128)S(1)} %broadcast_select_fusion.refs_1_, f32[3,16,64,256]{3,2,1,0:T(8,128)} %refs_2_.1, f32[3,1,64,256]{3,2,1,0:T(8,128)S(1)} %collective-permute-done.refs_3_, f32[3,1,64,256]{3,2,1,0:T(8,128)S(1)} %collective-permute-done.1.refs_4_, ...), custom_call_target="tpu_custom_call" | custom-call | tf_op jit(solution)/shard_map/pallas_call | solution.py:220
  98.8 1.9 %fusion.54 = (f32[3,1,64,256]{3,2,1,0:T(8,128)}, f32[3,1,64,256]{3,2,1,0:T(8,128)}) fusion(f32[3,16,64,256]{3,2,1,0:T(8,128)} %shard_map.122.refs_2_), kind=kLoop, calls=%fused_computation.77 | loop fusion | bytes 786432 | tf_op jit(solution)/shard_map/slice | solution.py:238
  101.8 9.3 %all-to-all-done.1 = bf16[128,3,2,2048]{3,2,1,0:T(2,128)(2,1)} async-done(((bf16[128,3,2,2048]{3,2,1,0:T(2,128)(2,1)}), bf16[128,3,2,2048]{3,2,1,0:T(2,128)(2,1)}, u32[]{:S(2)}, u32[]{:S(2)}) %all-to-all-start.1) | async-done | bytes 3145760 | tf_op jit(solution)/shard_map/all_to_all | solution.py:293
  111.1 3.3 %fusion.13 = bf16[3,128,2048]{1,2,0:T(8,128)(2,1)S(1)} fusion(bf16[128,3,2,2048]{3,2,1,0:T(2,128)(2,1)} %all-to-all-done.1, s32[128,2]{0,1:T(2,128)S(1)} %multiply_add_fusion, s32[128]{0:T(128)S(1)} %copy-done.12), kind=kOutput, calls=%fused_computation.11 | convolution fusion | flops 403472384 | bytes 4720128 | tf_op jit(solution)/shard_map/jsr,scrb->cjb/dot_general | solution.py:294
  116.6 2.5 %copy.59 = f32[1,128,2048]{2,1,0:T(8,128)} copy(f32[1,128,2048]{1,2,0:T(8,128)} %convert_multiply_fusion) | data formatting | bytes 2097152 | tf_op jit(solution)/shard_map/mul | solution.py:245
  119.1 2.4 %mul.181 = f32[1024,256]{1,0:T(8,128)} reshape(f32[1,128,2048]{2,1,0:T(8,128)} %copy.59) | data formatting | bytes 2097152 | tf_op jit(solution)/shard_map/mul | solution.py:245
  122.8 2.4 %mul.176 = f32[1024,256]{1,0:T(8,128)} reshape(f32[1,128,2048]{2,1,0:T(8,128)} %copy.58) | data formatting | bytes 2097152 | tf_op jit(solution)/shard_map/mul | solution.py:245
  125.3 1.8 %bitcast_multiply_fusion.1 = f32[1024,256]{1,0:T(8,128)S(1)} fusion(f32[1024,256]{1,0:T(8,128)} %mul.176, f32[1,16,64,256]{3,2,1,0:T(8,128)} %slice.86), kind=kLoop, calls=%fused_computation.21 | loop fusion | flops 262144 | bytes 3145728 | tf_op jit(solution)/shard_map/mul | solution.py:245
  134.6 2.7 %copy.57 = bf16[3,128,2048]{2,1,0:T(8,128)(2,1)} copy(bf16[3,128,2048]{1,2,0:T(8,128)(2,1)} %copy-done.4) | data formatting | bytes 3145728 | tf_op jit(solution)/shard_map/convert_element_type | solution.py:296
  137.2 2.6 %reshape.176.refs_7_ = bf16[3,16,64,256]{3,2,1,0:T(8,128)(2,1)S(1)} reshape(bf16[3,128,2048]{2,1,0:T(8,128)(2,1)} %copy.57) | data formatting | bytes 3145728 | tf_op jit(solution)/shard_map/reshape | solution.py:297
  139.9 20.4 %shard_map.123 = (f32[3,16,64,256]{3,2,1,0:T(8,128)}, f32[8,128]{1,0:T(8,128)S(1)}) custom-call(s32[32,8]{1,0:T(8,128)S(1)} %copy.60.refs_0_, f32[16]{0:T(128)S(1)} %broadcast_select_fusion.refs_1_, f32[3,16,64,256]{3,2,1,0:T(8,128)} %shard_map.122.refs_2_, f32[3,1,64,256]{3,2,1,0:T(8,128)S(1)} %collective-permute-done.4.refs_3_, ...), custom_call_target="tpu_custom_call" | custom-call | tf_op jit(solution)/shard_map/pallas_call | solution.py:220
  160.9 3.9 %copy.79 = f32[3,16,64,256]{3,2,1,0:T(8,128)} copy(f32[3,16,64,256]{3,2,1,0:T(8,128)} %get-tuple-element.33) | data formatting | bytes 6291456
  (76 shorter events, 26.0 us)
Async XLA Ops:
  10.4 22.9 %copy-start.10 = (f32[80]{0:T(128)S(1)}, f32[80]{0:T(128)}, u32[]{:S(2)}) copy-start(f32[80]{0:T(128)} %param.20) | copy-start | bytes 964
  10.4 22.9 %copy-start.6 = (s32[32,8]{0,1:T(8,128)S(1)}, s32[32,8]{0,1:T(8,128)}, u32[]{:S(2)}) copy-start(s32[32,8]{0,1:T(8,128)} %param.17) | copy-start | bytes 3076
  10.4 53.2 %all-to-all-start = ((bf16[128,3,2,2048]{3,2,1,0:T(2,128)(2,1)}), bf16[128,3,2,2048]{3,2,1,0:T(2,128)(2,1)}, u32[]{:S(2)}, u32[]{:S(2)}) async-start(bf16[128,3,2,2048]{3,2,1,0:T(2,128)(2,1)} %copy.49), calls=%async_computation | async-start | bytes 6291456 | tf_op jit(solution)/shard_map/all_to_all | solution.py:293
  23.5 57.5 %collective-permute-start.3 = (f32[3,16,1,256]{3,2,1,0:T(1,128)S(1)}, f32[3,16,1,256]{3,2,1,0:T(1,128)S(1)}, u32[]{:S(2)}, u32[]{:S(2)}) collective-permute-start(f32[3,16,1,256]{3,2,1,0:T(1,128)S(1)} %get-tuple-element.22), channel_id=1, source_target_pairs={{1,0},{0,1},{3,2},{2,3},{5,4},{4,5},{7,6},{6,7},{9,8},{8,9},{11,10... | collective-permute-start | bytes 147464 | tf_op jit(solution)/shard_map/ppermute | solution.py:238
  25.1 55.9 %collective-permute-start.2 = (f32[3,16,1,256]{3,2,1,0:T(1,128)S(1)}, f32[3,16,1,256]{3,2,1,0:T(1,128)S(1)}, u32[]{:S(2)}, u32[]{:S(2)}) collective-permute-start(f32[3,16,1,256]{3,2,1,0:T(1,128)S(1)} %get-tuple-element.23), channel_id=1, source_target_pairs={{0,1},{1,0},{2,3},{3,2},{4,5},{5,4},{6,7},{7,6},{8,9},{9,8},{10,11... | collective-permute-start | bytes 147464 | tf_op jit(solution)/shard_map/ppermute | solution.py:237
  27.0 54.0 %collective-permute-start.1 = (f32[3,1,64,256]{3,2,1,0:T(8,128)}, f32[3,1,64,256]{3,2,1,0:T(8,128)S(1)}, u32[]{:S(2)}, u32[]{:S(2)}) collective-permute-start(f32[3,1,64,256]{3,2,1,0:T(8,128)} %get-tuple-element.24), channel_id=1, source_target_pairs={{2,0},{4,2},{6,4},{8,6},{10,8},{12,10},{14,12},{16,14},{18,16},{20... | collective-permute-start | bytes 589832 | tf_op jit(solution)/shard_map/ppermute | solution.py:238
  28.5 52.4 %collective-permute-start = (f32[3,1,64,256]{3,2,1,0:T(8,128)}, f32[3,1,64,256]{3,2,1,0:T(8,128)S(1)}, u32[]{:S(2)}, u32[]{:S(2)}) collective-permute-start(f32[3,1,64,256]{3,2,1,0:T(8,128)} %get-tuple-element.25), channel_id=1, source_target_pairs={{0,2},{2,4},{4,6},{6,8},{8,10},{10,12},{12,14},{14,16},{16,18},{18... | collective-permute-start | bytes 589832 | tf_op jit(solution)/shard_map/ppermute | solution.py:237
  35.8 4.9 %copy-start.9 = (f32[3,80]{1,0:T(4,128)S(1)}, f32[3,80]{1,0:T(4,128)}, u32[]{:S(2)}) copy-start(f32[3,80]{1,0:T(4,128)} %param.21) | copy-start | bytes 2884
  40.7 29.8 %copy-start.7 = (s32[80]{0:T(128)S(1)}, s32[80]{0:T(128)}, u32[]{:S(2)}) copy-start(s32[80]{0:T(128)} %param.22) | copy-start | bytes 964
  40.8 29.8 %copy-start.8 = (f32[80]{0:T(128)S(1)}, f32[80]{0:T(128)}, u32[]{:S(2)}) copy-start(f32[80]{0:T(128)} %param.19) | copy-start | bytes 964
  63.5 47.5 %all-to-all-start.1 = ((bf16[128,3,2,2048]{3,2,1,0:T(2,128)(2,1)}), bf16[128,3,2,2048]{3,2,1,0:T(2,128)(2,1)}, u32[]{:S(2)}, u32[]{:S(2)}) async-start(bf16[128,3,2,2048]{3,2,1,0:T(2,128)(2,1)} %copy.55), calls=%async_computation.1 | async-start | bytes 6291456 | tf_op jit(solution)/shard_map/all_to_all | solution.py:293
  69.8 1.0 copy-start.11
  69.8 2.5 %copy-start.12 = (s32[128]{0:T(128)S(1)}, s32[128]{0:T(128)}, u32[]{:S(2)}) copy-start(s32[128]{0:T(128)} %param.16) | copy-start | bytes 1540
  70.5 0.7 copy-start.1
  75.6 1.2 copy-start.5
  76.8 4.2 %copy-start = (bf16[8,128,128]{2,1,0:T(8,128)(2,1)S(1)}, bf16[8,128,128]{2,1,0:T(8,128)(2,1)}, u32[]{:S(2)}) copy-start(bf16[8,128,128]{2,1,0:T(8,128)(2,1)} %refs_9_.3) | copy-start | bytes 786436
  114.4 1.2 copy-start.4
  122.8 4.2 %copy-start.2 = (f32[80,1024]{1,0:T(8,128)S(1)}, f32[80,1024]{1,0:T(8,128)}, u32[]{:S(2)}) copy-start(f32[80,1024]{1,0:T(8,128)} %copy-done.1) | copy-start | bytes 983044
  122.8 10.3 %slice-start = ((f32[3,16,64,256]{3,2,1,0:T(8,128)}), f32[1,16,64,256]{3,2,1,0:T(8,128)S(1)}, s32[]{:S(2)}) async-start(f32[3,16,64,256]{3,2,1,0:T(8,128)} %shard_map.122.refs_2_), calls=%async_computation.2 | async-start | bytes 2097152 | tf_op jit(solution)/shard_map/slice | solution.py:245
  125.3 7.9 %copy-start.3 = (f32[1024,256]{1,0:T(8,128)S(1)}, f32[1024,256]{1,0:T(8,128)}, u32[]{:S(2)}) copy-start(f32[1024,256]{1,0:T(8,128)} %mul.181) | copy-start | bytes 3145732
  128.3 11.5 %collective-permute-start.7 = (f32[3,16,1,256]{3,2,1,0:T(1,128)S(1)}, f32[3,16,1,256]{3,2,1,0:T(1,128)S(1)}, u32[]{:S(2)}, u32[]{:S(2)}) collective-permute-start(f32[3,16,1,256]{3,2,1,0:T(1,128)S(1)} %get-tuple-element.18), channel_id=1, source_target_pairs={{1,0},{0,1},{3,2},{2,3},{5,4},{4,5},{7,6},{6,7},{9,8},{8,9},{11,10... | collective-permute-start | bytes 147464 | tf_op jit(solution)/shard_map/ppermute | solution.py:238
  129.0 10.9 %collective-permute-start.6 = (f32[3,16,1,256]{3,2,1,0:T(1,128)S(1)}, f32[3,16,1,256]{3,2,1,0:T(1,128)S(1)}, u32[]{:S(2)}, u32[]{:S(2)}) collective-permute-start(f32[3,16,1,256]{3,2,1,0:T(1,128)S(1)} %get-tuple-element.19), channel_id=1, source_target_pairs={{0,1},{1,0},{2,3},{3,2},{4,5},{5,4},{6,7},{7,6},{8,9},{9,8},{10,11... | collective-permute-start | bytes 147464 | tf_op jit(solution)/shard_map/ppermute | solution.py:237
  129.9 10.0 %collective-permute-start.5 = (f32[3,1,64,256]{3,2,1,0:T(8,128)}, f32[3,1,64,256]{3,2,1,0:T(8,128)S(1)}, u32[]{:S(2)}, u32[]{:S(2)}) collective-permute-start(f32[3,1,64,256]{3,2,1,0:T(8,128)} %get-tuple-element.20), channel_id=1, source_target_pairs={{2,0},{4,2},{6,4},{8,6},{10,8},{12,10},{14,12},{16,14},{18,16},{20... | collective-permute-start | bytes 589832 | tf_op jit(solution)/shard_map/ppermute | solution.py:238
  131.4 8.4 %collective-permute-start.4 = (f32[3,1,64,256]{3,2,1,0:T(8,128)}, f32[3,1,64,256]{3,2,1,0:T(8,128)S(1)}, u32[]{:S(2)}, u32[]{:S(2)}) collective-permute-start(f32[3,1,64,256]{3,2,1,0:T(8,128)} %get-tuple-element.21), channel_id=1, source_target_pairs={{0,2},{2,4},{4,6},{6,8},{8,10},{10,12},{12,14},{14,16},{16,18},{18... | collective-permute-start | bytes 589832 | tf_op jit(solution)/shard_map/ppermute | solution.py:237

commit v3 on v2

--- a/solution.py
+++ b/solution.py
@@ -63,14 +63,11 @@
 
 
 def advance_kernel(count_y, group, exchange, *refs):
-    if exchange:
-        (cols_ref, fringe_ref, a_ref, w_ref, e_ref, s_ref, n_ref, u_ref, drag_ref, eddy_ref, part_ref,
-         out_ref, sum_ref, xq, prod, near, far, sems) = refs
-    else:
-        (cols_ref, fringe_ref, a_ref, w_ref, e_ref, s_ref, n_ref, u_ref, drag_ref, eddy_ref,
-         out_ref, xq, prod) = refs
+    (cols_ref, fringe_ref, a_ref, w_ref, e_ref, s_ref, n_ref, u_ref, drag_ref, eddy_ref, pk_ref, azh_ref,
+     prior_ref, out_ref, sum_ref, xq, prod) = refs[:17]
     components, width_x, width_y, height = a_ref.shape
     if exchange:
+        near, far, sems = refs[17:]
         total = lax.axis_size("gx") * count_y
         groups = total // group
         me = lax.axis_index("gx") * count_y + lax.axis_index("gy")
@@ -96,22 +93,34 @@
 
         lax.fori_loop(1, group, greet_near, 0)
         lax.fori_loop(1, groups, greet_far, 0)
+
+    def turbine_plane(x, acc):
+        velocity = u_ref[0, x].astype(jnp.float32)
+        density = velocity * velocity * a_ref[0, x]
+        projected = jnp.dot(
+            density, azh_ref[...], precision=lax.Precision.HIGHEST, preferred_element_type=jnp.float32
+        )
+        return acc + pk_ref[x] * projected
+
+    acc = lax.fori_loop(0, width_x, turbine_plane, jnp.zeros(pk_ref.shape[1:], jnp.float32))
+    first_row = lax.broadcasted_iota(jnp.int32, prior_ref.shape, 0) == 0
+    part = prior_ref[...] + jnp.where(first_row, jnp.sum(acc, axis=0, keepdims=True), 0.0)
+    if exchange:
         pl.semaphore_wait(barrier, group + groups - 2)
-        near[mine] = part_ref[...]
+        near[mine] = part
 
         def send_near(i, carry):
             pltpu.make_async_remote_copy(
-                src_ref=part_ref, dst_ref=near.at[mine], send_sem=sems.at[0], recv_sem=sems.at[1],
+                src_ref=near.at[mine], dst_ref=near.at[mine], send_sem=sems.at[0], recv_sem=sems.at[1],
                 device_id=near_device(i), device_id_type=MESH,
             ).start()
             return carry
 
         lax.fori_loop(1, group, send_near, 0)
+    else:
+        sum_ref[...] = part
+
     half = height // NZB
-    def fill(px, src):
-        for zb in range(NZB):
-            for c in range(components):
-                xq[2 * px + zb, c * width_y : (c + 1) * width_y, :] = src[c, :, zb * half : (zb + 1) * half].astype(jnp.bfloat16)
 
     def fill_plane(x, carry):
         for zb in range(NZB):
@@ -192,42 +201,45 @@
         sum_ref[...] = jnp.sum(far[...], axis=0)
 
 
-def advance(adjoint, west, east, south, north, forward, columns, eddy_blocks, drag_field, fringe_scale, part=None):
+def advance(adjoint, west, east, south, north, forward, columns, eddy_blocks, drag_field, fringe_scale, turbine, prior, exchange):
     components, width_x, width_y, height = adjoint.shape
     vmem = pl.BlockSpec(memory_space=pltpu.VMEM)
     smem = pl.BlockSpec(memory_space=pltpu.SMEM)
     count_y = lax.axis_size("gy")
     total = lax.axis_size("gx") * count_y
     group = 8 if total % 8 == 0 and total > 8 else total // 2
-    exchange = part is not None
     operands = [columns, fringe_scale, adjoint, west, east, south, north, forward, drag_field, eddy_blocks]
-    out_shape = [jax.ShapeDtypeStruct(adjoint.shape, jnp.float32)]
+    operands += list(turbine) + [prior]
+    out_shape = (jax.ShapeDtypeStruct(adjoint.shape, jnp.float32), jax.ShapeDtypeStruct(prior.shape, jnp.float32))
     scratch = [
         pltpu.VMEM(((width_x + 2) * NZB, components * width_y, height // NZB), jnp.bfloat16),
         pltpu.VMEM((width_x * NZB, components * width_y, height // NZB), jnp.float32),
     ]
     params = dict(vmem_limit_bytes=48 * 1024 * 1024)
     if exchange:
-        width = part.shape[0]
-        operands.append(jnp.zeros((8, 128), jnp.float32).at[0, :width].set(part))
-        out_shape.append(jax.ShapeDtypeStruct((8, 128), jnp.float32))
         scratch += [
-            pltpu.VMEM((group, 8, 128), jnp.float32),
-            pltpu.VMEM((total // group, 8, 128), jnp.float32),
+            pltpu.VMEM((group,) + prior.shape, jnp.float32),
+            pltpu.VMEM((total // group,) + prior.shape, jnp.float32),
             pltpu.SemaphoreType.DMA((4,)),
         ]
         params.update(collective_id=0, has_side_effects=True)
-    results = pl.pallas_call(
+    return pl.pallas_call(
         functools.partial(advance_kernel, count_y, group, exchange),
-        out_shape=tuple(out_shape),
+        out_shape=out_shape,
         in_specs=[smem, smem] + [vmem] * (len(operands) - 2),
-        out_specs=tuple([vmem] * len(out_shape)),
+        out_specs=(vmem, vmem),
         scratch_shapes=scratch,
         compiler_params=pltpu.CompilerParams(**params),
     )(*operands)
-    if exchange:
-        return results[0], results[1][0, :width]
-    return results[0]
+
+
+def turbine_tables(owned_mask, plan_kernel, along_z, width_x, width_y):
+    lanes = 128
+    count = plan_kernel.shape[0]
+    weights = (plan_kernel * owned_mask[:, None]).T.reshape(width_x, width_y, count)
+    weights = jnp.zeros((width_x, width_y, lanes), jnp.float32).at[:, :, :count].set(weights)
+    column = jnp.zeros((along_z.shape[1], lanes), jnp.float32).at[:, :count].set(along_z.T)
+    return weights, column
 
 
 def halo(block, axis, dim):
@@ -237,14 +249,6 @@
     low = lax.ppermute(lax.slice_in_dim(block, block.shape[dim] - 1, None, axis=dim), axis, forward)
     high = lax.ppermute(lax.slice_in_dim(block, 0, 1, axis=dim), axis, backward)
     return low, high
-
-
-def gradient_terms(adjoint, forward, owned_mask, plan_kernel, along_z):
-    components, width_x, width_y, height = adjoint.shape
-    velocity = forward[0].astype(jnp.float32)
-    density = (velocity * velocity * adjoint[0]).reshape(width_x * width_y, height)
-    projected = jnp.dot(density, along_z.T, precision=lax.Precision.HIGHEST)
-    return owned_mask * jnp.sum(plan_kernel.T * projected, axis=0)
 
 
 def shards(
@@ -283,8 +287,9 @@
     owned_mask, plan_kernel, along_z, drag_field = turbine_terms(
         tile_index, thrust, yaw_angle, turbine_place, turbine_tile, width_x, width_y, height
     )
+    turbine = turbine_tables(owned_mask, plan_kernel, along_z, width_x, width_y)
     adjoint = adjoint_in
-    gradient_sum = jnp.zeros((thrust.shape[0],), jnp.float32)
+    gradient_block = jnp.zeros((8, 128), jnp.float32)
     for step_index in range(steps_total):
         stored = checkpoints[steps_total - 1 - step_index]
         packed = jnp.einsum(
@@ -297,16 +302,11 @@
         forward = forward.reshape(components, width_x, width_y, height)
         west, east = halo(adjoint, "gx", 1)
         south, north = halo(adjoint, "gy", 2)
-        gradient_sum = gradient_sum + gradient_terms(adjoint, forward, owned_mask, plan_kernel, along_z)
-        last = step_index == steps_total - 1
-        stepped = advance(
+        adjoint, gradient_block = advance(
             adjoint, west, east, south, north, forward, block_columns, eddy_blocks, drag_field, fringe_scale,
-            gradient_sum if last else None,
-        )
-        if last:
-            adjoint, gradient_sum = stepped
-        else:
-            adjoint = stepped
+            turbine, gradient_block, step_index == steps_total - 1,
+        )
+    gradient_sum = gradient_block[0, : thrust.shape[0]]
     cosine = jnp.cos(yaw_angle)
     sine = jnp.sin(yaw_angle)
     control_gradient = jnp.stack(

time: 167 us -> 153 us (0.916)
  local copies, waits for them, and re-layouts: 43.3 us -> 33.8 us
  Pallas kernels: 37 us -> 43.6 us
  waiting for transfers between devices: 32.1 us -> 26 us
  matrix products: 15.1 us -> 10.7 us
  other arithmetic: 7.73 us -> 5.49 us
    mul x5 -> x0, local copies, waits for them, and re-layouts: 8.86 us -> none  [the longest x4 8.65 us: gradient_terms(): velocity * velocity * adjoint[0]]
    pallas_call x2, Pallas kernels: 37 us -> 43.6 us  [advance(): pl.pallas_call(functools.partial(advance_kernel, count_y, group, exchange...]
    all_to_all x2, waiting for transfers between devices: 32.1 us -> 26 us  [shards(): lax.all_to_all(packed, ('gx', 'gy'), split_axis=0, concat_axis=0, tiled=T...]
    mul x4 -> x1, other arithmetic: 4.07 us -> 0.07 us  [turbine_tables(): plan_kernel * owned_mask[:, None]]
    dot_general x2 -> x0, matrix products: 2.55 us -> none  [gradient_terms(): projected = jnp.dot(density, along_z.T, precision=lax.Precision.HIGHEST)]
    slice x3 -> x0, local copies, waits for them, and re-layouts: 2.31 us -> none  [gradient_terms(): adjoint[0]]
    dot_general x2, matrix products: 6.65 us -> 4.8 us  [shards(): jnp.einsum('jsr,scrb->cjb', pick_table, arrived, preferred_element_type=j...]
    unnamed x28 -> x42, local copies, waits for them, and re-layouts: 6.53 us -> 8.33 us
  transfers between devices with their start and end apart: 10 -> 10, of which waited for: 2 -> 2; matrix products, arithmetic and copies ran while one was open for 20% -> 21% of each run, Pallas kernels for 10% -> 14%
where the time goes in v3:
time: 153 us; the launch traced here: 150 us
  Pallas kernels  43.6 us (28%)
  local copies, waits for them, and re-layouts  33.8 us (22%)
  starting transfers between devices  29.1 us (19%)
  waiting for transfers between devices  26 us (17%)
  matrix products  10.7 us (7%)
  other arithmetic  5.49 us (4%)
    pallas_call x2, Pallas kernels, advance(): pl.pallas_call(functools.partial(advance_kernel, count_y, group, exchange...  43.6 us
    all_to_all x2, waiting for transfers between devices, shards(): lax.all_to_all(packed, ('gx', 'gy'), split_axis=0, concat_axis=0, tiled=T...  26 us
    all_to_all x2, starting transfers between devices, shards(): lax.all_to_all(packed, ('gx', 'gy'), split_axis=0, concat_axis=0, tiled=T...  18 us
    convert_element_type x2, local copies, waits for them, and re-layouts, shards(): packed = jnp.einsum('drs,scb->dcrb', pack_table, stored, preferred_elemen...  9.77 us
    unnamed x42, local copies, waits for them, and re-layouts  8.33 us
    slice x4, local copies, waits for them, and re-layouts, halo(): high = lax.ppermute(lax.slice_in_dim(block, 0, 1, axis=dim), axis, backward)  7.24 us
    ppermute x4, starting transfers between devices, halo(): high = lax.ppermute(lax.slice_in_dim(block, 0, 1, axis=dim), axis, backward)  6.36 us
    reshape x2, local copies, waits for them, and re-layouts, shards(): forward = forward.reshape(components, width_x, width_y, height)  5.16 us
  transfers between devices with their start and end apart: 10, of which 2 were waited for; matrix products, arithmetic and copies ran while one was open for 21% of the time, Pallas kernels for 14%

profile of v3, /device:TPU:1, one launch (start us, length us, event | category | flops | bytes accessed | tf_op | source)
XLA Modules:
  0.0 149.7 jit_solution(2340313143872918612)
XLA Ops:
  3.1 2.4 %fusion.4 = bf16[128,3,2,2048]{3,0,1,2:T(8,128)(2,1)S(1)} fusion(bf16[2,128,3,2048]{3,1,2,0:T(8,128)(2,1)} %param.16, s32[128]{0:T(128)S(1)} %add_add_fusion, s32[128,2]{0,1:T(2,128)S(1)} %multiply_add_fusion), kind=kOutput, calls=%fused_computation.8 | convolution fusion | flops 404258816 | bytes 4720128 | tf_op jit(solution)/shard_map/drs,scb->dcrb/dot_general | solution.py:295
  5.5 4.9 %copy.25 = bf16[128,3,2,2048]{3,2,1,0:T(2,128)(2,1)} copy(bf16[128,3,2,2048]{3,0,1,2:T(8,128)(2,1)S(1)} %fusion.4) | data formatting | bytes 6291456 | tf_op jit(solution)/shard_map/convert_element_type | solution.py:297
  10.4 11.5 %all-to-all-start = ((bf16[128,3,2,2048]{3,2,1,0:T(2,128)(2,1)}), bf16[128,3,2,2048]{3,2,1,0:T(2,128)(2,1)S(1)}, u32[]{:S(2)}, u32[]{:S(2)}) async-start(bf16[128,3,2,2048]{3,2,1,0:T(2,128)(2,1)} %copy.25), calls=%async_computation | async-start | bytes 6291456 | tf_op jit(solution)/shard_map/all_to_all | solution.py:298
  21.9 1.8 %fusion.53 = (f32[3,16,1,256]{3,2,1,0:T(1,128)}, f32[3,16,1,256]{3,2,1,0:T(1,128)}) fusion(f32[3,16,64,256]{3,2,1,0:T(8,128)} %refs_2_.1), kind=kLoop, calls=%fused_computation.72 | loop fusion | bytes 196608 | tf_op jit(solution)/shard_map/slice | solution.py:250
  25.3 1.8 %fusion.54 = (f32[3,1,64,256]{3,2,1,0:T(8,128)}, f32[3,1,64,256]{3,2,1,0:T(8,128)}) fusion(f32[3,16,64,256]{3,2,1,0:T(8,128)} %refs_2_.1), kind=kLoop, calls=%fused_computation.73 | loop fusion | bytes 786432 | tf_op jit(solution)/shard_map/slice | solution.py:250
  28.6 2.5 %collective-permute-start = (f32[3,1,64,256]{3,2,1,0:T(8,128)}, f32[3,1,64,256]{3,2,1,0:T(8,128)}, u32[]{:S(2)}, u32[]{:S(2)}) collective-permute-start(f32[3,1,64,256]{3,2,1,0:T(8,128)} %get-tuple-element.41), channel_id=1, source_target_pairs={{0,2},{2,4},{4,6},{6,8},{8,10},{10,12},{12,14},{14,16},{16,18},{18... | collective-permute-start | bytes 589832 | tf_op jit(solution)/shard_map/ppermute | solution.py:249
  31.2 2.4 %fusion.5 = bf16[128,3,2,2048]{3,0,1,2:T(8,128)(2,1)S(1)} fusion(bf16[2,128,3,2048]{3,1,2,0:T(8,128)(2,1)} %param.16, s32[128]{0:T(128)S(1)} %add_add_fusion, s32[128,2]{0,1:T(2,128)S(1)} %multiply_add_fusion), kind=kOutput, calls=%fused_computation.9 | convolution fusion | flops 404258816 | bytes 4720128 | tf_op jit(solution)/shard_map/drs,scb->dcrb/dot_general | solution.py:295
  33.7 4.9 %copy.29 = bf16[128,3,2,2048]{3,2,1,0:T(2,128)(2,1)} copy(bf16[128,3,2,2048]{3,0,1,2:T(8,128)(2,1)S(1)} %fusion.5) | data formatting | bytes 6291456 | tf_op jit(solution)/shard_map/convert_element_type | solution.py:297
  39.2 24.2 %all-to-all-done = bf16[128,3,2,2048]{3,2,1,0:T(2,128)(2,1)S(1)} async-done(((bf16[128,3,2,2048]{3,2,1,0:T(2,128)(2,1)}), bf16[128,3,2,2048]{3,2,1,0:T(2,128)(2,1)S(1)}, u32[]{:S(2)}, u32[]{:S(2)}) %all-to-all-start) | async-done | bytes 3145760 | tf_op jit(solution)/shard_map/all_to_all | solution.py:298
  63.4 1.7 %copy-done.5 = bf16[128,3,2,2048]{3,2,1,0:T(2,128)(2,1)} copy-done((bf16[128,3,2,2048]{3,2,1,0:T(2,128)(2,1)}, bf16[128,3,2,2048]{3,2,1,0:T(2,128)(2,1)S(1)}, u32[]{:S(2)}) %copy-start.5) | copy-done | bytes 3145752
  65.1 6.5 %all-to-all-start.1 = ((bf16[128,3,2,2048]{3,2,1,0:T(2,128)(2,1)}), bf16[128,3,2,2048]{3,2,1,0:T(2,128)(2,1)}, u32[]{:S(2)}, u32[]{:S(2)}) async-start(bf16[128,3,2,2048]{3,2,1,0:T(2,128)(2,1)} %copy.29), calls=%async_computation.1 | async-start | bytes 6291456 | tf_op jit(solution)/shard_map/all_to_all | solution.py:298
  76.1 1.6 %copy.27 = bf16[3,128,2048]{2,1,0:T(8,128)(2,1)} copy(bf16[3,128,2048]{1,2,0:T(8,128)(2,1)S(1)} %fusion.10) | data formatting | bytes 3145728 | tf_op jit(solution)/shard_map/convert_element_type | solution.py:301
  77.7 2.6 %reshape.191.refs_7_ = bf16[3,16,64,256]{3,2,1,0:T(8,128)(2,1)S(1)} reshape(bf16[3,128,2048]{2,1,0:T(8,128)(2,1)} %copy.27) | data formatting | bytes 3145728 | tf_op jit(solution)/shard_map/reshape | solution.py:302
  81.0 20.2 %shard_map.122 = (f32[3,16,64,256]{3,2,1,0:T(8,128)}, f32[8,128]{1,0:T(8,128)S(1)}) custom-call(s32[32,8]{1,0:T(8,128)S(1)} %copy.32.refs_0_, f32[16]{0:T(128)S(1)} %copy-done.3, f32[3,16,64,256]{3,2,1,0:T(8,128)} %refs_2_.1, f32[3,1,64,256]{3,2,1,0:T(8,128)} %collective-permute-done.refs_3_, f32[3,1,64,256]{3,2,1,0:T(8,128)} %collective-permute-done.1.refs_4_, ...), custom_call_target="tpu_custom_call" | custom-call | tf_op jit(solution)/shard_map/pallas_call | solution.py:226
  101.9 1.8 %fusion.51 = (f32[3,16,1,256]{3,2,1,0:T(1,128)}, f32[3,16,1,256]{3,2,1,0:T(1,128)}) fusion(f32[3,16,64,256]{3,2,1,0:T(8,128)} %get-tuple-element.30.refs_2_), kind=kLoop, calls=%fused_computation.70 | loop fusion | bytes 196608 | tf_op jit(solution)/shard_map/slice | solution.py:250
  105.2 1.8 %fusion.52 = (f32[3,1,64,256]{3,2,1,0:T(8,128)}, f32[3,1,64,256]{3,2,1,0:T(8,128)}) fusion(f32[3,16,64,256]{3,2,1,0:T(8,128)} %get-tuple-element.30.refs_2_), kind=kLoop, calls=%fused_computation.71 | loop fusion | bytes 786432 | tf_op jit(solution)/shard_map/slice | solution.py:250
  107.0 1.8 %collective-permute-start.5 = (f32[3,1,64,256]{3,2,1,0:T(8,128)}, f32[3,1,64,256]{3,2,1,0:T(8,128)}, u32[]{:S(2)}, u32[]{:S(2)}) collective-permute-start(f32[3,1,64,256]{3,2,1,0:T(8,128)} %get-tuple-element.36), channel_id=1, source_target_pairs={{2,0},{4,2},{6,4},{8,6},{10,8},{12,10},{14,12},{16,14},{18,16},{20... | collective-permute-start | bytes 589832 | tf_op jit(solution)/shard_map/ppermute | solution.py:250
  108.8 2.2 %collective-permute-start.4 = (f32[3,1,64,256]{3,2,1,0:T(8,128)}, f32[3,1,64,256]{3,2,1,0:T(8,128)}, u32[]{:S(2)}, u32[]{:S(2)}) collective-permute-start(f32[3,1,64,256]{3,2,1,0:T(8,128)} %get-tuple-element.37), channel_id=1, source_target_pairs={{0,2},{2,4},{4,6},{6,8},{8,10},{10,12},{12,14},{14,16},{16,18},{18... | collective-permute-start | bytes 589832 | tf_op jit(solution)/shard_map/ppermute | solution.py:249
  111.1 1.8 %all-to-all-done.1 = bf16[128,3,2,2048]{3,2,1,0:T(2,128)(2,1)} async-done(((bf16[128,3,2,2048]{3,2,1,0:T(2,128)(2,1)}), bf16[128,3,2,2048]{3,2,1,0:T(2,128)(2,1)}, u32[]{:S(2)}, u32[]{:S(2)}) %all-to-all-start.1) | async-done | bytes 3145760 | tf_op jit(solution)/shard_map/all_to_all | solution.py:298
  112.8 3.3 %fusion.13 = bf16[3,128,2048]{1,2,0:T(8,128)(2,1)S(1)} fusion(bf16[128,3,2,2048]{3,2,1,0:T(2,128)(2,1)} %all-to-all-done.1, s32[128,2]{0,1:T(2,128)} %copy-done.7, s32[128]{0:T(128)} %param.18), kind=kOutput, calls=%fused_computation.11 | convolution fusion | flops 403472384 | bytes 4720128 | tf_op jit(solution)/shard_map/jsr,scrb->cjb/dot_general | solution.py:299
  116.2 1.6 %copy.31 = bf16[3,128,2048]{2,1,0:T(8,128)(2,1)} copy(bf16[3,128,2048]{1,2,0:T(8,128)(2,1)S(1)} %fusion.13) | data formatting | bytes 3145728 | tf_op jit(solution)/shard_map/convert_element_type | solution.py:301
  117.8 2.6 %reshape.193.refs_7_ = bf16[3,16,64,256]{3,2,1,0:T(8,128)(2,1)S(1)} reshape(bf16[3,128,2048]{2,1,0:T(8,128)(2,1)} %copy.31) | data formatting | bytes 3145728 | tf_op jit(solution)/shard_map/reshape | solution.py:302
  121.8 23.4 %shard_map.123 = (f32[3,16,64,256]{3,2,1,0:T(8,128)}, f32[8,128]{1,0:T(8,128)S(1)}) custom-call(s32[32,8]{1,0:T(8,128)S(1)} %copy.32.refs_0_, f32[16]{0:T(128)S(1)} %copy-done.4, f32[3,16,64,256]{3,2,1,0:T(8,128)} %get-tuple-element.30.refs_2_, f32[3,1,64,256]{3,2,1,0:T(8,128)} %collective-permute-done.4.refs_3_, ...), custom_call_target="tpu_custom_call" | custom-call | tf_op jit(solution)/shard_map/pallas_call | solution.py:226
  145.8 3.9 %copy.49 = f32[3,16,64,256]{3,2,1,0:T(8,128)} copy(f32[3,16,64,256]{3,2,1,0:T(8,128)} %get-tuple-element.51) | data formatting | bytes 6291456
  (78 shorter events, 15.5 us)
Async XLA Ops:
  0.6 30.6 %copy-start.7 = (s32[128,2]{0,1:T(2,128)}, s32[128,2]{0,1:T(2,128)S(1)}, u32[]{:S(2)}) copy-start(s32[128,2]{0,1:T(2,128)S(1)} %multiply_add_fusion) | copy-start | bytes 3076
  10.4 20.7 %copy-start.16 = (f32[80]{0:T(128)S(1)}, f32[80]{0:T(128)}, u32[]{:S(2)}) copy-start(f32[80]{0:T(128)} %param.22) | copy-start | bytes 964
  10.4 20.7 %copy-start.9 = (s32[32,8]{0,1:T(8,128)S(1)}, s32[32,8]{0,1:T(8,128)}, u32[]{:S(2)}) copy-start(s32[32,8]{0,1:T(8,128)} %param.19) | copy-start | bytes 3076
  10.4 53.0 %all-to-all-start = ((bf16[128,3,2,2048]{3,2,1,0:T(2,128)(2,1)}), bf16[128,3,2,2048]{3,2,1,0:T(2,128)(2,1)S(1)}, u32[]{:S(2)}, u32[]{:S(2)}) async-start(bf16[128,3,2,2048]{3,2,1,0:T(2,128)(2,1)} %copy.25), calls=%async_computation | async-start | bytes 6291456 | tf_op jit(solution)/shard_map/all_to_all | solution.py:298
  23.7 56.6 %collective-permute-start.3 = (f32[3,16,1,256]{3,2,1,0:T(1,128)}, f32[3,16,1,256]{3,2,1,0:T(1,128)}, u32[]{:S(2)}, u32[]{:S(2)}) collective-permute-start(f32[3,16,1,256]{3,2,1,0:T(1,128)} %get-tuple-element.38), channel_id=1, source_target_pairs={{1,0},{0,1},{3,2},{2,3},{5,4},{4,5},{7,6},{6,7},{9,8},{8,9},{11,10... | collective-permute-start | bytes 147464 | tf_op jit(solution)/shard_map/ppermute | solution.py:250
  25.2 55.1 %collective-permute-start.2 = (f32[3,16,1,256]{3,2,1,0:T(1,128)}, f32[3,16,1,256]{3,2,1,0:T(1,128)}, u32[]{:S(2)}, u32[]{:S(2)}) collective-permute-start(f32[3,16,1,256]{3,2,1,0:T(1,128)} %get-tuple-element.39), channel_id=1, source_target_pairs={{0,1},{1,0},{2,3},{3,2},{4,5},{5,4},{6,7},{7,6},{8,9},{9,8},{10,11... | collective-permute-start | bytes 147464 | tf_op jit(solution)/shard_map/ppermute | solution.py:249
  27.1 53.3 %collective-permute-start.1 = (f32[3,1,64,256]{3,2,1,0:T(8,128)}, f32[3,1,64,256]{3,2,1,0:T(8,128)}, u32[]{:S(2)}, u32[]{:S(2)}) collective-permute-start(f32[3,1,64,256]{3,2,1,0:T(8,128)} %get-tuple-element.40), channel_id=1, source_target_pairs={{2,0},{4,2},{6,4},{8,6},{10,8},{12,10},{14,12},{16,14},{18,16},{20... | collective-permute-start | bytes 589832 | tf_op jit(solution)/shard_map/ppermute | solution.py:250
  28.6 51.7 %collective-permute-start = (f32[3,1,64,256]{3,2,1,0:T(8,128)}, f32[3,1,64,256]{3,2,1,0:T(8,128)}, u32[]{:S(2)}, u32[]{:S(2)}) collective-permute-start(f32[3,1,64,256]{3,2,1,0:T(8,128)} %get-tuple-element.41), channel_id=1, source_target_pairs={{0,2},{2,4},{4,6},{6,8},{8,10},{10,12},{12,14},{14,16},{16,18},{18... | collective-permute-start | bytes 589832 | tf_op jit(solution)/shard_map/ppermute | solution.py:249
  31.1 41.4 %copy-start.12 = (f32[80]{0:T(128)}, f32[80]{0:T(128)S(1)}, u32[]{:S(2)}) copy-start(f32[80]{0:T(128)S(1)} %cos.4) | copy-start | bytes 964
  33.6 5.5 %copy-start.14 = (f32[3,80]{1,0:T(4,128)S(1)}, f32[3,80]{1,0:T(4,128)}, u32[]{:S(2)}) copy-start(f32[3,80]{1,0:T(4,128)} %param.23) | copy-start | bytes 2884
  39.2 33.3 %copy-start.15 = (s32[80]{0:T(128)S(1)}, s32[80]{0:T(128)}, u32[]{:S(2)}) copy-start(s32[80]{0:T(128)} %param.24) | copy-start | bytes 964
  39.2 33.3 %copy-start.10 = (f32[80]{0:T(128)S(1)}, f32[80]{0:T(128)}, u32[]{:S(2)}) copy-start(f32[80]{0:T(128)} %param.21) | copy-start | bytes 964
  65.1 47.7 %all-to-all-start.1 = ((bf16[128,3,2,2048]{3,2,1,0:T(2,128)(2,1)}), bf16[128,3,2,2048]{3,2,1,0:T(2,128)(2,1)}, u32[]{:S(2)}, u32[]{:S(2)}) async-start(bf16[128,3,2,2048]{3,2,1,0:T(2,128)(2,1)} %copy.29), calls=%async_computation.1 | async-start | bytes 6291456 | tf_op jit(solution)/shard_map/all_to_all | solution.py:298
  71.6 3.0 %copy-start.6 = (bf16[128,3,2,2048]{3,2,1,0:T(2,128)(2,1)S(1)}, bf16[128,3,2,2048]{3,2,1,0:T(2,128)(2,1)}, u32[]{:S(2)}) copy-start(bf16[128,3,2,2048]{3,2,1,0:T(2,128)(2,1)} %copy-done.5) | copy-start | bytes 9437188
  71.6 3.0 %copy-start.8 = (s32[128,2]{0,1:T(2,128)S(1)}, s32[128,2]{0,1:T(2,128)}, u32[]{:S(2)}) copy-start(s32[128,2]{0,1:T(2,128)} %copy-done.7) | copy-start | bytes 3076
  71.6 3.0 %copy-start.19 = (s32[128]{0:T(128)S(1)}, s32[128]{0:T(128)}, u32[]{:S(2)}) copy-start(s32[128]{0:T(128)} %param.18) | copy-start | bytes 1540
  76.1 4.2 %copy-start = (bf16[8,128,128]{2,1,0:T(8,128)(2,1)S(1)}, bf16[8,128,128]{2,1,0:T(8,128)(2,1)}, u32[]{:S(2)}) copy-start(bf16[8,128,128]{2,1,0:T(8,128)(2,1)} %refs_9_.3) | copy-start | bytes 786436
  103.7 16.7 %collective-permute-start.7 = (f32[3,16,1,256]{3,2,1,0:T(1,128)}, f32[3,16,1,256]{3,2,1,0:T(1,128)}, u32[]{:S(2)}, u32[]{:S(2)}) collective-permute-start(f32[3,16,1,256]{3,2,1,0:T(1,128)} %get-tuple-element.34), channel_id=1, source_target_pairs={{1,0},{0,1},{3,2},{2,3},{5,4},{4,5},{7,6},{6,7},{9,8},{8,9},{11,10... | collective-permute-start | bytes 147464 | tf_op jit(solution)/shard_map/ppermute | solution.py:250
  105.2 15.2 %collective-permute-start.6 = (f32[3,16,1,256]{3,2,1,0:T(1,128)}, f32[3,16,1,256]{3,2,1,0:T(1,128)}, u32[]{:S(2)}, u32[]{:S(2)}) collective-permute-start(f32[3,16,1,256]{3,2,1,0:T(1,128)} %get-tuple-element.35), channel_id=1, source_target_pairs={{0,1},{1,0},{2,3},{3,2},{4,5},{5,4},{6,7},{7,6},{8,9},{9,8},{10,11... | collective-permute-start | bytes 147464 | tf_op jit(solution)/shard_map/ppermute | solution.py:249
  107.0 13.3 %collective-permute-start.5 = (f32[3,1,64,256]{3,2,1,0:T(8,128)}, f32[3,1,64,256]{3,2,1,0:T(8,128)}, u32[]{:S(2)}, u32[]{:S(2)}) collective-permute-start(f32[3,1,64,256]{3,2,1,0:T(8,128)} %get-tuple-element.36), channel_id=1, source_target_pairs={{2,0},{4,2},{6,4},{8,6},{10,8},{12,10},{14,12},{16,14},{18,16},{20... | collective-permute-start | bytes 589832 | tf_op jit(solution)/shard_map/ppermute | solution.py:250
  108.8 11.6 %collective-permute-start.4 = (f32[3,1,64,256]{3,2,1,0:T(8,128)}, f32[3,1,64,256]{3,2,1,0:T(8,128)}, u32[]{:S(2)}, u32[]{:S(2)}) collective-permute-start(f32[3,1,64,256]{3,2,1,0:T(8,128)} %get-tuple-element.37), channel_id=1, source_target_pairs={{0,2},{2,4},{4,6},{6,8},{8,10},{10,12},{12,14},{14,16},{16,18},{18... | collective-permute-start | bytes 589832 | tf_op jit(solution)/shard_map/ppermute | solution.py:249
  121.7 23.4 %copy-start.11 = (f32[80]{0:T(128)S(1)}, f32[80]{0:T(128)}, u32[]{:S(2)}) copy-start(f32[80]{0:T(128)} %param.21) | copy-start | bytes 964
  121.8 23.4 %copy-start.13 = (f32[80]{0:T(128)S(1)}, f32[80]{0:T(128)}, u32[]{:S(2)}) copy-start(f32[80]{0:T(128)} %copy-done.12) | copy-start | bytes 964
  121.8 23.4 %copy-start.17 = (f32[80]{0:T(128)S(1)}, f32[80]{0:T(128)}, u32[]{:S(2)}) copy-start(f32[80]{0:T(128)} %param.22) | copy-start | bytes 964
  (6 other events, 5.5 us)

commit v4 on v3

--- a/solution.py
+++ b/solution.py
@@ -136,8 +136,9 @@
 
     def eddy_block(p, carry):
         acc = jnp.zeros((components * width_y, half), jnp.float32)
-        for k in range(KB):
-            acc = acc + jnp.dot(xq[cols_ref[p, k]], eddy_ref[k], preferred_element_type=jnp.float32)
+        for k in range(0, KB, 2):
+            pair = jnp.concatenate([xq[cols_ref[p, k]], xq[cols_ref[p, k + 1]]], axis=1)
+            acc = acc + jnp.dot(pair, eddy_ref[k // 2], preferred_element_type=jnp.float32)
         prod[p] = acc
         return carry
 
@@ -208,7 +209,8 @@
     count_y = lax.axis_size("gy")
     total = lax.axis_size("gx") * count_y
     group = 8 if total % 8 == 0 and total > 8 else total // 2
-    operands = [columns, fringe_scale, adjoint, west, east, south, north, forward, drag_field, eddy_blocks]
+    paired = eddy_blocks.reshape(KB // 2, 2 * eddy_blocks.shape[1], eddy_blocks.shape[2])
+    operands = [columns, fringe_scale, adjoint, west, east, south, north, forward, drag_field, paired]
     operands += list(turbine) + [prior]
     out_shape = (jax.ShapeDtypeStruct(adjoint.shape, jnp.float32), jax.ShapeDtypeStruct(prior.shape, jnp.float32))
     scratch = [

time: 153 us -> 152 us (level)
  transfers between devices with their start and end apart: 10 -> 10, of which waited for: 2 -> 2; matrix products, arithmetic and copies ran while one was open for 21% -> 21% of each run, Pallas kernels for 14% -> 13%
where the time goes in v4:
time: 152 us; the launch traced here: 149 us
  Pallas kernels  43.2 us (28%)
  local copies, waits for them, and re-layouts  33.8 us (22%)
  starting transfers between devices  29.1 us (19%)
  waiting for transfers between devices  26.1 us (17%)
  matrix products  10.7 us (7%)
  other arithmetic  5.49 us (4%)
    pallas_call x2, Pallas kernels, advance(): pl.pallas_call(functools.partial(advance_kernel, count_y, group, exchange...  43.2 us
    all_to_all x2, waiting for transfers between devices, shards(): lax.all_to_all(packed, ('gx', 'gy'), split_axis=0, concat_axis=0, tiled=T...  26.1 us
    all_to_all x2, starting transfers between devices, shards(): lax.all_to_all(packed, ('gx', 'gy'), split_axis=0, concat_axis=0, tiled=T...  18 us
    convert_element_type x2, local copies, waits for them, and re-layouts, shards(): packed = jnp.einsum('drs,scb->dcrb', pack_table, stored, preferred_elemen...  9.77 us
    unnamed x42, local copies, waits for them, and re-layouts  8.33 us
    slice x4, local copies, waits for them, and re-layouts, halo(): high = lax.ppermute(lax.slice_in_dim(block, 0, 1, axis=dim), axis, backward)  7.24 us
    ppermute x4, starting transfers between devices, halo(): high = lax.ppermute(lax.slice_in_dim(block, 0, 1, axis=dim), axis, backward)  6.36 us
    reshape x2, local copies, waits for them, and re-layouts, shards(): forward = forward.reshape(components, width_x, width_y, height)  5.16 us
  transfers between devices with their start and end apart: 10, of which 2 were waited for; matrix products, arithmetic and copies ran while one was open for 21% of the time, Pallas kernels for 13%

profile of v4, /device:TPU:1, one launch (start us, length us, event | category | flops | bytes accessed | tf_op | source)
XLA Modules:
  0.0 149.4 jit_solution(16481342553683229610)
XLA Ops:
  3.1 2.4 %fusion.4 = bf16[128,3,2,2048]{3,0,1,2:T(8,128)(2,1)S(1)} fusion(bf16[2,128,3,2048]{3,1,2,0:T(8,128)(2,1)} %param.16, s32[128]{0:T(128)S(1)} %add_add_fusion, s32[128,2]{0,1:T(2,128)S(1)} %multiply_add_fusion), kind=kOutput, calls=%fused_computation.8 | convolution fusion | flops 404258816 | bytes 4720128 | tf_op jit(solution)/shard_map/drs,scb->dcrb/dot_general | solution.py:297
  5.5 4.9 %copy.25 = bf16[128,3,2,2048]{3,2,1,0:T(2,128)(2,1)} copy(bf16[128,3,2,2048]{3,0,1,2:T(8,128)(2,1)S(1)} %fusion.4) | data formatting | bytes 6291456 | tf_op jit(solution)/shard_map/convert_element_type | solution.py:299
  10.4 11.5 %all-to-all-start = ((bf16[128,3,2,2048]{3,2,1,0:T(2,128)(2,1)}), bf16[128,3,2,2048]{3,2,1,0:T(2,128)(2,1)S(1)}, u32[]{:S(2)}, u32[]{:S(2)}) async-start(bf16[128,3,2,2048]{3,2,1,0:T(2,128)(2,1)} %copy.25), calls=%async_computation | async-start | bytes 6291456 | tf_op jit(solution)/shard_map/all_to_all | solution.py:300
  21.9 1.8 %fusion.53 = (f32[3,16,1,256]{3,2,1,0:T(1,128)}, f32[3,16,1,256]{3,2,1,0:T(1,128)}) fusion(f32[3,16,64,256]{3,2,1,0:T(8,128)} %refs_2_.1), kind=kLoop, calls=%fused_computation.72 | loop fusion | bytes 196608 | tf_op jit(solution)/shard_map/slice | solution.py:252
  25.3 1.8 %fusion.54 = (f32[3,1,64,256]{3,2,1,0:T(8,128)}, f32[3,1,64,256]{3,2,1,0:T(8,128)}) fusion(f32[3,16,64,256]{3,2,1,0:T(8,128)} %refs_2_.1), kind=kLoop, calls=%fused_computation.73 | loop fusion | bytes 786432 | tf_op jit(solution)/shard_map/slice | solution.py:252
  28.6 2.5 %collective-permute-start = (f32[3,1,64,256]{3,2,1,0:T(8,128)}, f32[3,1,64,256]{3,2,1,0:T(8,128)}, u32[]{:S(2)}, u32[]{:S(2)}) collective-permute-start(f32[3,1,64,256]{3,2,1,0:T(8,128)} %get-tuple-element.41), channel_id=1, source_target_pairs={{0,2},{2,4},{4,6},{6,8},{8,10},{10,12},{12,14},{14,16},{16,18},{18... | collective-permute-start | bytes 589832 | tf_op jit(solution)/shard_map/ppermute | solution.py:251
  31.2 2.4 %fusion.5 = bf16[128,3,2,2048]{3,0,1,2:T(8,128)(2,1)S(1)} fusion(bf16[2,128,3,2048]{3,1,2,0:T(8,128)(2,1)} %param.16, s32[128]{0:T(128)S(1)} %add_add_fusion, s32[128,2]{0,1:T(2,128)S(1)} %multiply_add_fusion), kind=kOutput, calls=%fused_computation.9 | convolution fusion | flops 404258816 | bytes 4720128 | tf_op jit(solution)/shard_map/drs,scb->dcrb/dot_general | solution.py:297
  33.7 4.9 %copy.29 = bf16[128,3,2,2048]{3,2,1,0:T(2,128)(2,1)} copy(bf16[128,3,2,2048]{3,0,1,2:T(8,128)(2,1)S(1)} %fusion.5) | data formatting | bytes 6291456 | tf_op jit(solution)/shard_map/convert_element_type | solution.py:299
  39.2 24.2 %all-to-all-done = bf16[128,3,2,2048]{3,2,1,0:T(2,128)(2,1)S(1)} async-done(((bf16[128,3,2,2048]{3,2,1,0:T(2,128)(2,1)}), bf16[128,3,2,2048]{3,2,1,0:T(2,128)(2,1)S(1)}, u32[]{:S(2)}, u32[]{:S(2)}) %all-to-all-start) | async-done | bytes 3145760 | tf_op jit(solution)/shard_map/all_to_all | solution.py:300
  63.4 1.7 %copy-done.5 = bf16[128,3,2,2048]{3,2,1,0:T(2,128)(2,1)} copy-done((bf16[128,3,2,2048]{3,2,1,0:T(2,128)(2,1)}, bf16[128,3,2,2048]{3,2,1,0:T(2,128)(2,1)S(1)}, u32[]{:S(2)}) %copy-start.5) | copy-done | bytes 3145752
  65.1 6.5 %all-to-all-start.1 = ((bf16[128,3,2,2048]{3,2,1,0:T(2,128)(2,1)}), bf16[128,3,2,2048]{3,2,1,0:T(2,128)(2,1)}, u32[]{:S(2)}, u32[]{:S(2)}) async-start(bf16[128,3,2,2048]{3,2,1,0:T(2,128)(2,1)} %copy.29), calls=%async_computation.1 | async-start | bytes 6291456 | tf_op jit(solution)/shard_map/all_to_all | solution.py:300
  76.1 1.6 %copy.27 = bf16[3,128,2048]{2,1,0:T(8,128)(2,1)} copy(bf16[3,128,2048]{1,2,0:T(8,128)(2,1)S(1)} %fusion.10) | data formatting | bytes 3145728 | tf_op jit(solution)/shard_map/convert_element_type | solution.py:303
  77.7 2.6 %reshape.195.refs_7_ = bf16[3,16,64,256]{3,2,1,0:T(8,128)(2,1)S(1)} reshape(bf16[3,128,2048]{2,1,0:T(8,128)(2,1)} %copy.27) | data formatting | bytes 3145728 | tf_op jit(solution)/shard_map/reshape | solution.py:304
  81.0 20.1 %shard_map.122 = (f32[3,16,64,256]{3,2,1,0:T(8,128)}, f32[8,128]{1,0:T(8,128)S(1)}) custom-call(s32[32,8]{1,0:T(8,128)S(1)} %copy.32.refs_0_, f32[16]{0:T(128)S(1)} %copy-done.3, f32[3,16,64,256]{3,2,1,0:T(8,128)} %refs_2_.1, f32[3,1,64,256]{3,2,1,0:T(8,128)} %collective-permute-done.refs_3_, f32[3,1,64,256]{3,2,1,0:T(8,128)} %collective-permute-done.1.refs_4_, ...), custom_call_target="tpu_custom_call" | custom-call | tf_op jit(solution)/shard_map/pallas_call | solution.py:228
  101.7 1.8 %fusion.51 = (f32[3,16,1,256]{3,2,1,0:T(1,128)}, f32[3,16,1,256]{3,2,1,0:T(1,128)}) fusion(f32[3,16,64,256]{3,2,1,0:T(8,128)} %get-tuple-element.30.refs_2_), kind=kLoop, calls=%fused_computation.70 | loop fusion | bytes 196608 | tf_op jit(solution)/shard_map/slice | solution.py:252
  105.1 1.8 %fusion.52 = (f32[3,1,64,256]{3,2,1,0:T(8,128)}, f32[3,1,64,256]{3,2,1,0:T(8,128)}) fusion(f32[3,16,64,256]{3,2,1,0:T(8,128)} %get-tuple-element.30.refs_2_), kind=kLoop, calls=%fused_computation.71 | loop fusion | bytes 786432 | tf_op jit(solution)/shard_map/slice | solution.py:252
  106.9 1.8 %collective-permute-start.5 = (f32[3,1,64,256]{3,2,1,0:T(8,128)}, f32[3,1,64,256]{3,2,1,0:T(8,128)}, u32[]{:S(2)}, u32[]{:S(2)}) collective-permute-start(f32[3,1,64,256]{3,2,1,0:T(8,128)} %get-tuple-element.36), channel_id=1, source_target_pairs={{2,0},{4,2},{6,4},{8,6},{10,8},{12,10},{14,12},{16,14},{18,16},{20... | collective-permute-start | bytes 589832 | tf_op jit(solution)/shard_map/ppermute | solution.py:252
  108.7 2.2 %collective-permute-start.4 = (f32[3,1,64,256]{3,2,1,0:T(8,128)}, f32[3,1,64,256]{3,2,1,0:T(8,128)}, u32[]{:S(2)}, u32[]{:S(2)}) collective-permute-start(f32[3,1,64,256]{3,2,1,0:T(8,128)} %get-tuple-element.37), channel_id=1, source_target_pairs={{0,2},{2,4},{4,6},{6,8},{8,10},{10,12},{12,14},{14,16},{16,18},{18... | collective-permute-start | bytes 589832 | tf_op jit(solution)/shard_map/ppermute | solution.py:251
  110.9 1.9 %all-to-all-done.1 = bf16[128,3,2,2048]{3,2,1,0:T(2,128)(2,1)} async-done(((bf16[128,3,2,2048]{3,2,1,0:T(2,128)(2,1)}), bf16[128,3,2,2048]{3,2,1,0:T(2,128)(2,1)}, u32[]{:S(2)}, u32[]{:S(2)}) %all-to-all-start.1) | async-done | bytes 3145760 | tf_op jit(solution)/shard_map/all_to_all | solution.py:300
  112.8 3.3 %fusion.13 = bf16[3,128,2048]{1,2,0:T(8,128)(2,1)S(1)} fusion(bf16[128,3,2,2048]{3,2,1,0:T(2,128)(2,1)} %all-to-all-done.1, s32[128,2]{0,1:T(2,128)} %copy-done.7, s32[128]{0:T(128)} %param.18), kind=kOutput, calls=%fused_computation.11 | convolution fusion | flops 403472384 | bytes 4720128 | tf_op jit(solution)/shard_map/jsr,scrb->cjb/dot_general | solution.py:301
  116.2 1.6 %copy.31 = bf16[3,128,2048]{2,1,0:T(8,128)(2,1)} copy(bf16[3,128,2048]{1,2,0:T(8,128)(2,1)S(1)} %fusion.13) | data formatting | bytes 3145728 | tf_op jit(solution)/shard_map/convert_element_type | solution.py:303
  117.8 2.6 %reshape.198.refs_7_ = bf16[3,16,64,256]{3,2,1,0:T(8,128)(2,1)S(1)} reshape(bf16[3,128,2048]{2,1,0:T(8,128)(2,1)} %copy.31) | data formatting | bytes 3145728 | tf_op jit(solution)/shard_map/reshape | solution.py:304
  121.8 23.1 %shard_map.123 = (f32[3,16,64,256]{3,2,1,0:T(8,128)}, f32[8,128]{1,0:T(8,128)S(1)}) custom-call(s32[32,8]{1,0:T(8,128)S(1)} %copy.32.refs_0_, f32[16]{0:T(128)S(1)} %copy-done.4, f32[3,16,64,256]{3,2,1,0:T(8,128)} %get-tuple-element.30.refs_2_, f32[3,1,64,256]{3,2,1,0:T(8,128)} %collective-permute-done.4.refs_3_, ...), custom_call_target="tpu_custom_call" | custom-call | tf_op jit(solution)/shard_map/pallas_call | solution.py:228
  145.5 3.9 %copy.49 = f32[3,16,64,256]{3,2,1,0:T(8,128)} copy(f32[3,16,64,256]{3,2,1,0:T(8,128)} %get-tuple-element.51) | data formatting | bytes 6291456
  (78 shorter events, 15.5 us)
Async XLA Ops:
  0.6 30.6 %copy-start.7 = (s32[128,2]{0,1:T(2,128)}, s32[128,2]{0,1:T(2,128)S(1)}, u32[]{:S(2)}) copy-start(s32[128,2]{0,1:T(2,128)S(1)} %multiply_add_fusion) | copy-start | bytes 3076
  10.4 20.7 %copy-start.16 = (f32[80]{0:T(128)S(1)}, f32[80]{0:T(128)}, u32[]{:S(2)}) copy-start(f32[80]{0:T(128)} %param.22) | copy-start | bytes 964
  10.4 20.7 %copy-start.9 = (s32[32,8]{0,1:T(8,128)S(1)}, s32[32,8]{0,1:T(8,128)}, u32[]{:S(2)}) copy-start(s32[32,8]{0,1:T(8,128)} %param.19) | copy-start | bytes 3076
  10.4 53.0 %all-to-all-start = ((bf16[128,3,2,2048]{3,2,1,0:T(2,128)(2,1)}), bf16[128,3,2,2048]{3,2,1,0:T(2,128)(2,1)S(1)}, u32[]{:S(2)}, u32[]{:S(2)}) async-start(bf16[128,3,2,2048]{3,2,1,0:T(2,128)(2,1)} %copy.25), calls=%async_computation | async-start | bytes 6291456 | tf_op jit(solution)/shard_map/all_to_all | solution.py:300
  23.7 56.6 %collective-permute-start.3 = (f32[3,16,1,256]{3,2,1,0:T(1,128)}, f32[3,16,1,256]{3,2,1,0:T(1,128)}, u32[]{:S(2)}, u32[]{:S(2)}) collective-permute-start(f32[3,16,1,256]{3,2,1,0:T(1,128)} %get-tuple-element.38), channel_id=1, source_target_pairs={{1,0},{0,1},{3,2},{2,3},{5,4},{4,5},{7,6},{6,7},{9,8},{8,9},{11,10... | collective-permute-start | bytes 147464 | tf_op jit(solution)/shard_map/ppermute | solution.py:252
  25.2 55.1 %collective-permute-start.2 = (f32[3,16,1,256]{3,2,1,0:T(1,128)}, f32[3,16,1,256]{3,2,1,0:T(1,128)}, u32[]{:S(2)}, u32[]{:S(2)}) collective-permute-start(f32[3,16,1,256]{3,2,1,0:T(1,128)} %get-tuple-element.39), channel_id=1, source_target_pairs={{0,1},{1,0},{2,3},{3,2},{4,5},{5,4},{6,7},{7,6},{8,9},{9,8},{10,11... | collective-permute-start | bytes 147464 | tf_op jit(solution)/shard_map/ppermute | solution.py:251
  27.1 53.3 %collective-permute-start.1 = (f32[3,1,64,256]{3,2,1,0:T(8,128)}, f32[3,1,64,256]{3,2,1,0:T(8,128)}, u32[]{:S(2)}, u32[]{:S(2)}) collective-permute-start(f32[3,1,64,256]{3,2,1,0:T(8,128)} %get-tuple-element.40), channel_id=1, source_target_pairs={{2,0},{4,2},{6,4},{8,6},{10,8},{12,10},{14,12},{16,14},{18,16},{20... | collective-permute-start | bytes 589832 | tf_op jit(solution)/shard_map/ppermute | solution.py:252
  28.6 51.7 %collective-permute-start = (f32[3,1,64,256]{3,2,1,0:T(8,128)}, f32[3,1,64,256]{3,2,1,0:T(8,128)}, u32[]{:S(2)}, u32[]{:S(2)}) collective-permute-start(f32[3,1,64,256]{3,2,1,0:T(8,128)} %get-tuple-element.41), channel_id=1, source_target_pairs={{0,2},{2,4},{4,6},{6,8},{8,10},{10,12},{12,14},{14,16},{16,18},{18... | collective-permute-start | bytes 589832 | tf_op jit(solution)/shard_map/ppermute | solution.py:251
  31.1 41.4 %copy-start.12 = (f32[80]{0:T(128)}, f32[80]{0:T(128)S(1)}, u32[]{:S(2)}) copy-start(f32[80]{0:T(128)S(1)} %cos.4) | copy-start | bytes 964
  33.6 5.5 %copy-start.14 = (f32[3,80]{1,0:T(4,128)S(1)}, f32[3,80]{1,0:T(4,128)}, u32[]{:S(2)}) copy-start(f32[3,80]{1,0:T(4,128)} %param.23) | copy-start | bytes 2884
  39.2 33.3 %copy-start.15 = (s32[80]{0:T(128)S(1)}, s32[80]{0:T(128)}, u32[]{:S(2)}) copy-start(s32[80]{0:T(128)} %param.24) | copy-start | bytes 964
  39.2 33.3 %copy-start.10 = (f32[80]{0:T(128)S(1)}, f32[80]{0:T(128)}, u32[]{:S(2)}) copy-start(f32[80]{0:T(128)} %param.21) | copy-start | bytes 964
  65.1 47.7 %all-to-all-start.1 = ((bf16[128,3,2,2048]{3,2,1,0:T(2,128)(2,1)}), bf16[128,3,2,2048]{3,2,1,0:T(2,128)(2,1)}, u32[]{:S(2)}, u32[]{:S(2)}) async-start(bf16[128,3,2,2048]{3,2,1,0:T(2,128)(2,1)} %copy.29), calls=%async_computation.1 | async-start | bytes 6291456 | tf_op jit(solution)/shard_map/all_to_all | solution.py:300
  71.6 3.0 %copy-start.6 = (bf16[128,3,2,2048]{3,2,1,0:T(2,128)(2,1)S(1)}, bf16[128,3,2,2048]{3,2,1,0:T(2,128)(2,1)}, u32[]{:S(2)}) copy-start(bf16[128,3,2,2048]{3,2,1,0:T(2,128)(2,1)} %copy-done.5) | copy-start | bytes 9437188
  71.6 3.0 %copy-start.8 = (s32[128,2]{0,1:T(2,128)S(1)}, s32[128,2]{0,1:T(2,128)}, u32[]{:S(2)}) copy-start(s32[128,2]{0,1:T(2,128)} %copy-done.7) | copy-start | bytes 3076
  71.6 3.0 %copy-start.19 = (s32[128]{0:T(128)S(1)}, s32[128]{0:T(128)}, u32[]{:S(2)}) copy-start(s32[128]{0:T(128)} %param.18) | copy-start | bytes 1540
  76.1 4.2 %copy-start = (bf16[8,128,128]{2,1,0:T(8,128)(2,1)S(1)}, bf16[8,128,128]{2,1,0:T(8,128)(2,1)}, u32[]{:S(2)}) copy-start(bf16[8,128,128]{2,1,0:T(8,128)(2,1)} %param.20) | copy-start | bytes 786436
  103.6 16.8 %collective-permute-start.7 = (f32[3,16,1,256]{3,2,1,0:T(1,128)}, f32[3,16,1,256]{3,2,1,0:T(1,128)}, u32[]{:S(2)}, u32[]{:S(2)}) collective-permute-start(f32[3,16,1,256]{3,2,1,0:T(1,128)} %get-tuple-element.34), channel_id=1, source_target_pairs={{1,0},{0,1},{3,2},{2,3},{5,4},{4,5},{7,6},{6,7},{9,8},{8,9},{11,10... | collective-permute-start | bytes 147464 | tf_op jit(solution)/shard_map/ppermute | solution.py:252
  105.1 15.3 %collective-permute-start.6 = (f32[3,16,1,256]{3,2,1,0:T(1,128)}, f32[3,16,1,256]{3,2,1,0:T(1,128)}, u32[]{:S(2)}, u32[]{:S(2)}) collective-permute-start(f32[3,16,1,256]{3,2,1,0:T(1,128)} %get-tuple-element.35), channel_id=1, source_target_pairs={{0,1},{1,0},{2,3},{3,2},{4,5},{5,4},{6,7},{7,6},{8,9},{9,8},{10,11... | collective-permute-start | bytes 147464 | tf_op jit(solution)/shard_map/ppermute | solution.py:251
  106.9 13.5 %collective-permute-start.5 = (f32[3,1,64,256]{3,2,1,0:T(8,128)}, f32[3,1,64,256]{3,2,1,0:T(8,128)}, u32[]{:S(2)}, u32[]{:S(2)}) collective-permute-start(f32[3,1,64,256]{3,2,1,0:T(8,128)} %get-tuple-element.36), channel_id=1, source_target_pairs={{2,0},{4,2},{6,4},{8,6},{10,8},{12,10},{14,12},{16,14},{18,16},{20... | collective-permute-start | bytes 589832 | tf_op jit(solution)/shard_map/ppermute | solution.py:252
  108.7 11.7 %collective-permute-start.4 = (f32[3,1,64,256]{3,2,1,0:T(8,128)}, f32[3,1,64,256]{3,2,1,0:T(8,128)}, u32[]{:S(2)}, u32[]{:S(2)}) collective-permute-start(f32[3,1,64,256]{3,2,1,0:T(8,128)} %get-tuple-element.37), channel_id=1, source_target_pairs={{0,2},{2,4},{4,6},{6,8},{8,10},{10,12},{12,14},{14,16},{16,18},{18... | collective-permute-start | bytes 589832 | tf_op jit(solution)/shard_map/ppermute | solution.py:251
  121.7 23.1 %copy-start.11 = (f32[80]{0:T(128)S(1)}, f32[80]{0:T(128)}, u32[]{:S(2)}) copy-start(f32[80]{0:T(128)} %param.21) | copy-start | bytes 964
  121.8 23.1 %copy-start.13 = (f32[80]{0:T(128)S(1)}, f32[80]{0:T(128)}, u32[]{:S(2)}) copy-start(f32[80]{0:T(128)} %copy-done.12) | copy-start | bytes 964
  121.8 23.1 %copy-start.17 = (f32[80]{0:T(128)S(1)}, f32[80]{0:T(128)}, u32[]{:S(2)}) copy-start(f32[80]{0:T(128)} %param.22) | copy-start | bytes 964
  (6 other events, 5.5 us)

commit v5 on v4

--- a/solution.py
+++ b/solution.py
@@ -164,34 +164,49 @@
     row = lax.broadcasted_iota(jnp.int32, (width_y, height), 0)
     lane = lax.broadcasted_iota(jnp.int32, (width_y, height), 1)
 
-    def plane(x, carry):
+    def plane(x, west_of, east_of):
         u0 = u_ref[0, x].astype(jnp.float32)
         u1 = u_ref[1, x].astype(jnp.float32)
         u2 = u_ref[2, x].astype(jnp.float32)
-        viscous = EDDY_COEF * jnp.sqrt(1.0 + (u0 * u0 + u1 * u1 + u2 * u2))
-        west_index = jnp.maximum(x - 1, 0)
-        east_index = jnp.minimum(x + 1, width_x - 1)
+        viscous = (TIME_STEP * EDDY_COEF) * jnp.sqrt(1.0 + (u0 * u0 + u1 * u1 + u2 * u2))
+        diffuse = TIME_STEP * BASE_VISC
+        carry_x, carry_y, carry_z = (0.5 * TIME_STEP) * u0, (0.5 * TIME_STEP) * u1, (0.5 * TIME_STEP) * u2
+        east_weight, west_weight = diffuse + carry_x, diffuse - carry_x
+        north_weight, south_weight = diffuse + carry_y, diffuse - carry_y
+        upper_weight = jnp.where(lane == height - 1, 0.0, diffuse + carry_z)
+        lower_weight = jnp.where(lane == 0, 0.0, diffuse - carry_z)
+        centre_weight = 1.0 - 6.0 * diffuse
+        drag = TIME_STEP * drag_ref[x] * u0
         scale = fringe_ref[x]
         for c in range(components):
             center = a_ref[c, x]
-            west = jnp.where(x == 0, w_ref[c, 0], a_ref[c, west_index])
-            east = jnp.where(x == width_x - 1, e_ref[c, 0], a_ref[c, east_index])
             north = jnp.where(row == width_y - 1, jnp.broadcast_to(n_ref[c, x], (width_y, height)), pltpu.roll(center, width_y - 1, 0))
             south = jnp.where(row == 0, jnp.broadcast_to(s_ref[c, x], (width_y, height)), pltpu.roll(center, 1, 0))
-            upper = jnp.where(lane == height - 1, 0.0, pltpu.roll(center, height - 1, 1))
-            lower = jnp.where(lane == 0, 0.0, pltpu.roll(center, 1, 1))
-            laplace = east + west + north + south + upper + lower - 6.0 * center
-            advect = 0.5 * (u0 * (east - west) + u1 * (north - south) + u2 * (upper - lower))
             product = jnp.concatenate(
                 [prod[2 * x + zb, c * width_y : (c + 1) * width_y, :] for zb in range(NZB)], axis=1
             )
-            update = center + TIME_STEP * (advect + BASE_VISC * laplace + viscous * product)
+            update = (
+                centre_weight * center
+                + east_weight * east_of(c)
+                + west_weight * west_of(c)
+                + north_weight * north
+                + south_weight * south
+                + upper_weight * pltpu.roll(center, height - 1, 1)
+                + lower_weight * pltpu.roll(center, 1, 1)
+                + viscous * product
+            )
             if c == 0:
-                update = update - TIME_STEP * drag_ref[x] * u0 * center
+                update = update - drag * center
             out_ref[c, x] = update * scale
+
+    plane(0, lambda c: w_ref[c, 0], lambda c: a_ref[c, 1])
+
+    def inner_plane(x, carry):
+        plane(x, lambda c: a_ref[c, x - 1], lambda c: a_ref[c, x + 1])
         return carry
 
-    lax.fori_loop(0, width_x, plane, 0)
+    lax.fori_loop(1, width_x - 1, inner_plane, 0)
+    plane(width_x - 1, lambda c: a_ref[c, width_x - 2], lambda c: e_ref[c, 0])
     if exchange:
         second = pltpu.make_async_remote_copy(
             src_ref=far.at[pl.ds(0, groups - 1)], dst_ref=far.at[pl.ds(0, groups - 1)],

time: 152 us -> 151 us (level)
  no operation moved by 1% of the time
where the time goes in v5:
time: 151 us; the launch traced here: 149 us
  Pallas kernels  41.8 us (28%)
  local copies, waits for them, and re-layouts  33.8 us (22%)
  starting transfers between devices  29.1 us (19%)
  waiting for transfers between devices  26.7 us (18%)
  matrix products  10.7 us (7%)
  other arithmetic  5.49 us (4%)
    pallas_call x2, Pallas kernels, advance(): pl.pallas_call(functools.partial(advance_kernel, count_y, group, exchange...  41.8 us
    all_to_all x2, waiting for transfers between devices, shards(): lax.all_to_all(packed, ('gx', 'gy'), split_axis=0, concat_axis=0, tiled=T...  26.7 us
    all_to_all x2, starting transfers between devices, shards(): lax.all_to_all(packed, ('gx', 'gy'), split_axis=0, concat_axis=0, tiled=T...  18 us
    convert_element_type x2, local copies, waits for them, and re-layouts, shards(): packed = jnp.einsum('drs,scb->dcrb', pack_table, stored, preferred_elemen...  9.77 us
    unnamed x42, local copies, waits for them, and re-layouts  8.33 us
    slice x4, local copies, waits for them, and re-layouts, halo(): high = lax.ppermute(lax.slice_in_dim(block, 0, 1, axis=dim), axis, backward)  7.24 us
    ppermute x4, starting transfers between devices, halo(): high = lax.ppermute(lax.slice_in_dim(block, 0, 1, axis=dim), axis, backward)  6.36 us
    reshape x2, local copies, waits for them, and re-layouts, shards(): forward = forward.reshape(components, width_x, width_y, height)  5.16 us
  transfers between devices with their start and end apart: 10, of which 2 were waited for; matrix products, arithmetic and copies ran while one was open for 21% of the time, Pallas kernels for 13%

profile of v5, /device:TPU:1, one launch (start us, length us, event | category | flops | bytes accessed | tf_op | source)
XLA Modules:
  0.0 148.5 jit_solution(12264194676037421257)
XLA Ops:
  3.1 2.4 %fusion.4 = bf16[128,3,2,2048]{3,0,1,2:T(8,128)(2,1)S(1)} fusion(bf16[2,128,3,2048]{3,1,2,0:T(8,128)(2,1)} %param.16, s32[128]{0:T(128)S(1)} %add_add_fusion, s32[128,2]{0,1:T(2,128)S(1)} %multiply_add_fusion), kind=kOutput, calls=%fused_computation.8 | convolution fusion | flops 404258816 | bytes 4720128 | tf_op jit(solution)/shard_map/drs,scb->dcrb/dot_general | solution.py:312
  5.5 4.9 %copy.25 = bf16[128,3,2,2048]{3,2,1,0:T(2,128)(2,1)} copy(bf16[128,3,2,2048]{3,0,1,2:T(8,128)(2,1)S(1)} %fusion.4) | data formatting | bytes 6291456 | tf_op jit(solution)/shard_map/convert_element_type | solution.py:314
  10.4 11.5 %all-to-all-start = ((bf16[128,3,2,2048]{3,2,1,0:T(2,128)(2,1)}), bf16[128,3,2,2048]{3,2,1,0:T(2,128)(2,1)S(1)}, u32[]{:S(2)}, u32[]{:S(2)}) async-start(bf16[128,3,2,2048]{3,2,1,0:T(2,128)(2,1)} %copy.25), calls=%async_computation | async-start | bytes 6291456 | tf_op jit(solution)/shard_map/all_to_all | solution.py:315
  21.9 1.8 %fusion.53 = (f32[3,16,1,256]{3,2,1,0:T(1,128)}, f32[3,16,1,256]{3,2,1,0:T(1,128)}) fusion(f32[3,16,64,256]{3,2,1,0:T(8,128)} %refs_2_.1), kind=kLoop, calls=%fused_computation.72 | loop fusion | bytes 196608 | tf_op jit(solution)/shard_map/slice | solution.py:267
  25.3 1.8 %fusion.54 = (f32[3,1,64,256]{3,2,1,0:T(8,128)}, f32[3,1,64,256]{3,2,1,0:T(8,128)}) fusion(f32[3,16,64,256]{3,2,1,0:T(8,128)} %refs_2_.1), kind=kLoop, calls=%fused_computation.73 | loop fusion | bytes 786432 | tf_op jit(solution)/shard_map/slice | solution.py:267
  28.6 2.5 %collective-permute-start = (f32[3,1,64,256]{3,2,1,0:T(8,128)}, f32[3,1,64,256]{3,2,1,0:T(8,128)}, u32[]{:S(2)}, u32[]{:S(2)}) collective-permute-start(f32[3,1,64,256]{3,2,1,0:T(8,128)} %get-tuple-element.41), channel_id=1, source_target_pairs={{0,2},{2,4},{4,6},{6,8},{8,10},{10,12},{12,14},{14,16},{16,18},{18... | collective-permute-start | bytes 589832 | tf_op jit(solution)/shard_map/ppermute | solution.py:266
  31.2 2.4 %fusion.5 = bf16[128,3,2,2048]{3,0,1,2:T(8,128)(2,1)S(1)} fusion(bf16[2,128,3,2048]{3,1,2,0:T(8,128)(2,1)} %param.16, s32[128]{0:T(128)S(1)} %add_add_fusion, s32[128,2]{0,1:T(2,128)S(1)} %multiply_add_fusion), kind=kOutput, calls=%fused_computation.9 | convolution fusion | flops 404258816 | bytes 4720128 | tf_op jit(solution)/shard_map/drs,scb->dcrb/dot_general | solution.py:312
  33.7 4.9 %copy.29 = bf16[128,3,2,2048]{3,2,1,0:T(2,128)(2,1)} copy(bf16[128,3,2,2048]{3,0,1,2:T(8,128)(2,1)S(1)} %fusion.5) | data formatting | bytes 6291456 | tf_op jit(solution)/shard_map/convert_element_type | solution.py:314
  39.2 24.2 %all-to-all-done = bf16[128,3,2,2048]{3,2,1,0:T(2,128)(2,1)S(1)} async-done(((bf16[128,3,2,2048]{3,2,1,0:T(2,128)(2,1)}), bf16[128,3,2,2048]{3,2,1,0:T(2,128)(2,1)S(1)}, u32[]{:S(2)}, u32[]{:S(2)}) %all-to-all-start) | async-done | bytes 3145760 | tf_op jit(solution)/shard_map/all_to_all | solution.py:315
  63.4 1.7 %copy-done.5 = bf16[128,3,2,2048]{3,2,1,0:T(2,128)(2,1)} copy-done((bf16[128,3,2,2048]{3,2,1,0:T(2,128)(2,1)}, bf16[128,3,2,2048]{3,2,1,0:T(2,128)(2,1)S(1)}, u32[]{:S(2)}) %copy-start.5) | copy-done | bytes 3145752
  65.1 6.5 %all-to-all-start.1 = ((bf16[128,3,2,2048]{3,2,1,0:T(2,128)(2,1)}), bf16[128,3,2,2048]{3,2,1,0:T(2,128)(2,1)}, u32[]{:S(2)}, u32[]{:S(2)}) async-start(bf16[128,3,2,2048]{3,2,1,0:T(2,128)(2,1)} %copy.29), calls=%async_computation.1 | async-start | bytes 6291456 | tf_op jit(solution)/shard_map/all_to_all | solution.py:315
  76.1 1.6 %copy.27 = bf16[3,128,2048]{2,1,0:T(8,128)(2,1)} copy(bf16[3,128,2048]{1,2,0:T(8,128)(2,1)S(1)} %fusion.10) | data formatting | bytes 3145728 | tf_op jit(solution)/shard_map/convert_element_type | solution.py:318
  77.7 2.6 %reshape.195.refs_7_ = bf16[3,16,64,256]{3,2,1,0:T(8,128)(2,1)S(1)} reshape(bf16[3,128,2048]{2,1,0:T(8,128)(2,1)} %copy.27) | data formatting | bytes 3145728 | tf_op jit(solution)/shard_map/reshape | solution.py:319
  81.0 19.6 %shard_map.122 = (f32[3,16,64,256]{3,2,1,0:T(8,128)}, f32[8,128]{1,0:T(8,128)S(1)}) custom-call(s32[32,8]{1,0:T(8,128)S(1)} %copy.32.refs_0_, f32[16]{0:T(128)S(1)} %copy-done.3, f32[3,16,64,256]{3,2,1,0:T(8,128)} %refs_2_.1, f32[3,1,64,256]{3,2,1,0:T(8,128)} %collective-permute-done.refs_3_, f32[3,1,64,256]{3,2,1,0:T(8,128)} %collective-permute-done.1.refs_4_, ...), custom_call_target="tpu_custom_call" | custom-call | tf_op jit(solution)/shard_map/pallas_call | solution.py:243
  101.2 1.8 %fusion.51 = (f32[3,16,1,256]{3,2,1,0:T(1,128)}, f32[3,16,1,256]{3,2,1,0:T(1,128)}) fusion(f32[3,16,64,256]{3,2,1,0:T(8,128)} %get-tuple-element.30.refs_2_), kind=kLoop, calls=%fused_computation.70 | loop fusion | bytes 196608 | tf_op jit(solution)/shard_map/slice | solution.py:267
  104.5 1.8 %fusion.52 = (f32[3,1,64,256]{3,2,1,0:T(8,128)}, f32[3,1,64,256]{3,2,1,0:T(8,128)}) fusion(f32[3,16,64,256]{3,2,1,0:T(8,128)} %get-tuple-element.30.refs_2_), kind=kLoop, calls=%fused_computation.71 | loop fusion | bytes 786432 | tf_op jit(solution)/shard_map/slice | solution.py:267
  106.3 1.8 %collective-permute-start.5 = (f32[3,1,64,256]{3,2,1,0:T(8,128)}, f32[3,1,64,256]{3,2,1,0:T(8,128)}, u32[]{:S(2)}, u32[]{:S(2)}) collective-permute-start(f32[3,1,64,256]{3,2,1,0:T(8,128)} %get-tuple-element.36), channel_id=1, source_target_pairs={{2,0},{4,2},{6,4},{8,6},{10,8},{12,10},{14,12},{16,14},{18,16},{20... | collective-permute-start | bytes 589832 | tf_op jit(solution)/shard_map/ppermute | solution.py:267
  108.1 2.2 %collective-permute-start.4 = (f32[3,1,64,256]{3,2,1,0:T(8,128)}, f32[3,1,64,256]{3,2,1,0:T(8,128)}, u32[]{:S(2)}, u32[]{:S(2)}) collective-permute-start(f32[3,1,64,256]{3,2,1,0:T(8,128)} %get-tuple-element.37), channel_id=1, source_target_pairs={{0,2},{2,4},{4,6},{6,8},{8,10},{10,12},{12,14},{14,16},{16,18},{18... | collective-permute-start | bytes 589832 | tf_op jit(solution)/shard_map/ppermute | solution.py:266
  110.4 2.4 %all-to-all-done.1 = bf16[128,3,2,2048]{3,2,1,0:T(2,128)(2,1)} async-done(((bf16[128,3,2,2048]{3,2,1,0:T(2,128)(2,1)}), bf16[128,3,2,2048]{3,2,1,0:T(2,128)(2,1)}, u32[]{:S(2)}, u32[]{:S(2)}) %all-to-all-start.1) | async-done | bytes 3145760 | tf_op jit(solution)/shard_map/all_to_all | solution.py:315
  112.8 3.3 %fusion.13 = bf16[3,128,2048]{1,2,0:T(8,128)(2,1)S(1)} fusion(bf16[128,3,2,2048]{3,2,1,0:T(2,128)(2,1)} %all-to-all-done.1, s32[128,2]{0,1:T(2,128)} %copy-done.7, s32[128]{0:T(128)} %param.18), kind=kOutput, calls=%fused_computation.11 | convolution fusion | flops 403472384 | bytes 4720128 | tf_op jit(solution)/shard_map/jsr,scrb->cjb/dot_general | solution.py:316
  116.2 1.6 %copy.31 = bf16[3,128,2048]{2,1,0:T(8,128)(2,1)} copy(bf16[3,128,2048]{1,2,0:T(8,128)(2,1)S(1)} %fusion.13) | data formatting | bytes 3145728 | tf_op jit(solution)/shard_map/convert_element_type | solution.py:318
  117.8 2.6 %reshape.198.refs_7_ = bf16[3,16,64,256]{3,2,1,0:T(8,128)(2,1)S(1)} reshape(bf16[3,128,2048]{2,1,0:T(8,128)(2,1)} %copy.31) | data formatting | bytes 3145728 | tf_op jit(solution)/shard_map/reshape | solution.py:319
  121.8 22.2 %shard_map.123 = (f32[3,16,64,256]{3,2,1,0:T(8,128)}, f32[8,128]{1,0:T(8,128)S(1)}) custom-call(s32[32,8]{1,0:T(8,128)S(1)} %copy.32.refs_0_, f32[16]{0:T(128)S(1)} %copy-done.4, f32[3,16,64,256]{3,2,1,0:T(8,128)} %get-tuple-element.30.refs_2_, f32[3,1,64,256]{3,2,1,0:T(8,128)} %collective-permute-done.4.refs_3_, ...), custom_call_target="tpu_custom_call" | custom-call | tf_op jit(solution)/shard_map/pallas_call | solution.py:243
  144.6 3.9 %copy.49 = f32[3,16,64,256]{3,2,1,0:T(8,128)} copy(f32[3,16,64,256]{3,2,1,0:T(8,128)} %get-tuple-element.51) | data formatting | bytes 6291456
  (78 shorter events, 15.5 us)
Async XLA Ops:
  0.6 30.6 %copy-start.7 = (s32[128,2]{0,1:T(2,128)}, s32[128,2]{0,1:T(2,128)S(1)}, u32[]{:S(2)}) copy-start(s32[128,2]{0,1:T(2,128)S(1)} %multiply_add_fusion) | copy-start | bytes 3076
  10.4 20.7 %copy-start.16 = (f32[80]{0:T(128)S(1)}, f32[80]{0:T(128)}, u32[]{:S(2)}) copy-start(f32[80]{0:T(128)} %param.22) | copy-start | bytes 964
  10.4 20.7 %copy-start.9 = (s32[32,8]{0,1:T(8,128)S(1)}, s32[32,8]{0,1:T(8,128)}, u32[]{:S(2)}) copy-start(s32[32,8]{0,1:T(8,128)} %param.19) | copy-start | bytes 3076
  10.4 53.0 %all-to-all-start = ((bf16[128,3,2,2048]{3,2,1,0:T(2,128)(2,1)}), bf16[128,3,2,2048]{3,2,1,0:T(2,128)(2,1)S(1)}, u32[]{:S(2)}, u32[]{:S(2)}) async-start(bf16[128,3,2,2048]{3,2,1,0:T(2,128)(2,1)} %copy.25), calls=%async_computation | async-start | bytes 6291456 | tf_op jit(solution)/shard_map/all_to_all | solution.py:315
  23.7 56.6 %collective-permute-start.3 = (f32[3,16,1,256]{3,2,1,0:T(1,128)}, f32[3,16,1,256]{3,2,1,0:T(1,128)}, u32[]{:S(2)}, u32[]{:S(2)}) collective-permute-start(f32[3,16,1,256]{3,2,1,0:T(1,128)} %get-tuple-element.38), channel_id=1, source_target_pairs={{1,0},{0,1},{3,2},{2,3},{5,4},{4,5},{7,6},{6,7},{9,8},{8,9},{11,10... | collective-permute-start | bytes 147464 | tf_op jit(solution)/shard_map/ppermute | solution.py:267
  25.2 55.1 %collective-permute-start.2 = (f32[3,16,1,256]{3,2,1,0:T(1,128)}, f32[3,16,1,256]{3,2,1,0:T(1,128)}, u32[]{:S(2)}, u32[]{:S(2)}) collective-permute-start(f32[3,16,1,256]{3,2,1,0:T(1,128)} %get-tuple-element.39), channel_id=1, source_target_pairs={{0,1},{1,0},{2,3},{3,2},{4,5},{5,4},{6,7},{7,6},{8,9},{9,8},{10,11... | collective-permute-start | bytes 147464 | tf_op jit(solution)/shard_map/ppermute | solution.py:266
  27.1 53.3 %collective-permute-start.1 = (f32[3,1,64,256]{3,2,1,0:T(8,128)}, f32[3,1,64,256]{3,2,1,0:T(8,128)}, u32[]{:S(2)}, u32[]{:S(2)}) collective-permute-start(f32[3,1,64,256]{3,2,1,0:T(8,128)} %get-tuple-element.40), channel_id=1, source_target_pairs={{2,0},{4,2},{6,4},{8,6},{10,8},{12,10},{14,12},{16,14},{18,16},{20... | collective-permute-start | bytes 589832 | tf_op jit(solution)/shard_map/ppermute | solution.py:267
  28.6 51.7 %collective-permute-start = (f32[3,1,64,256]{3,2,1,0:T(8,128)}, f32[3,1,64,256]{3,2,1,0:T(8,128)}, u32[]{:S(2)}, u32[]{:S(2)}) collective-permute-start(f32[3,1,64,256]{3,2,1,0:T(8,128)} %get-tuple-element.41), channel_id=1, source_target_pairs={{0,2},{2,4},{4,6},{6,8},{8,10},{10,12},{12,14},{14,16},{16,18},{18... | collective-permute-start | bytes 589832 | tf_op jit(solution)/shard_map/ppermute | solution.py:266
  31.1 41.4 %copy-start.12 = (f32[80]{0:T(128)}, f32[80]{0:T(128)S(1)}, u32[]{:S(2)}) copy-start(f32[80]{0:T(128)S(1)} %cos.4) | copy-start | bytes 964
  33.6 5.5 %copy-start.14 = (f32[3,80]{1,0:T(4,128)S(1)}, f32[3,80]{1,0:T(4,128)}, u32[]{:S(2)}) copy-start(f32[3,80]{1,0:T(4,128)} %param.23) | copy-start | bytes 2884
  39.2 33.3 %copy-start.15 = (s32[80]{0:T(128)S(1)}, s32[80]{0:T(128)}, u32[]{:S(2)}) copy-start(s32[80]{0:T(128)} %param.24) | copy-start | bytes 964
  39.2 33.3 %copy-start.10 = (f32[80]{0:T(128)S(1)}, f32[80]{0:T(128)}, u32[]{:S(2)}) copy-start(f32[80]{0:T(128)} %param.21) | copy-start | bytes 964
  65.1 47.7 %all-to-all-start.1 = ((bf16[128,3,2,2048]{3,2,1,0:T(2,128)(2,1)}), bf16[128,3,2,2048]{3,2,1,0:T(2,128)(2,1)}, u32[]{:S(2)}, u32[]{:S(2)}) async-start(bf16[128,3,2,2048]{3,2,1,0:T(2,128)(2,1)} %copy.29), calls=%async_computation.1 | async-start | bytes 6291456 | tf_op jit(solution)/shard_map/all_to_all | solution.py:315
  71.6 3.0 %copy-start.6 = (bf16[128,3,2,2048]{3,2,1,0:T(2,128)(2,1)S(1)}, bf16[128,3,2,2048]{3,2,1,0:T(2,128)(2,1)}, u32[]{:S(2)}) copy-start(bf16[128,3,2,2048]{3,2,1,0:T(2,128)(2,1)} %copy-done.5) | copy-start | bytes 9437188
  71.6 3.0 %copy-start.8 = (s32[128,2]{0,1:T(2,128)S(1)}, s32[128,2]{0,1:T(2,128)}, u32[]{:S(2)}) copy-start(s32[128,2]{0,1:T(2,128)} %copy-done.7) | copy-start | bytes 3076
  71.6 3.0 %copy-start.19 = (s32[128]{0:T(128)S(1)}, s32[128]{0:T(128)}, u32[]{:S(2)}) copy-start(s32[128]{0:T(128)} %param.18) | copy-start | bytes 1540
  76.1 4.2 %copy-start = (bf16[8,128,128]{2,1,0:T(8,128)(2,1)S(1)}, bf16[8,128,128]{2,1,0:T(8,128)(2,1)}, u32[]{:S(2)}) copy-start(bf16[8,128,128]{2,1,0:T(8,128)(2,1)} %param.20) | copy-start | bytes 786436
  103.0 17.3 %collective-permute-start.7 = (f32[3,16,1,256]{3,2,1,0:T(1,128)}, f32[3,16,1,256]{3,2,1,0:T(1,128)}, u32[]{:S(2)}, u32[]{:S(2)}) collective-permute-start(f32[3,16,1,256]{3,2,1,0:T(1,128)} %get-tuple-element.34), channel_id=1, source_target_pairs={{1,0},{0,1},{3,2},{2,3},{5,4},{4,5},{7,6},{6,7},{9,8},{8,9},{11,10... | collective-permute-start | bytes 147464 | tf_op jit(solution)/shard_map/ppermute | solution.py:267
  104.5 15.8 %collective-permute-start.6 = (f32[3,16,1,256]{3,2,1,0:T(1,128)}, f32[3,16,1,256]{3,2,1,0:T(1,128)}, u32[]{:S(2)}, u32[]{:S(2)}) collective-permute-start(f32[3,16,1,256]{3,2,1,0:T(1,128)} %get-tuple-element.35), channel_id=1, source_target_pairs={{0,1},{1,0},{2,3},{3,2},{4,5},{5,4},{6,7},{7,6},{8,9},{9,8},{10,11... | collective-permute-start | bytes 147464 | tf_op jit(solution)/shard_map/ppermute | solution.py:266
  106.3 14.0 %collective-permute-start.5 = (f32[3,1,64,256]{3,2,1,0:T(8,128)}, f32[3,1,64,256]{3,2,1,0:T(8,128)}, u32[]{:S(2)}, u32[]{:S(2)}) collective-permute-start(f32[3,1,64,256]{3,2,1,0:T(8,128)} %get-tuple-element.36), channel_id=1, source_target_pairs={{2,0},{4,2},{6,4},{8,6},{10,8},{12,10},{14,12},{16,14},{18,16},{20... | collective-permute-start | bytes 589832 | tf_op jit(solution)/shard_map/ppermute | solution.py:267
  108.1 12.2 %collective-permute-start.4 = (f32[3,1,64,256]{3,2,1,0:T(8,128)}, f32[3,1,64,256]{3,2,1,0:T(8,128)}, u32[]{:S(2)}, u32[]{:S(2)}) collective-permute-start(f32[3,1,64,256]{3,2,1,0:T(8,128)} %get-tuple-element.37), channel_id=1, source_target_pairs={{0,2},{2,4},{4,6},{6,8},{8,10},{10,12},{12,14},{14,16},{16,18},{18... | collective-permute-start | bytes 589832 | tf_op jit(solution)/shard_map/ppermute | solution.py:266
  121.7 22.2 %copy-start.11 = (f32[80]{0:T(128)S(1)}, f32[80]{0:T(128)}, u32[]{:S(2)}) copy-start(f32[80]{0:T(128)} %param.21) | copy-start | bytes 964
  121.8 22.2 %copy-start.13 = (f32[80]{0:T(128)S(1)}, f32[80]{0:T(128)}, u32[]{:S(2)}) copy-start(f32[80]{0:T(128)} %copy-done.12) | copy-start | bytes 964
  121.8 22.2 %copy-start.17 = (f32[80]{0:T(128)S(1)}, f32[80]{0:T(128)}, u32[]{:S(2)}) copy-start(f32[80]{0:T(128)} %param.22) | copy-start | bytes 964
  (6 other events, 5.5 us)

commit v6 on v5

--- a/solution.py
+++ b/solution.py
@@ -97,8 +97,12 @@
     def turbine_plane(x, acc):
         velocity = u_ref[0, x].astype(jnp.float32)
         density = velocity * velocity * a_ref[0, x]
-        projected = jnp.dot(
-            density, azh_ref[...], precision=lax.Precision.HIGHEST, preferred_element_type=jnp.float32
+        high = density.astype(jnp.bfloat16)
+        low = (density - high.astype(jnp.float32)).astype(jnp.bfloat16)
+        projected = (
+            jnp.dot(high, azh_ref[0], preferred_element_type=jnp.float32)
+            + jnp.dot(high, azh_ref[1], preferred_element_type=jnp.float32)
+            + jnp.dot(low, azh_ref[0], preferred_element_type=jnp.float32)
         )
         return acc + pk_ref[x] * projected
 
@@ -256,7 +260,9 @@
     weights = (plan_kernel * owned_mask[:, None]).T.reshape(width_x, width_y, count)
     weights = jnp.zeros((width_x, width_y, lanes), jnp.float32).at[:, :, :count].set(weights)
     column = jnp.zeros((along_z.shape[1], lanes), jnp.float32).at[:, :count].set(along_z.T)
-    return weights, column
+    high = lax.reduce_precision(column, exponent_bits=8, mantissa_bits=7)
+    low = column - high
+    return weights, jnp.stack([high, low]).astype(jnp.bfloat16)
 
 
 def halo(block, axis, dim):

time: 151 us -> 149 us (0.987)
  local copies, waits for them, and re-layouts: 33.8 us -> 32 us
    unnamed x42, local copies, waits for them, and re-layouts: 8.33 us -> 6.54 us
where the time goes in v6:
time: 149 us; the launch traced here: 146 us
  Pallas kernels  40.5 us (27%)
  local copies, waits for them, and re-layouts  32 us (21%)
  starting transfers between devices  29.1 us (20%)
  waiting for transfers between devices  27.6 us (19%)
  matrix products  10.7 us (7%)
  other arithmetic  5.35 us (4%)
    pallas_call x2, Pallas kernels, advance(): pl.pallas_call(functools.partial(advance_kernel, count_y, group, exchange...  40.5 us
    all_to_all x2, waiting for transfers between devices, shards(): lax.all_to_all(packed, ('gx', 'gy'), split_axis=0, concat_axis=0, tiled=T...  27.6 us
    all_to_all x2, starting transfers between devices, shards(): lax.all_to_all(packed, ('gx', 'gy'), split_axis=0, concat_axis=0, tiled=T...  18 us
    convert_element_type x2, local copies, waits for them, and re-layouts, shards(): packed = jnp.einsum('drs,scb->dcrb', pack_table, stored, preferred_elemen...  9.81 us
    slice x4, local copies, waits for them, and re-layouts, halo(): high = lax.ppermute(lax.slice_in_dim(block, 0, 1, axis=dim), axis, backward)  7.26 us
    unnamed x42, local copies, waits for them, and re-layouts  6.54 us
    ppermute x4, starting transfers between devices, halo(): high = lax.ppermute(lax.slice_in_dim(block, 0, 1, axis=dim), axis, backward)  6.36 us
    reshape x2, local copies, waits for them, and re-layouts, shards(): forward = forward.reshape(components, width_x, width_y, height)  5.16 us
  transfers between devices with their start and end apart: 10, of which 2 were waited for; matrix products, arithmetic and copies ran while one was open for 21% of the time, Pallas kernels for 13%

profile of v6, /device:TPU:1, one launch (start us, length us, event | category | flops | bytes accessed | tf_op | source)
XLA Modules:
  0.0 146.4 jit_solution(3955895622260959219)
XLA Ops:
  3.1 2.4 %fusion.4 = bf16[128,3,2,2048]{3,0,1,2:T(8,128)(2,1)S(1)} fusion(bf16[2,128,3,2048]{3,1,2,0:T(8,128)(2,1)} %param.16, s32[128]{0:T(128)S(1)} %add_add_fusion, s32[128,2]{0,1:T(2,128)S(1)} %multiply_add_fusion), kind=kOutput, calls=%fused_computation.8 | convolution fusion | flops 404258816 | bytes 4720128 | tf_op jit(solution)/shard_map/drs,scb->dcrb/dot_general | solution.py:318
  5.5 4.9 %copy.25 = bf16[128,3,2,2048]{3,2,1,0:T(2,128)(2,1)} copy(bf16[128,3,2,2048]{3,0,1,2:T(8,128)(2,1)S(1)} %fusion.4) | data formatting | bytes 6291456 | tf_op jit(solution)/shard_map/convert_element_type | solution.py:320
  10.4 11.5 %all-to-all-start = ((bf16[128,3,2,2048]{3,2,1,0:T(2,128)(2,1)}), bf16[128,3,2,2048]{3,2,1,0:T(2,128)(2,1)S(1)}, u32[]{:S(2)}, u32[]{:S(2)}) async-start(bf16[128,3,2,2048]{3,2,1,0:T(2,128)(2,1)} %copy.25), calls=%async_computation | async-start | bytes 6291456 | tf_op jit(solution)/shard_map/all_to_all | solution.py:321
  21.9 1.8 %fusion.56 = (f32[3,16,1,256]{3,2,1,0:T(1,128)}, f32[3,16,1,256]{3,2,1,0:T(1,128)}) fusion(f32[3,16,64,256]{3,2,1,0:T(8,128)} %refs_2_.1), kind=kLoop, calls=%fused_computation.78 | loop fusion | bytes 196608 | tf_op jit(solution)/shard_map/slice | solution.py:273
  25.3 1.8 %fusion.57 = (f32[3,1,64,256]{3,2,1,0:T(8,128)}, f32[3,1,64,256]{3,2,1,0:T(8,128)}) fusion(f32[3,16,64,256]{3,2,1,0:T(8,128)} %refs_2_.1), kind=kLoop, calls=%fused_computation.79 | loop fusion | bytes 786432 | tf_op jit(solution)/shard_map/slice | solution.py:273
  27.1 1.6 %collective-permute-start.1 = (f32[3,1,64,256]{3,2,1,0:T(8,128)}, f32[3,1,64,256]{3,2,1,0:T(8,128)}, u32[]{:S(2)}, u32[]{:S(2)}) collective-permute-start(f32[3,1,64,256]{3,2,1,0:T(8,128)} %get-tuple-element.40), channel_id=1, source_target_pairs={{2,0},{4,2},{6,4},{8,6},{10,8},{12,10},{14,12},{16,14},{18,16},{20... | collective-permute-start | bytes 589832 | tf_op jit(solution)/shard_map/ppermute | solution.py:273
  28.6 2.5 %collective-permute-start = (f32[3,1,64,256]{3,2,1,0:T(8,128)}, f32[3,1,64,256]{3,2,1,0:T(8,128)}, u32[]{:S(2)}, u32[]{:S(2)}) collective-permute-start(f32[3,1,64,256]{3,2,1,0:T(8,128)} %get-tuple-element.41), channel_id=1, source_target_pairs={{0,2},{2,4},{4,6},{6,8},{8,10},{10,12},{12,14},{14,16},{16,18},{18... | collective-permute-start | bytes 589832 | tf_op jit(solution)/shard_map/ppermute | solution.py:272
  31.2 2.4 %fusion.5 = bf16[128,3,2,2048]{3,0,1,2:T(8,128)(2,1)S(1)} fusion(bf16[2,128,3,2048]{3,1,2,0:T(8,128)(2,1)} %param.16, s32[128]{0:T(128)S(1)} %add_add_fusion, s32[128,2]{0,1:T(2,128)S(1)} %multiply_add_fusion), kind=kOutput, calls=%fused_computation.9 | convolution fusion | flops 404258816 | bytes 4720128 | tf_op jit(solution)/shard_map/drs,scb->dcrb/dot_general | solution.py:318
  33.7 4.9 %copy.29 = bf16[128,3,2,2048]{3,2,1,0:T(2,128)(2,1)} copy(bf16[128,3,2,2048]{3,0,1,2:T(8,128)(2,1)S(1)} %fusion.5) | data formatting | bytes 6291456 | tf_op jit(solution)/shard_map/convert_element_type | solution.py:320
  38.6 24.8 %all-to-all-done = bf16[128,3,2,2048]{3,2,1,0:T(2,128)(2,1)S(1)} async-done(((bf16[128,3,2,2048]{3,2,1,0:T(2,128)(2,1)}), bf16[128,3,2,2048]{3,2,1,0:T(2,128)(2,1)S(1)}, u32[]{:S(2)}, u32[]{:S(2)}) %all-to-all-start) | async-done | bytes 3145760 | tf_op jit(solution)/shard_map/all_to_all | solution.py:321
  63.4 6.5 %all-to-all-start.1 = ((bf16[128,3,2,2048]{3,2,1,0:T(2,128)(2,1)}), bf16[128,3,2,2048]{3,2,1,0:T(2,128)(2,1)}, u32[]{:S(2)}, u32[]{:S(2)}) async-start(bf16[128,3,2,2048]{3,2,1,0:T(2,128)(2,1)} %copy.29), calls=%async_computation.1 | async-start | bytes 6291456 | tf_op jit(solution)/shard_map/all_to_all | solution.py:321
  74.9 1.6 %copy.27 = bf16[3,128,2048]{2,1,0:T(8,128)(2,1)} copy(bf16[3,128,2048]{1,2,0:T(8,128)(2,1)S(1)} %fusion.10) | data formatting | bytes 3145728 | tf_op jit(solution)/shard_map/convert_element_type | solution.py:324
  76.5 2.6 %reshape.195.refs_7_ = bf16[3,16,64,256]{3,2,1,0:T(8,128)(2,1)S(1)} reshape(bf16[3,128,2048]{2,1,0:T(8,128)(2,1)} %copy.27) | data formatting | bytes 3145728 | tf_op jit(solution)/shard_map/reshape | solution.py:325
  79.8 18.8 %shard_map.122 = (f32[3,16,64,256]{3,2,1,0:T(8,128)}, f32[8,128]{1,0:T(8,128)S(1)}) custom-call(s32[32,8]{1,0:T(8,128)S(1)} %copy.32.refs_0_, f32[16]{0:T(128)S(1)} %copy-done.3, f32[3,16,64,256]{3,2,1,0:T(8,128)} %refs_2_.1, f32[3,1,64,256]{3,2,1,0:T(8,128)} %collective-permute-done.refs_3_, f32[3,1,64,256]{3,2,1,0:T(8,128)} %collective-permute-done.1.refs_4_, ...), custom_call_target="tpu_custom_call" | custom-call | tf_op jit(solution)/shard_map/pallas_call | solution.py:247
  99.1 1.8 %fusion.54 = (f32[3,16,1,256]{3,2,1,0:T(1,128)}, f32[3,16,1,256]{3,2,1,0:T(1,128)}) fusion(f32[3,16,64,256]{3,2,1,0:T(8,128)} %get-tuple-element.30.refs_2_), kind=kLoop, calls=%fused_computation.76 | loop fusion | bytes 196608 | tf_op jit(solution)/shard_map/slice | solution.py:273
  102.5 1.8 %fusion.55 = (f32[3,1,64,256]{3,2,1,0:T(8,128)}, f32[3,1,64,256]{3,2,1,0:T(8,128)}) fusion(f32[3,16,64,256]{3,2,1,0:T(8,128)} %get-tuple-element.30.refs_2_), kind=kLoop, calls=%fused_computation.77 | loop fusion | bytes 786432 | tf_op jit(solution)/shard_map/slice | solution.py:273
  104.3 1.8 %collective-permute-start.5 = (f32[3,1,64,256]{3,2,1,0:T(8,128)}, f32[3,1,64,256]{3,2,1,0:T(8,128)}, u32[]{:S(2)}, u32[]{:S(2)}) collective-permute-start(f32[3,1,64,256]{3,2,1,0:T(8,128)} %get-tuple-element.36), channel_id=1, source_target_pairs={{2,0},{4,2},{6,4},{8,6},{10,8},{12,10},{14,12},{16,14},{18,16},{20... | collective-permute-start | bytes 589832 | tf_op jit(solution)/shard_map/ppermute | solution.py:273
  106.1 2.2 %collective-permute-start.4 = (f32[3,1,64,256]{3,2,1,0:T(8,128)}, f32[3,1,64,256]{3,2,1,0:T(8,128)}, u32[]{:S(2)}, u32[]{:S(2)}) collective-permute-start(f32[3,1,64,256]{3,2,1,0:T(8,128)} %get-tuple-element.37), channel_id=1, source_target_pairs={{0,2},{2,4},{4,6},{6,8},{8,10},{10,12},{12,14},{14,16},{16,18},{18... | collective-permute-start | bytes 589832 | tf_op jit(solution)/shard_map/ppermute | solution.py:272
  108.3 2.8 %all-to-all-done.1 = bf16[128,3,2,2048]{3,2,1,0:T(2,128)(2,1)} async-done(((bf16[128,3,2,2048]{3,2,1,0:T(2,128)(2,1)}), bf16[128,3,2,2048]{3,2,1,0:T(2,128)(2,1)}, u32[]{:S(2)}, u32[]{:S(2)}) %all-to-all-start.1) | async-done | bytes 3145760 | tf_op jit(solution)/shard_map/all_to_all | solution.py:321
  111.1 3.3 %fusion.13 = bf16[3,128,2048]{1,2,0:T(8,128)(2,1)S(1)} fusion(bf16[128,3,2,2048]{3,2,1,0:T(2,128)(2,1)} %all-to-all-done.1, s32[128,2]{0,1:T(2,128)} %copy-done.7, s32[128]{0:T(128)} %param.18), kind=kOutput, calls=%fused_computation.11 | convolution fusion | flops 403472384 | bytes 4720128 | tf_op jit(solution)/shard_map/jsr,scrb->cjb/dot_general | solution.py:322
  114.5 1.6 %copy.31 = bf16[3,128,2048]{2,1,0:T(8,128)(2,1)} copy(bf16[3,128,2048]{1,2,0:T(8,128)(2,1)S(1)} %fusion.13) | data formatting | bytes 3145728 | tf_op jit(solution)/shard_map/convert_element_type | solution.py:324
  116.1 2.6 %reshape.198.refs_7_ = bf16[3,16,64,256]{3,2,1,0:T(8,128)(2,1)S(1)} reshape(bf16[3,128,2048]{2,1,0:T(8,128)(2,1)} %copy.31) | data formatting | bytes 3145728 | tf_op jit(solution)/shard_map/reshape | solution.py:325
  120.0 21.8 %shard_map.123 = (f32[3,16,64,256]{3,2,1,0:T(8,128)}, f32[8,128]{1,0:T(8,128)S(1)}) custom-call(s32[32,8]{1,0:T(8,128)S(1)} %copy.32.refs_0_, f32[16]{0:T(128)S(1)} %copy-done.4, f32[3,16,64,256]{3,2,1,0:T(8,128)} %get-tuple-element.30.refs_2_, f32[3,1,64,256]{3,2,1,0:T(8,128)} %collective-permute-done.4.refs_3_, ...), custom_call_target="tpu_custom_call" | custom-call | tf_op jit(solution)/shard_map/pallas_call | solution.py:247
  142.4 3.9 %copy.49 = f32[3,16,64,256]{3,2,1,0:T(8,128)} copy(f32[3,16,64,256]{3,2,1,0:T(8,128)} %get-tuple-element.53) | data formatting | bytes 6291456
  (79 shorter events, 13.7 us)
Async XLA Ops:
  0.6 30.6 %copy-start.7 = (s32[128,2]{0,1:T(2,128)}, s32[128,2]{0,1:T(2,128)S(1)}, u32[]{:S(2)}) copy-start(s32[128,2]{0,1:T(2,128)S(1)} %multiply_add_fusion) | copy-start | bytes 3076
  10.4 20.7 %copy-start.16 = (f32[80]{0:T(128)S(1)}, f32[80]{0:T(128)}, u32[]{:S(2)}) copy-start(f32[80]{0:T(128)} %param.22) | copy-start | bytes 964
  10.4 20.7 %copy-start.9 = (s32[32,8]{0,1:T(8,128)S(1)}, s32[32,8]{0,1:T(8,128)}, u32[]{:S(2)}) copy-start(s32[32,8]{0,1:T(8,128)} %param.19) | copy-start | bytes 3076
  10.4 53.0 %all-to-all-start = ((bf16[128,3,2,2048]{3,2,1,0:T(2,128)(2,1)}), bf16[128,3,2,2048]{3,2,1,0:T(2,128)(2,1)S(1)}, u32[]{:S(2)}, u32[]{:S(2)}) async-start(bf16[128,3,2,2048]{3,2,1,0:T(2,128)(2,1)} %copy.25), calls=%async_computation | async-start | bytes 6291456 | tf_op jit(solution)/shard_map/all_to_all | solution.py:321
  23.7 55.4 %collective-permute-start.3 = (f32[3,16,1,256]{3,2,1,0:T(1,128)}, f32[3,16,1,256]{3,2,1,0:T(1,128)}, u32[]{:S(2)}, u32[]{:S(2)}) collective-permute-start(f32[3,16,1,256]{3,2,1,0:T(1,128)} %get-tuple-element.38), channel_id=1, source_target_pairs={{1,0},{0,1},{3,2},{2,3},{5,4},{4,5},{7,6},{6,7},{9,8},{8,9},{11,10... | collective-permute-start | bytes 147464 | tf_op jit(solution)/shard_map/ppermute | solution.py:273
  25.2 53.9 %collective-permute-start.2 = (f32[3,16,1,256]{3,2,1,0:T(1,128)}, f32[3,16,1,256]{3,2,1,0:T(1,128)}, u32[]{:S(2)}, u32[]{:S(2)}) collective-permute-start(f32[3,16,1,256]{3,2,1,0:T(1,128)} %get-tuple-element.39), channel_id=1, source_target_pairs={{0,1},{1,0},{2,3},{3,2},{4,5},{5,4},{6,7},{7,6},{8,9},{9,8},{10,11... | collective-permute-start | bytes 147464 | tf_op jit(solution)/shard_map/ppermute | solution.py:272
  27.1 52.1 %collective-permute-start.1 = (f32[3,1,64,256]{3,2,1,0:T(8,128)}, f32[3,1,64,256]{3,2,1,0:T(8,128)}, u32[]{:S(2)}, u32[]{:S(2)}) collective-permute-start(f32[3,1,64,256]{3,2,1,0:T(8,128)} %get-tuple-element.40), channel_id=1, source_target_pairs={{2,0},{4,2},{6,4},{8,6},{10,8},{12,10},{14,12},{16,14},{18,16},{20... | collective-permute-start | bytes 589832 | tf_op jit(solution)/shard_map/ppermute | solution.py:273
  28.6 50.5 %collective-permute-start = (f32[3,1,64,256]{3,2,1,0:T(8,128)}, f32[3,1,64,256]{3,2,1,0:T(8,128)}, u32[]{:S(2)}, u32[]{:S(2)}) collective-permute-start(f32[3,1,64,256]{3,2,1,0:T(8,128)} %get-tuple-element.41), channel_id=1, source_target_pairs={{0,2},{2,4},{4,6},{6,8},{8,10},{10,12},{12,14},{14,16},{16,18},{18... | collective-permute-start | bytes 589832 | tf_op jit(solution)/shard_map/ppermute | solution.py:272
  31.1 7.5 %copy-start.12 = (f32[80]{0:T(128)}, f32[80]{0:T(128)S(1)}, u32[]{:S(2)}) copy-start(f32[80]{0:T(128)S(1)} %cos.4) | copy-start | bytes 964
  33.7 4.9 %copy-start.10 = (f32[80]{0:T(128)S(1)}, f32[80]{0:T(128)}, u32[]{:S(2)}) copy-start(f32[80]{0:T(128)} %param.21) | copy-start | bytes 964
  33.7 4.9 %copy-start.15 = (s32[80]{0:T(128)S(1)}, s32[80]{0:T(128)}, u32[]{:S(2)}) copy-start(s32[80]{0:T(128)} %param.24) | copy-start | bytes 964
  33.7 4.9 %copy-start.14 = (f32[3,80]{1,0:T(4,128)S(1)}, f32[3,80]{1,0:T(4,128)}, u32[]{:S(2)}) copy-start(f32[3,80]{1,0:T(4,128)} %param.23) | copy-start | bytes 2884
  63.4 6.5 %copy-start.5 = (bf16[128,3,2,2048]{3,2,1,0:T(2,128)(2,1)}, bf16[128,3,2,2048]{3,2,1,0:T(2,128)(2,1)S(1)}, u32[]{:S(2)}) copy-start(bf16[128,3,2,2048]{3,2,1,0:T(2,128)(2,1)S(1)} %all-to-all-done) | copy-start | bytes 9437188
  63.4 47.7 %all-to-all-start.1 = ((bf16[128,3,2,2048]{3,2,1,0:T(2,128)(2,1)}), bf16[128,3,2,2048]{3,2,1,0:T(2,128)(2,1)}, u32[]{:S(2)}, u32[]{:S(2)}) async-start(bf16[128,3,2,2048]{3,2,1,0:T(2,128)(2,1)} %copy.29), calls=%async_computation.1 | async-start | bytes 6291456 | tf_op jit(solution)/shard_map/all_to_all | solution.py:321
  69.9 3.5 %copy-start.8 = (s32[128,2]{0,1:T(2,128)S(1)}, s32[128,2]{0,1:T(2,128)}, u32[]{:S(2)}) copy-start(s32[128,2]{0,1:T(2,128)} %copy-done.7) | copy-start | bytes 3076
  69.9 3.5 %copy-start.19 = (s32[128]{0:T(128)S(1)}, s32[128]{0:T(128)}, u32[]{:S(2)}) copy-start(s32[128]{0:T(128)} %param.18) | copy-start | bytes 1540
  74.9 4.2 %copy-start = (bf16[8,128,128]{2,1,0:T(8,128)(2,1)S(1)}, bf16[8,128,128]{2,1,0:T(8,128)(2,1)}, u32[]{:S(2)}) copy-start(bf16[8,128,128]{2,1,0:T(8,128)(2,1)} %param.20) | copy-start | bytes 786436
  101.0 17.7 %collective-permute-start.7 = (f32[3,16,1,256]{3,2,1,0:T(1,128)}, f32[3,16,1,256]{3,2,1,0:T(1,128)}, u32[]{:S(2)}, u32[]{:S(2)}) collective-permute-start(f32[3,16,1,256]{3,2,1,0:T(1,128)} %get-tuple-element.34), channel_id=1, source_target_pairs={{1,0},{0,1},{3,2},{2,3},{5,4},{4,5},{7,6},{6,7},{9,8},{8,9},{11,10... | collective-permute-start | bytes 147464 | tf_op jit(solution)/shard_map/ppermute | solution.py:273
  102.5 16.2 %collective-permute-start.6 = (f32[3,16,1,256]{3,2,1,0:T(1,128)}, f32[3,16,1,256]{3,2,1,0:T(1,128)}, u32[]{:S(2)}, u32[]{:S(2)}) collective-permute-start(f32[3,16,1,256]{3,2,1,0:T(1,128)} %get-tuple-element.35), channel_id=1, source_target_pairs={{0,1},{1,0},{2,3},{3,2},{4,5},{5,4},{6,7},{7,6},{8,9},{9,8},{10,11... | collective-permute-start | bytes 147464 | tf_op jit(solution)/shard_map/ppermute | solution.py:272
  104.3 14.4 %collective-permute-start.5 = (f32[3,1,64,256]{3,2,1,0:T(8,128)}, f32[3,1,64,256]{3,2,1,0:T(8,128)}, u32[]{:S(2)}, u32[]{:S(2)}) collective-permute-start(f32[3,1,64,256]{3,2,1,0:T(8,128)} %get-tuple-element.36), channel_id=1, source_target_pairs={{2,0},{4,2},{6,4},{8,6},{10,8},{12,10},{14,12},{16,14},{18,16},{20... | collective-permute-start | bytes 589832 | tf_op jit(solution)/shard_map/ppermute | solution.py:273
  106.1 12.6 %collective-permute-start.4 = (f32[3,1,64,256]{3,2,1,0:T(8,128)}, f32[3,1,64,256]{3,2,1,0:T(8,128)}, u32[]{:S(2)}, u32[]{:S(2)}) collective-permute-start(f32[3,1,64,256]{3,2,1,0:T(8,128)} %get-tuple-element.37), channel_id=1, source_target_pairs={{0,2},{2,4},{4,6},{6,8},{8,10},{10,12},{12,14},{14,16},{16,18},{18... | collective-permute-start | bytes 589832 | tf_op jit(solution)/shard_map/ppermute | solution.py:272
  120.0 21.8 %copy-start.11 = (f32[80]{0:T(128)S(1)}, f32[80]{0:T(128)}, u32[]{:S(2)}) copy-start(f32[80]{0:T(128)} %param.21) | copy-start | bytes 964
  120.0 21.8 %copy-start.13 = (f32[80]{0:T(128)S(1)}, f32[80]{0:T(128)}, u32[]{:S(2)}) copy-start(f32[80]{0:T(128)} %copy-done.12) | copy-start | bytes 964
  120.0 21.8 %copy-start.17 = (f32[80]{0:T(128)S(1)}, f32[80]{0:T(128)}, u32[]{:S(2)}) copy-start(f32[80]{0:T(128)} %param.22) | copy-start | bytes 964
  (6 other events, 7.0 us)

commit v7 on v6

--- a/solution.py
+++ b/solution.py
@@ -64,10 +64,10 @@
 
 def advance_kernel(count_y, group, exchange, *refs):
     (cols_ref, fringe_ref, a_ref, w_ref, e_ref, s_ref, n_ref, u_ref, drag_ref, eddy_ref, pk_ref, azh_ref,
-     prior_ref, out_ref, sum_ref, xq, prod) = refs[:17]
+     prior_ref, out_ref, sum_ref, first_plane, last_plane, first_row, last_row, xq, prod) = refs[:21]
     components, width_x, width_y, height = a_ref.shape
     if exchange:
-        near, far, sems = refs[17:]
+        near, far, sems = refs[21:]
         total = lax.axis_size("gx") * count_y
         groups = total // group
         me = lax.axis_index("gx") * count_y + lax.axis_index("gy")
@@ -107,8 +107,8 @@
         return acc + pk_ref[x] * projected
 
     acc = lax.fori_loop(0, width_x, turbine_plane, jnp.zeros(pk_ref.shape[1:], jnp.float32))
-    first_row = lax.broadcasted_iota(jnp.int32, prior_ref.shape, 0) == 0
-    part = prior_ref[...] + jnp.where(first_row, jnp.sum(acc, axis=0, keepdims=True), 0.0)
+    leading_row = lax.broadcasted_iota(jnp.int32, prior_ref.shape, 0) == 0
+    part = prior_ref[...] + jnp.where(leading_row, jnp.sum(acc, axis=0, keepdims=True), 0.0)
     if exchange:
         pl.semaphore_wait(barrier, group + groups - 2)
         near[mine] = part
@@ -201,7 +201,14 @@
             )
             if c == 0:
                 update = update - drag * center
-            out_ref[c, x] = update * scale
+            final = update * scale
+            out_ref[c, x] = final
+            first_row[c, x] = final[0:1, :]
+            last_row[c, x] = final[width_y - 1 :, :]
+            if isinstance(x, int) and x == 0:
+                first_plane[c, 0] = final
+            if isinstance(x, int) and x == width_x - 1:
+                last_plane[c, 0] = final
 
     plane(0, lambda c: w_ref[c, 0], lambda c: a_ref[c, 1])
 
@@ -231,7 +238,14 @@
     paired = eddy_blocks.reshape(KB // 2, 2 * eddy_blocks.shape[1], eddy_blocks.shape[2])
     operands = [columns, fringe_scale, adjoint, west, east, south, north, forward, drag_field, paired]
     operands += list(turbine) + [prior]
-    out_shape = (jax.ShapeDtypeStruct(adjoint.shape, jnp.float32), jax.ShapeDtypeStruct(prior.shape, jnp.float32))
+    out_shape = (
+        jax.ShapeDtypeStruct(adjoint.shape, jnp.float32),
+        jax.ShapeDtypeStruct(prior.shape, jnp.float32),
+        jax.ShapeDtypeStruct((components, 1, width_y, height), jnp.float32),
+        jax.ShapeDtypeStruct((components, 1, width_y, height), jnp.float32),
+        jax.ShapeDtypeStruct((components, width_x, 1, height), jnp.float32),
+        jax.ShapeDtypeStruct((components, width_x, 1, height), jnp.float32),
+    )
     scratch = [
         pltpu.VMEM(((width_x + 2) * NZB, components * width_y, height // NZB), jnp.bfloat16),
         pltpu.VMEM((width_x * NZB, components * width_y, height // NZB), jnp.float32),
@@ -248,7 +262,7 @@
         functools.partial(advance_kernel, count_y, group, exchange),
         out_shape=out_shape,
         in_specs=[smem, smem] + [vmem] * (len(operands) - 2),
-        out_specs=(vmem, vmem),
+        out_specs=tuple([vmem] * len(out_shape)),
         scratch_shapes=scratch,
         compiler_params=pltpu.CompilerParams(**params),
     )(*operands)
@@ -265,13 +279,11 @@
     return weights, jnp.stack([high, low]).astype(jnp.bfloat16)
 
 
-def halo(block, axis, dim):
+def halo(first, last, axis):
     count = lax.axis_size(axis)
     forward = [(i, (i + 1) % count) for i in range(count)]
     backward = [(target, source) for source, target in forward]
-    low = lax.ppermute(lax.slice_in_dim(block, block.shape[dim] - 1, None, axis=dim), axis, forward)
-    high = lax.ppermute(lax.slice_in_dim(block, 0, 1, axis=dim), axis, backward)
-    return low, high
+    return lax.ppermute(last, axis, forward), lax.ppermute(first, axis, backward)
 
 
 def shards(
@@ -313,6 +325,10 @@
     turbine = turbine_tables(owned_mask, plan_kernel, along_z, width_x, width_y)
     adjoint = adjoint_in
     gradient_block = jnp.zeros((8, 128), jnp.float32)
+    edges = (
+        (adjoint[:, :1], adjoint[:, -1:]),
+        (adjoint[:, :, :1], adjoint[:, :, -1:]),
+    )
     for step_index in range(steps_total):
         stored = checkpoints[steps_total - 1 - step_index]
         packed = jnp.einsum(
@@ -323,12 +339,13 @@
             "jsr,scrb->cjb", pick_table, arrived, preferred_element_type=jnp.float32
         ).astype(jnp.bfloat16)
         forward = forward.reshape(components, width_x, width_y, height)
-        west, east = halo(adjoint, "gx", 1)
-        south, north = halo(adjoint, "gy", 2)
-        adjoint, gradient_block = advance(
+        west, east = halo(*edges[0], "gx")
+        south, north = halo(*edges[1], "gy")
+        adjoint, gradient_block, first_plane, last_plane, first_row, last_row = advance(
             adjoint, west, east, south, north, forward, block_columns, eddy_blocks, drag_field, fringe_scale,
             turbine, gradient_block, step_index == steps_total - 1,
         )
+        edges = ((first_plane, last_plane), (first_row, last_row))
     gradient_sum = gradient_block[0, : thrust.shape[0]]
     cosine = jnp.cos(yaw_angle)
     sine = jnp.sin(yaw_angle)

time: 149 us -> 146 us (0.980)
  local copies, waits for them, and re-layouts: 32 us -> 28.5 us
  waiting for transfers between devices: 27.6 us -> 31 us
    slice x4 -> x2, local copies, waits for them, and re-layouts: 7.26 us -> 3.64 us  [the longest x1 1.84 us: shards(): adjoint[:, :, :1]]
    all_to_all x2, waiting for transfers between devices: 27.6 us -> 31 us  [shards(): lax.all_to_all(packed, ('gx', 'gy'), split_axis=0, concat_axis=0, tiled=T...]
  transfers between devices with their start and end apart: 10 -> 10, of which waited for: 2 -> 2; matrix products, arithmetic and copies ran while one was open for 21% -> 19% of each run, Pallas kernels for 13% -> 13%
where the time goes in v7:
time: 146 us; the launch traced here: 145 us
  Pallas kernels  39.1 us (27%)
  waiting for transfers between devices  31 us (21%)
  starting transfers between devices  29.1 us (20%)
  local copies, waits for them, and re-layouts  28.5 us (20%)
  matrix products  10.7 us (7%)
  other arithmetic  5.35 us (4%)
    pallas_call x2, Pallas kernels, advance(): pl.pallas_call(functools.partial(advance_kernel, count_y, group, exchange...  39.1 us
    all_to_all x2, waiting for transfers between devices, shards(): lax.all_to_all(packed, ('gx', 'gy'), split_axis=0, concat_axis=0, tiled=T...  31 us
    all_to_all x2, starting transfers between devices, shards(): lax.all_to_all(packed, ('gx', 'gy'), split_axis=0, concat_axis=0, tiled=T...  18 us
    convert_element_type x2, local copies, waits for them, and re-layouts, shards(): packed = jnp.einsum('drs,scb->dcrb', pack_table, stored, preferred_elemen...  9.8 us
    ppermute x4, starting transfers between devices, halo(): lax.ppermute(last, axis, forward)  8.01 us
    unnamed x42, local copies, waits for them, and re-layouts  6.64 us
    reshape x2, local copies, waits for them, and re-layouts, shards(): forward = forward.reshape(components, width_x, width_y, height)  5.16 us
    dot_general x2, matrix products, shards(): jnp.einsum('drs,scb->dcrb', pack_table, stored, preferred_element_type=jn...  4.84 us
  transfers between devices with their start and end apart: 10, of which 2 were waited for; matrix products, arithmetic and copies ran while one was open for 19% of the time, Pallas kernels for 13%

profile of v7, /device:TPU:1, one launch (start us, length us, event | category | flops | bytes accessed | tf_op | source)
XLA Modules:
  0.0 144.7 jit_solution(3136036882436731848)
XLA Ops:
  3.1 2.4 %fusion.4 = bf16[128,3,2,2048]{3,0,1,2:T(8,128)(2,1)S(1)} fusion(bf16[2,128,3,2048]{3,1,2,0:T(8,128)(2,1)} %param.16, s32[128]{0:T(128)S(1)} %add_add_fusion, s32[128,2]{0,1:T(2,128)S(1)} %multiply_add_fusion), kind=kOutput, calls=%fused_computation.8 | convolution fusion | flops 404258816 | bytes 4720128 | tf_op jit(solution)/shard_map/drs,scb->dcrb/dot_general | solution.py:334
  5.5 4.9 %copy.25 = bf16[128,3,2,2048]{3,2,1,0:T(2,128)(2,1)} copy(bf16[128,3,2,2048]{3,0,1,2:T(8,128)(2,1)S(1)} %fusion.4) | data formatting | bytes 6291456 | tf_op jit(solution)/shard_map/convert_element_type | solution.py:336
  10.4 11.5 %all-to-all-start = ((bf16[128,3,2,2048]{3,2,1,0:T(2,128)(2,1)}), bf16[128,3,2,2048]{3,2,1,0:T(2,128)(2,1)S(1)}, u32[]{:S(2)}, u32[]{:S(2)}) async-start(bf16[128,3,2,2048]{3,2,1,0:T(2,128)(2,1)} %copy.25), calls=%async_computation | async-start | bytes 6291456 | tf_op jit(solution)/shard_map/all_to_all | solution.py:337
  21.9 1.8 %fusion.54 = (f32[3,16,1,256]{3,2,1,0:T(1,128)}, f32[3,16,1,256]{3,2,1,0:T(1,128)}) fusion(f32[3,16,64,256]{3,2,1,0:T(8,128)} %refs_2_.1), kind=kLoop, calls=%fused_computation.76 | loop fusion | bytes 196608 | tf_op jit(solution)/shard_map/slice | solution.py:330
  23.7 1.5 %collective-permute-start.3 = (f32[3,16,1,256]{3,2,1,0:T(1,128)}, f32[3,16,1,256]{3,2,1,0:T(1,128)}, u32[]{:S(2)}, u32[]{:S(2)}) collective-permute-start(f32[3,16,1,256]{3,2,1,0:T(1,128)} %get-tuple-element.42), channel_id=1, source_target_pairs={{1,0},{0,1},{3,2},{2,3},{5,4},{4,5},{7,6},{6,7},{9,8},{8,9},{11,10... | collective-permute-start | bytes 147464 | tf_op jit(solution)/shard_map/ppermute | solution.py:286
  25.3 1.8 %fusion.55 = (f32[3,1,64,256]{3,2,1,0:T(8,128)}, f32[3,1,64,256]{3,2,1,0:T(8,128)}) fusion(f32[3,16,64,256]{3,2,1,0:T(8,128)} %refs_2_.1), kind=kLoop, calls=%fused_computation.77 | loop fusion | bytes 786432 | tf_op jit(solution)/shard_map/slice | solution.py:329
  27.1 1.6 %collective-permute-start.1 = (f32[3,1,64,256]{3,2,1,0:T(8,128)}, f32[3,1,64,256]{3,2,1,0:T(8,128)}, u32[]{:S(2)}, u32[]{:S(2)}) collective-permute-start(f32[3,1,64,256]{3,2,1,0:T(8,128)} %get-tuple-element.44), channel_id=1, source_target_pairs={{2,0},{4,2},{6,4},{8,6},{10,8},{12,10},{14,12},{16,14},{18,16},{20... | collective-permute-start | bytes 589832 | tf_op jit(solution)/shard_map/ppermute | solution.py:286
  28.6 2.5 %collective-permute-start = (f32[3,1,64,256]{3,2,1,0:T(8,128)}, f32[3,1,64,256]{3,2,1,0:T(8,128)}, u32[]{:S(2)}, u32[]{:S(2)}) collective-permute-start(f32[3,1,64,256]{3,2,1,0:T(8,128)} %get-tuple-element.45), channel_id=1, source_target_pairs={{0,2},{2,4},{4,6},{6,8},{8,10},{10,12},{12,14},{14,16},{16,18},{18... | collective-permute-start | bytes 589832 | tf_op jit(solution)/shard_map/ppermute | solution.py:286
  31.2 2.4 %fusion.5 = bf16[128,3,2,2048]{3,0,1,2:T(8,128)(2,1)S(1)} fusion(bf16[2,128,3,2048]{3,1,2,0:T(8,128)(2,1)} %param.16, s32[128]{0:T(128)S(1)} %add_add_fusion, s32[128,2]{0,1:T(2,128)S(1)} %multiply_add_fusion), kind=kOutput, calls=%fused_computation.9 | convolution fusion | flops 404258816 | bytes 4720128 | tf_op jit(solution)/shard_map/drs,scb->dcrb/dot_general | solution.py:334
  33.7 4.9 %copy.29 = bf16[128,3,2,2048]{3,2,1,0:T(2,128)(2,1)} copy(bf16[128,3,2,2048]{3,0,1,2:T(8,128)(2,1)S(1)} %fusion.5) | data formatting | bytes 6291456 | tf_op jit(solution)/shard_map/convert_element_type | solution.py:336
  38.6 24.9 %all-to-all-done = bf16[128,3,2,2048]{3,2,1,0:T(2,128)(2,1)S(1)} async-done(((bf16[128,3,2,2048]{3,2,1,0:T(2,128)(2,1)}), bf16[128,3,2,2048]{3,2,1,0:T(2,128)(2,1)S(1)}, u32[]{:S(2)}, u32[]{:S(2)}) %all-to-all-start) | async-done | bytes 3145760 | tf_op jit(solution)/shard_map/all_to_all | solution.py:337
  63.4 6.5 %all-to-all-start.1 = ((bf16[128,3,2,2048]{3,2,1,0:T(2,128)(2,1)}), bf16[128,3,2,2048]{3,2,1,0:T(2,128)(2,1)}, u32[]{:S(2)}, u32[]{:S(2)}) async-start(bf16[128,3,2,2048]{3,2,1,0:T(2,128)(2,1)} %copy.29), calls=%async_computation.1 | async-start | bytes 6291456 | tf_op jit(solution)/shard_map/all_to_all | solution.py:337
  73.5 1.5 %fusion.10 = bf16[3,128,2048]{1,2,0:T(8,128)(2,1)S(1)} fusion(bf16[128,3,2,2048]{3,2,1,0:T(2,128)(2,1)S(1)} %copy-done.6, s32[128,2]{0,1:T(2,128)S(1)} %copy-done.8, s32[128]{0:T(128)S(1)} %copy-done.19), kind=kOutput, calls=%fused_computation.10 | convolution fusion | flops 403472384 | bytes 4720128 | tf_op jit(solution)/shard_map/jsr,scrb->cjb/dot_general | solution.py:338
  75.0 1.6 %copy.27 = bf16[3,128,2048]{2,1,0:T(8,128)(2,1)} copy(bf16[3,128,2048]{1,2,0:T(8,128)(2,1)S(1)} %fusion.10) | data formatting | bytes 3145728 | tf_op jit(solution)/shard_map/convert_element_type | solution.py:340
  76.6 2.6 %reshape.195.refs_7_ = bf16[3,16,64,256]{3,2,1,0:T(8,128)(2,1)S(1)} reshape(bf16[3,128,2048]{2,1,0:T(8,128)(2,1)} %copy.27) | data formatting | bytes 3145728 | tf_op jit(solution)/shard_map/reshape | solution.py:341
  79.9 19.0 %shard_map.122 = (f32[3,16,64,256]{3,2,1,0:T(8,128)}, f32[8,128]{1,0:T(8,128)S(1)}, f32[3,1,64,256]{3,2,1,0:T(8,128)}, f32[3,1,64,256]{3,2,1,0:T(8,128)}, f32[3,...) custom-call(s32[32,8]{1,0:T(8,128)S(1)} %copy.32.refs_0_, f32[16]{0:T(128)S(1)} %copy-done.3, f32[3,16,64,256]{3,2,1,0:T(8,128)} %refs_2_.1, ...), custom_call_target="tpu_custom_call" | custom-call | tf_op jit(solution)/shard_map/pallas_call | solution.py:261
  99.5 1.5 %collective-permute-start.6 = (f32[3,16,1,256]{3,2,1,0:T(1,128)}, f32[3,16,1,256]{3,2,1,0:T(1,128)}, u32[]{:S(2)}, u32[]{:S(2)}) collective-permute-start(f32[3,16,1,256]{3,2,1,0:T(1,128)} %get-tuple-element.37), channel_id=1, source_target_pairs={{0,1},{1,0},{2,3},{3,2},{4,5},{5,4},{6,7},{7,6},{8,9},{9,8},{10,11... | collective-permute-start | bytes 147464 | tf_op jit(solution)/shard_map/ppermute | solution.py:286
  101.0 4.0 %collective-permute-start.4 = (f32[3,1,64,256]{3,2,1,0:T(8,128)}, f32[3,1,64,256]{3,2,1,0:T(8,128)}, u32[]{:S(2)}, u32[]{:S(2)}) collective-permute-start(f32[3,1,64,256]{3,2,1,0:T(8,128)} %get-tuple-element.35), channel_id=1, source_target_pairs={{0,2},{2,4},{4,6},{6,8},{8,10},{10,12},{12,14},{14,16},{16,18},{18... | collective-permute-start | bytes 589832 | tf_op jit(solution)/shard_map/ppermute | solution.py:286
  105.0 6.1 %all-to-all-done.1 = bf16[128,3,2,2048]{3,2,1,0:T(2,128)(2,1)} async-done(((bf16[128,3,2,2048]{3,2,1,0:T(2,128)(2,1)}), bf16[128,3,2,2048]{3,2,1,0:T(2,128)(2,1)}, u32[]{:S(2)}, u32[]{:S(2)}) %all-to-all-start.1) | async-done | bytes 3145760 | tf_op jit(solution)/shard_map/all_to_all | solution.py:337
  111.1 3.3 %fusion.13 = bf16[3,128,2048]{1,2,0:T(8,128)(2,1)S(1)} fusion(bf16[128,3,2,2048]{3,2,1,0:T(2,128)(2,1)} %all-to-all-done.1, s32[128,2]{0,1:T(2,128)} %copy-done.7, s32[128]{0:T(128)} %param.18), kind=kOutput, calls=%fused_computation.11 | convolution fusion | flops 403472384 | bytes 4720128 | tf_op jit(solution)/shard_map/jsr,scrb->cjb/dot_general | solution.py:338
  114.5 1.6 %copy.31 = bf16[3,128,2048]{2,1,0:T(8,128)(2,1)} copy(bf16[3,128,2048]{1,2,0:T(8,128)(2,1)S(1)} %fusion.13) | data formatting | bytes 3145728 | tf_op jit(solution)/shard_map/convert_element_type | solution.py:340
  116.1 2.6 %reshape.198.refs_7_ = bf16[3,16,64,256]{3,2,1,0:T(8,128)(2,1)S(1)} reshape(bf16[3,128,2048]{2,1,0:T(8,128)(2,1)} %copy.31) | data formatting | bytes 3145728 | tf_op jit(solution)/shard_map/reshape | solution.py:341
  120.1 20.1 %shard_map.123 = (f32[3,16,64,256]{3,2,1,0:T(8,128)}, f32[8,128]{1,0:T(8,128)S(1)}, f32[3,1,64,256]{3,2,1,0:T(8,128)}, f32[3,1,64,256]{3,2,1,0:T(8,128)}, f32[3,...) custom-call(s32[32,8]{1,0:T(8,128)S(1)} %copy.32.refs_0_, f32[16]{0:T(128)S(1)} %copy-done.4, ...), custom_call_target="tpu_custom_call" | custom-call | tf_op jit(solution)/shard_map/pallas_call | solution.py:261
  140.8 3.9 %copy.49 = f32[3,16,64,256]{3,2,1,0:T(8,128)} copy(f32[3,16,64,256]{3,2,1,0:T(8,128)} %get-tuple-element.57) | data formatting | bytes 6291456
  (77 shorter events, 9.3 us)
Async XLA Ops:
  0.6 30.6 %copy-start.7 = (s32[128,2]{0,1:T(2,128)}, s32[128,2]{0,1:T(2,128)S(1)}, u32[]{:S(2)}) copy-start(s32[128,2]{0,1:T(2,128)S(1)} %multiply_add_fusion) | copy-start | bytes 3076
  10.4 20.7 %copy-start.16 = (f32[80]{0:T(128)S(1)}, f32[80]{0:T(128)}, u32[]{:S(2)}) copy-start(f32[80]{0:T(128)} %param.22) | copy-start | bytes 964
  10.4 20.8 %copy-start.9 = (s32[32,8]{0,1:T(8,128)S(1)}, s32[32,8]{0,1:T(8,128)}, u32[]{:S(2)}) copy-start(s32[32,8]{0,1:T(8,128)} %param.19) | copy-start | bytes 3076
  10.4 53.0 %all-to-all-start = ((bf16[128,3,2,2048]{3,2,1,0:T(2,128)(2,1)}), bf16[128,3,2,2048]{3,2,1,0:T(2,128)(2,1)S(1)}, u32[]{:S(2)}, u32[]{:S(2)}) async-start(bf16[128,3,2,2048]{3,2,1,0:T(2,128)(2,1)} %copy.25), calls=%async_computation | async-start | bytes 6291456 | tf_op jit(solution)/shard_map/all_to_all | solution.py:337
  23.7 55.4 %collective-permute-start.3 = (f32[3,16,1,256]{3,2,1,0:T(1,128)}, f32[3,16,1,256]{3,2,1,0:T(1,128)}, u32[]{:S(2)}, u32[]{:S(2)}) collective-permute-start(f32[3,16,1,256]{3,2,1,0:T(1,128)} %get-tuple-element.42), channel_id=1, source_target_pairs={{1,0},{0,1},{3,2},{2,3},{5,4},{4,5},{7,6},{6,7},{9,8},{8,9},{11,10... | collective-permute-start | bytes 147464 | tf_op jit(solution)/shard_map/ppermute | solution.py:286
  25.2 53.9 %collective-permute-start.2 = (f32[3,16,1,256]{3,2,1,0:T(1,128)}, f32[3,16,1,256]{3,2,1,0:T(1,128)}, u32[]{:S(2)}, u32[]{:S(2)}) collective-permute-start(f32[3,16,1,256]{3,2,1,0:T(1,128)} %get-tuple-element.43), channel_id=1, source_target_pairs={{0,1},{1,0},{2,3},{3,2},{4,5},{5,4},{6,7},{7,6},{8,9},{9,8},{10,11... | collective-permute-start | bytes 147464 | tf_op jit(solution)/shard_map/ppermute | solution.py:286
  27.1 52.1 %collective-permute-start.1 = (f32[3,1,64,256]{3,2,1,0:T(8,128)}, f32[3,1,64,256]{3,2,1,0:T(8,128)}, u32[]{:S(2)}, u32[]{:S(2)}) collective-permute-start(f32[3,1,64,256]{3,2,1,0:T(8,128)} %get-tuple-element.44), channel_id=1, source_target_pairs={{2,0},{4,2},{6,4},{8,6},{10,8},{12,10},{14,12},{16,14},{18,16},{20... | collective-permute-start | bytes 589832 | tf_op jit(solution)/shard_map/ppermute | solution.py:286
  28.6 50.6 %collective-permute-start = (f32[3,1,64,256]{3,2,1,0:T(8,128)}, f32[3,1,64,256]{3,2,1,0:T(8,128)}, u32[]{:S(2)}, u32[]{:S(2)}) collective-permute-start(f32[3,1,64,256]{3,2,1,0:T(8,128)} %get-tuple-element.45), channel_id=1, source_target_pairs={{0,2},{2,4},{4,6},{6,8},{8,10},{10,12},{12,14},{14,16},{16,18},{18... | collective-permute-start | bytes 589832 | tf_op jit(solution)/shard_map/ppermute | solution.py:286
  31.2 38.8 %copy-start.12 = (f32[80]{0:T(128)}, f32[80]{0:T(128)S(1)}, u32[]{:S(2)}) copy-start(f32[80]{0:T(128)S(1)} %cos.4) | copy-start | bytes 964
  38.6 31.3 %copy-start.15 = (s32[80]{0:T(128)S(1)}, s32[80]{0:T(128)}, u32[]{:S(2)}) copy-start(s32[80]{0:T(128)} %param.24) | copy-start | bytes 964
  38.6 31.4 %copy-start.10 = (f32[80]{0:T(128)S(1)}, f32[80]{0:T(128)}, u32[]{:S(2)}) copy-start(f32[80]{0:T(128)} %param.21) | copy-start | bytes 964
  38.6 31.4 %copy-start.14 = (f32[3,80]{1,0:T(4,128)S(1)}, f32[3,80]{1,0:T(4,128)}, u32[]{:S(2)}) copy-start(f32[3,80]{1,0:T(4,128)} %param.23) | copy-start | bytes 2884
  63.4 6.5 %copy-start.5 = (bf16[128,3,2,2048]{3,2,1,0:T(2,128)(2,1)}, bf16[128,3,2,2048]{3,2,1,0:T(2,128)(2,1)S(1)}, u32[]{:S(2)}) copy-start(bf16[128,3,2,2048]{3,2,1,0:T(2,128)(2,1)S(1)} %all-to-all-done) | copy-start | bytes 9437188
  63.4 47.7 %all-to-all-start.1 = ((bf16[128,3,2,2048]{3,2,1,0:T(2,128)(2,1)}), bf16[128,3,2,2048]{3,2,1,0:T(2,128)(2,1)}, u32[]{:S(2)}, u32[]{:S(2)}) async-start(bf16[128,3,2,2048]{3,2,1,0:T(2,128)(2,1)} %copy.29), calls=%async_computation.1 | async-start | bytes 6291456 | tf_op jit(solution)/shard_map/all_to_all | solution.py:337
  69.9 3.6 %copy-start.8 = (s32[128,2]{0,1:T(2,128)S(1)}, s32[128,2]{0,1:T(2,128)}, u32[]{:S(2)}) copy-start(s32[128,2]{0,1:T(2,128)} %copy-done.7) | copy-start | bytes 3076
  69.9 3.6 %copy-start.19 = (s32[128]{0:T(128)S(1)}, s32[128]{0:T(128)}, u32[]{:S(2)}) copy-start(s32[128]{0:T(128)} %param.18) | copy-start | bytes 1540
  75.0 4.2 %copy-start = (bf16[8,128,128]{2,1,0:T(8,128)(2,1)S(1)}, bf16[8,128,128]{2,1,0:T(8,128)(2,1)}, u32[]{:S(2)}) copy-start(bf16[8,128,128]{2,1,0:T(8,128)(2,1)} %param.20) | copy-start | bytes 786436
  99.5 19.2 %collective-permute-start.6 = (f32[3,16,1,256]{3,2,1,0:T(1,128)}, f32[3,16,1,256]{3,2,1,0:T(1,128)}, u32[]{:S(2)}, u32[]{:S(2)}) collective-permute-start(f32[3,16,1,256]{3,2,1,0:T(1,128)} %get-tuple-element.37), channel_id=1, source_target_pairs={{0,1},{1,0},{2,3},{3,2},{4,5},{5,4},{6,7},{7,6},{8,9},{9,8},{10,11... | collective-permute-start | bytes 147464 | tf_op jit(solution)/shard_map/ppermute | solution.py:286
  101.0 17.7 %collective-permute-start.7 = (f32[3,16,1,256]{3,2,1,0:T(1,128)}, f32[3,16,1,256]{3,2,1,0:T(1,128)}, u32[]{:S(2)}, u32[]{:S(2)}) collective-permute-start(f32[3,16,1,256]{3,2,1,0:T(1,128)} %get-tuple-element.38), channel_id=1, source_target_pairs={{1,0},{0,1},{3,2},{2,3},{5,4},{4,5},{7,6},{6,7},{9,8},{8,9},{11,10... | collective-permute-start | bytes 147464 | tf_op jit(solution)/shard_map/ppermute | solution.py:286
  101.0 17.7 %collective-permute-start.4 = (f32[3,1,64,256]{3,2,1,0:T(8,128)}, f32[3,1,64,256]{3,2,1,0:T(8,128)}, u32[]{:S(2)}, u32[]{:S(2)}) collective-permute-start(f32[3,1,64,256]{3,2,1,0:T(8,128)} %get-tuple-element.35), channel_id=1, source_target_pairs={{0,2},{2,4},{4,6},{6,8},{8,10},{10,12},{12,14},{14,16},{16,18},{18... | collective-permute-start | bytes 589832 | tf_op jit(solution)/shard_map/ppermute | solution.py:286
  105.0 13.7 %collective-permute-start.5 = (f32[3,1,64,256]{3,2,1,0:T(8,128)}, f32[3,1,64,256]{3,2,1,0:T(8,128)}, u32[]{:S(2)}, u32[]{:S(2)}) collective-permute-start(f32[3,1,64,256]{3,2,1,0:T(8,128)} %get-tuple-element.36), channel_id=1, source_target_pairs={{2,0},{4,2},{6,4},{8,6},{10,8},{12,10},{14,12},{16,14},{18,16},{20... | collective-permute-start | bytes 589832 | tf_op jit(solution)/shard_map/ppermute | solution.py:286
  120.0 20.1 %copy-start.11 = (f32[80]{0:T(128)S(1)}, f32[80]{0:T(128)}, u32[]{:S(2)}) copy-start(f32[80]{0:T(128)} %param.21) | copy-start | bytes 964
  120.0 20.1 %copy-start.13 = (f32[80]{0:T(128)S(1)}, f32[80]{0:T(128)}, u32[]{:S(2)}) copy-start(f32[80]{0:T(128)} %copy-done.12) | copy-start | bytes 964
  120.0 20.1 %copy-start.17 = (f32[80]{0:T(128)S(1)}, f32[80]{0:T(128)}, u32[]{:S(2)}) copy-start(f32[80]{0:T(128)} %param.22) | copy-start | bytes 964
  (6 other events, 7.1 us)

commit v8 on v7

--- a/solution.py
+++ b/solution.py
@@ -279,11 +279,48 @@
     return weights, jnp.stack([high, low]).astype(jnp.bfloat16)
 
 
-def halo(first, last, axis):
-    count = lax.axis_size(axis)
-    forward = [(i, (i + 1) % count) for i in range(count)]
-    backward = [(target, source) for source, target in forward]
-    return lax.ppermute(last, axis, forward), lax.ppermute(first, axis, backward)
+def halo_kernel(count_x, count_y, first_plane, last_plane, first_row, last_row, west, east, south, north, send, recv):
+    gx, gy = lax.axis_index("gx"), lax.axis_index("gy")
+    ahead_x, behind_x = lax.rem(gx + 1, count_x), lax.rem(gx + count_x - 1, count_x)
+    ahead_y, behind_y = lax.rem(gy + 1, count_y), lax.rem(gy + count_y - 1, count_y)
+    peers = [(ahead_x, gy), (behind_x, gy), (gx, ahead_y)]
+    if count_y > 2:
+        peers.append((gx, behind_y))
+    barrier = pltpu.get_barrier_semaphore()
+    for peer in peers:
+        pl.semaphore_signal(barrier, inc=1, device_id=peer, device_id_type=MESH)
+    pl.semaphore_wait(barrier, len(peers))
+    routes = [
+        (last_plane, west, (ahead_x, gy)),
+        (first_plane, east, (behind_x, gy)),
+        (last_row, south, (gx, ahead_y)),
+        (first_row, north, (gx, behind_y)),
+    ]
+    copies = []
+    for index, (source, target, peer) in enumerate(routes):
+        copy = pltpu.make_async_remote_copy(
+            src_ref=source, dst_ref=target, send_sem=send.at[index], recv_sem=recv.at[index],
+            device_id=peer, device_id_type=MESH,
+        )
+        copy.start()
+        copies.append(copy)
+    for copy in copies:
+        copy.wait()
+
+
+def halos(edges, call):
+    (first_plane, last_plane), (first_row, last_row) = edges
+    vmem = pl.BlockSpec(memory_space=pltpu.VMEM)
+    planes = jax.ShapeDtypeStruct(first_plane.shape, jnp.float32)
+    rows = jax.ShapeDtypeStruct(first_row.shape, jnp.float32)
+    return pl.pallas_call(
+        functools.partial(halo_kernel, lax.axis_size("gx"), lax.axis_size("gy")),
+        out_shape=(planes, planes, rows, rows),
+        in_specs=[vmem] * 4,
+        out_specs=(vmem,) * 4,
+        scratch_shapes=[pltpu.SemaphoreType.DMA((4,)), pltpu.SemaphoreType.DMA((4,))],
+        compiler_params=pltpu.CompilerParams(collective_id=1 + call, has_side_effects=True),
+    )(first_plane, last_plane, first_row, last_row)
 
 
 def shards(
@@ -339,8 +376,7 @@
             "jsr,scrb->cjb", pick_table, arrived, preferred_element_type=jnp.float32
         ).astype(jnp.bfloat16)
         forward = forward.reshape(components, width_x, width_y, height)
-        west, east = halo(*edges[0], "gx")
-        south, north = halo(*edges[1], "gy")
+        west, east, south, north = halos(edges, step_index)
         adjoint, gradient_block, first_plane, last_plane, first_row, last_row = advance(
             adjoint, west, east, south, north, forward, block_columns, eddy_blocks, drag_field, fringe_scale,
             turbine, gradient_block, step_index == steps_total - 1,

time: 146 us -> 205 us (1.40)
  Pallas kernels: 39.1 us -> 91.7 us
  local copies, waits for them, and re-layouts: 28.5 us -> 41.6 us
  starting transfers between devices: 29.1 us -> 17 us
  matrix products: 10.7 us -> 13.7 us
  waiting for transfers between devices: 31 us -> 34 us
    pallas_call x0 -> x2, Pallas kernels: none -> 52.3 us  [halos(): pl.pallas_call(functools.partial(halo_kernel, lax.axis_size('gx'), lax.ax...]
    ppermute x8 -> x0, starting transfers between devices: 11.1 us -> none  [the longest x4 8.01 us: halo(): lax.ppermute(last, axis, forward)]
    unnamed x42 -> x62, local copies, waits for them, and re-layouts: 6.64 us -> 17.5 us
    all_to_all x2, waiting for transfers between devices: 31 us -> 34 us  [shards(): lax.all_to_all(packed, ('gx', 'gy'), split_axis=0, concat_axis=0, tiled=T...]
    dot_general x2, matrix products: 4.8 us -> 7.81 us  [shards(): jnp.einsum('jsr,scrb->cjb', pick_table, arrived, preferred_element_type=j...]
  transfers between devices with their start and end apart: 10 -> 2, of which waited for: 2 -> 1; matrix products, arithmetic and copies ran while one was open for 19% -> 11% of each run, Pallas kernels for 13% -> 20%
where the time goes in v8:
time: 205 us; the launch traced here: 204 us
  Pallas kernels  91.7 us (45%)
  local copies, waits for them, and re-layouts  41.6 us (20%)
  waiting for transfers between devices  34 us (17%)
  starting transfers between devices  17 us (8%)
  matrix products  13.7 us (7%)
  other arithmetic  5.3 us (3%)
    pallas_call x2, Pallas kernels, halos(): pl.pallas_call(functools.partial(halo_kernel, lax.axis_size('gx'), lax.ax...  52.3 us
    pallas_call x2, Pallas kernels, advance(): pl.pallas_call(functools.partial(advance_kernel, count_y, group, exchange...  39.4 us
    all_to_all x2, waiting for transfers between devices, shards(): lax.all_to_all(packed, ('gx', 'gy'), split_axis=0, concat_axis=0, tiled=T...  34 us
    unnamed x62, local copies, waits for them, and re-layouts  17.5 us
    all_to_all x2, starting transfers between devices, shards(): lax.all_to_all(packed, ('gx', 'gy'), split_axis=0, concat_axis=0, tiled=T...  17 us
    convert_element_type x2, local copies, waits for them, and re-layouts, shards(): packed = jnp.einsum('drs,scb->dcrb', pack_table, stored, preferred_elemen...  9.77 us
    dot_general x2, matrix products, shards(): jnp.einsum('jsr,scrb->cjb', pick_table, arrived, preferred_element_type=j...  7.81 us
    reshape x2, local copies, waits for them, and re-layouts, shards(): forward = forward.reshape(components, width_x, width_y, height)  6.32 us
  transfers between devices with their start and end apart: 2, of which 1 were waited for; matrix products, arithmetic and copies ran while one was open for 11% of the time, Pallas kernels for 20%

profile of v8, /device:TPU:1, one launch (start us, length us, event | category | flops | bytes accessed | tf_op | source)
XLA Modules:
  0.0 204.2 jit_solution(16511659700241989031)
XLA Ops:
  3.1 2.4 %fusion.5 = bf16[128,3,2,2048]{3,0,1,2:T(8,128)(2,1)S(1)} fusion(bf16[2,128,3,2048]{3,1,2,0:T(8,128)(2,1)} %param.16, s32[128]{0:T(128)S(1)} %add_add_fusion, s32[128,2]{0,1:T(2,128)S(1)} %multiply_add_fusion), kind=kOutput, calls=%fused_computation.9 | convolution fusion | flops 404258816 | bytes 4720128 | tf_op jit(solution)/shard_map/drs,scb->dcrb/dot_general | solution.py:371
  5.5 4.9 %copy.29 = bf16[128,3,2,2048]{3,2,1,0:T(2,128)(2,1)} copy(bf16[128,3,2,2048]{3,0,1,2:T(8,128)(2,1)S(1)} %fusion.5) | data formatting | bytes 6291456 | tf_op jit(solution)/shard_map/convert_element_type | solution.py:373
  10.4 11.5 %all-to-all-start.1 = ((bf16[128,3,2,2048]{3,2,1,0:T(2,128)(2,1)}), bf16[128,3,2,2048]{3,2,1,0:T(2,128)(2,1)S(1)}, u32[]{:S(2)}, u32[]{:S(2)}) async-start(bf16[128,3,2,2048]{3,2,1,0:T(2,128)(2,1)} %copy.29), calls=%async_computation.1 | async-start | bytes 6291456 | tf_op jit(solution)/shard_map/all_to_all | solution.py:374
  22.0 2.4 %fusion.4 = bf16[128,3,2,2048]{3,0,1,2:T(8,128)(2,1)S(1)} fusion(bf16[2,128,3,2048]{3,1,2,0:T(8,128)(2,1)} %param.16, s32[128]{0:T(128)S(1)} %add_add_fusion, s32[128,2]{0,1:T(2,128)S(1)} %multiply_add_fusion), kind=kOutput, calls=%fused_computation.8 | convolution fusion | flops 404258816 | bytes 4720128 | tf_op jit(solution)/shard_map/drs,scb->dcrb/dot_general | solution.py:371
  24.5 4.9 %copy.25 = bf16[128,3,2,2048]{3,2,1,0:T(2,128)(2,1)} copy(bf16[128,3,2,2048]{3,0,1,2:T(8,128)(2,1)S(1)} %fusion.4) | data formatting | bytes 6291456 | tf_op jit(solution)/shard_map/convert_element_type | solution.py:373
  29.4 34.0 %all-to-all-done.1 = bf16[128,3,2,2048]{3,2,1,0:T(2,128)(2,1)S(1)} async-done(((bf16[128,3,2,2048]{3,2,1,0:T(2,128)(2,1)}), bf16[128,3,2,2048]{3,2,1,0:T(2,128)(2,1)S(1)}, u32[]{:S(2)}, u32[]{:S(2)}) %all-to-all-start.1) | async-done | bytes 3145760 | tf_op jit(solution)/shard_map/all_to_all | solution.py:374
  63.4 5.5 %all-to-all-start = ((bf16[128,3,2,2048]{3,2,1,0:T(2,128)(2,1)}), bf16[128,3,2,2048]{3,2,1,0:T(2,128)(2,1)}, u32[]{:S(2)}, u32[]{:S(2)}) async-start(bf16[128,3,2,2048]{3,2,1,0:T(2,128)(2,1)} %copy.25), calls=%async_computation | async-start | bytes 6291456 | tf_op jit(solution)/shard_map/all_to_all | solution.py:374
  69.2 1.8 fusion.54
  71.0 1.8 fusion.55
  72.8 41.6 %shard_map.122 = (f32[3,1,64,256]{3,2,1,0:T(8,128)}, f32[3,1,64,256]{3,2,1,0:T(8,128)}, f32[3,16,1,256]{3,2,1,0:T(1,128)}, f32[3,16,1,256]{3,2,1,0:T(1,128)}) custom-call(f32[3,1,64,256]{3,2,1,0:T(8,128)} %get-tuple-element.61.first_plane, f32[3,1,64,256]{3,2,1,0:T(8,128)} %get-tuple-element.60.last_plane, f32[3,16,1,256]{3,2,1,0:T(1,128)} %get-tuple-element.59.first_row, ...), custom_call_target="tpu_custom_call" | custom-call | tf_op jit(solution)/shard_map/pallas_call | solution.py:316
  116.5 1.0 fusion.29.refs_8_
  117.6 3.3 %fusion.13 = bf16[3,128,2048]{1,2,0:T(8,128)(2,1)S(1)} fusion(bf16[128,3,2,2048]{3,2,1,0:T(2,128)(2,1)} %copy-done.18, s32[128,2]{0,1:T(2,128)S(1)} %multiply_add_fusion, s32[128]{0:T(128)S(1)} %copy-done.29), kind=kOutput, calls=%fused_computation.11 | convolution fusion | flops 403472384 | bytes 4720128 | tf_op jit(solution)/shard_map/jsr,scrb->cjb/dot_general | solution.py:375
  120.9 1.6 copy.31
  122.5 2.6 %reshape.198.refs_7_ = bf16[3,16,64,256]{3,2,1,0:T(8,128)(2,1)S(1)} reshape(bf16[3,128,2048]{2,1,0:T(8,128)(2,1)} %copy.31) | data formatting | bytes 3145728 | tf_op jit(solution)/shard_map/reshape | solution.py:378
  125.1 4.5 %fusion.10 = bf16[3,128,2048]{1,2,0:T(8,128)(2,1)} fusion(bf16[128,3,2,2048]{3,2,1,0:T(2,128)(2,1)} %all-to-all-done, s32[128,2]{0,1:T(2,128)S(1)} %multiply_add_fusion, s32[128]{0:T(128)S(1)} %copy-done.29), kind=kOutput, calls=%fused_computation.10 | convolution fusion | flops 403472384 | bytes 4720128 | tf_op jit(solution)/shard_map/jsr,scrb->cjb/dot_general | solution.py:375
  129.6 2.6 %copy.27 = bf16[3,128,2048]{2,1,0:T(8,128)(2,1)} copy(bf16[3,128,2048]{1,2,0:T(8,128)(2,1)} %fusion.10) | data formatting | bytes 3145728 | tf_op jit(solution)/shard_map/convert_element_type | solution.py:377
  132.3 3.7 %reshape.195.refs_7_ = bf16[3,16,64,256]{3,2,1,0:T(8,128)(2,1)} reshape(bf16[3,128,2048]{2,1,0:T(8,128)(2,1)} %copy.27) | data formatting | bytes 3145728 | tf_op jit(solution)/shard_map/reshape | solution.py:378
  136.0 1.4 copy-done
  137.4 0.9 copy-done.4
  138.3 0.9 copy-done.5
  141.5 18.7 %shard_map.123 = (f32[3,16,64,256]{3,2,1,0:T(8,128)}, f32[8,128]{1,0:T(8,128)S(1)}, f32[3,1,64,256]{3,2,1,0:T(8,128)S(1)}, f32[3,1,64,256]{3,2,1,0:T(8,128)S(1)}...) custom-call(s32[32,8]{1,0:T(8,128)S(1)} %copy.32.refs_0_, f32[16]{0:T(128)S(1)} %copy-done.16, ...), custom_call_target="tpu_custom_call" | custom-call | tf_op jit(solution)/shard_map/pallas_call | solution.py:261
  163.4 10.7 %shard_map.124 = (f32[3,1,64,256]{3,2,1,0:T(8,128)}, f32[3,1,64,256]{3,2,1,0:T(8,128)}, f32[3,16,1,256]{3,2,1,0:T(1,128)}, f32[3,16,1,256]{3,2,1,0:T(1,128)}) custom-call(f32[3,1,64,256]{3,2,1,0:T(8,128)} %copy-done.2, f32[3,1,64,256]{3,2,1,0:T(8,128)} %copy-done.3, f32[3,16,1,256]{3,2,1,0:T(1,128)} %copy-done.12, f32[3,16,1,256]{3,2,1,0:T(1,128)} %copy-done.13), custom_call_target="tpu_custom_call" | custom-call | tf_op jit(solution)/shard_map/pallas_call | solution.py:316
  179.0 20.6 %shard_map.125 = (f32[3,16,64,256]{3,2,1,0:T(8,128)}, f32[8,128]{1,0:T(8,128)S(1)}, f32[3,1,64,256]{3,2,1,0:T(8,128)}, f32[3,1,64,256]{3,2,1,0:T(8,128)}, f32[3,...) custom-call(s32[32,8]{1,0:T(8,128)S(1)} %copy.32.refs_0_, f32[16]{0:T(128)S(1)} %copy-done.17, ...), custom_call_target="tpu_custom_call" | custom-call | tf_op jit(solution)/shard_map/pallas_call | solution.py:261
  200.3 3.9 %copy.49 = f32[3,16,64,256]{3,2,1,0:T(8,128)} copy(f32[3,16,64,256]{3,2,1,0:T(8,128)} %get-tuple-element.73) | data formatting | bytes 6291456
  (83 shorter events, 15.7 us)
Async XLA Ops:
  10.3 11.5 %copy-start.26 = (f32[80]{0:T(128)S(1)}, f32[80]{0:T(128)}, u32[]{:S(2)}) copy-start(f32[80]{0:T(128)} %param.22) | copy-start | bytes 964
  10.3 11.6 %copy-start.19 = (s32[32,8]{0,1:T(8,128)S(1)}, s32[32,8]{0,1:T(8,128)}, u32[]{:S(2)}) copy-start(s32[32,8]{0,1:T(8,128)} %param.19) | copy-start | bytes 3076
  10.4 53.0 %all-to-all-start.1 = ((bf16[128,3,2,2048]{3,2,1,0:T(2,128)(2,1)}), bf16[128,3,2,2048]{3,2,1,0:T(2,128)(2,1)S(1)}, u32[]{:S(2)}, u32[]{:S(2)}) async-start(bf16[128,3,2,2048]{3,2,1,0:T(2,128)(2,1)} %copy.29), calls=%async_computation.1 | async-start | bytes 6291456 | tf_op jit(solution)/shard_map/all_to_all | solution.py:374
  21.9 7.4 %copy-start.22 = (f32[80]{0:T(128)}, f32[80]{0:T(128)S(1)}, u32[]{:S(2)}) copy-start(f32[80]{0:T(128)S(1)} %cos.4) | copy-start | bytes 964
  24.4 4.9 %copy-start.20 = (f32[80]{0:T(128)S(1)}, f32[80]{0:T(128)}, u32[]{:S(2)}) copy-start(f32[80]{0:T(128)} %param.21) | copy-start | bytes 964
  24.4 4.9 %copy-start.25 = (s32[80]{0:T(128)S(1)}, s32[80]{0:T(128)}, u32[]{:S(2)}) copy-start(s32[80]{0:T(128)} %param.24) | copy-start | bytes 964
  24.5 4.9 %copy-start.24 = (f32[3,80]{1,0:T(4,128)S(1)}, f32[3,80]{1,0:T(4,128)}, u32[]{:S(2)}) copy-start(f32[3,80]{1,0:T(4,128)} %param.23) | copy-start | bytes 2884
  63.4 5.6 %copy-start.18 = (bf16[128,3,2,2048]{3,2,1,0:T(2,128)(2,1)}, bf16[128,3,2,2048]{3,2,1,0:T(2,128)(2,1)S(1)}, u32[]{:S(2)}) copy-start(bf16[128,3,2,2048]{3,2,1,0:T(2,128)(2,1)S(1)} %all-to-all-done.1) | copy-start | bytes 9437188
  63.4 61.7 %all-to-all-start = ((bf16[128,3,2,2048]{3,2,1,0:T(2,128)(2,1)}), bf16[128,3,2,2048]{3,2,1,0:T(2,128)(2,1)}, u32[]{:S(2)}, u32[]{:S(2)}) async-start(bf16[128,3,2,2048]{3,2,1,0:T(2,128)(2,1)} %copy.25), calls=%async_computation | async-start | bytes 6291456 | tf_op jit(solution)/shard_map/all_to_all | solution.py:374
  68.9 46.1 %copy-start.28 = (s32[128]{0:T(128)S(1)}, s32[128]{0:T(128)}, u32[]{:S(2)}) copy-start(s32[128]{0:T(128)} %param.25) | copy-start | bytes 1540
  69.1 48.5 %copy-start.29 = (s32[128]{0:T(128)S(1)}, s32[128]{0:T(128)}, u32[]{:S(2)}) copy-start(s32[128]{0:T(128)} %param.18) | copy-start | bytes 1540
  129.6 6.4 %copy-start.1 = (bf16[8,128,128]{2,1,0:T(8,128)(2,1)S(1)}, bf16[8,128,128]{2,1,0:T(8,128)(2,1)}, u32[]{:S(2)}) copy-start(bf16[8,128,128]{2,1,0:T(8,128)(2,1)} %param.20) | copy-start | bytes 786436
  136.0 1.4 copy-start
  137.4 0.9 copy-start.4
  138.3 0.9 copy-start.5
  139.3 0.8 copy-start.8
  140.1 0.8 copy-start.9
  174.2 0.9 copy-start.6
  175.1 0.9 copy-start.7
  176.0 0.8 copy-start.10
  176.8 0.8 copy-start.11
  178.9 20.7 %copy-start.21 = (f32[80]{0:T(128)S(1)}, f32[80]{0:T(128)}, u32[]{:S(2)}) copy-start(f32[80]{0:T(128)} %param.21) | copy-start | bytes 964
  178.9 20.7 %copy-start.23 = (f32[80]{0:T(128)S(1)}, f32[80]{0:T(128)}, u32[]{:S(2)}) copy-start(f32[80]{0:T(128)} %copy-done.22) | copy-start | bytes 964
  179.0 20.7 %copy-start.27 = (f32[80]{0:T(128)S(1)}, f32[80]{0:T(128)}, u32[]{:S(2)}) copy-start(f32[80]{0:T(128)} %param.22) | copy-start | bytes 964
  (8 other events, 5.2 us)

commit v9 on v7

--- a/solution.py
+++ b/solution.py
@@ -109,6 +109,19 @@
     acc = lax.fori_loop(0, width_x, turbine_plane, jnp.zeros(pk_ref.shape[1:], jnp.float32))
     leading_row = lax.broadcasted_iota(jnp.int32, prior_ref.shape, 0) == 0
     part = prior_ref[...] + jnp.where(leading_row, jnp.sum(acc, axis=0, keepdims=True), 0.0)
+    half = height // NZB
+
+    def fill_plane(x, carry):
+        for zb in range(NZB):
+            for c in range(components):
+                xq[2 * (x + 1) + zb, c * width_y : (c + 1) * width_y, :] = a_ref[c, x, :, zb * half : (zb + 1) * half].astype(jnp.bfloat16)
+        return carry
+
+    for zb in range(NZB):
+        for c in range(components):
+            xq[zb, c * width_y : (c + 1) * width_y, :] = w_ref[c, 0, :, zb * half : (zb + 1) * half].astype(jnp.bfloat16)
+            xq[2 * (width_x + 1) + zb, c * width_y : (c + 1) * width_y, :] = e_ref[c, 0, :, zb * half : (zb + 1) * half].astype(jnp.bfloat16)
+    lax.fori_loop(0, width_x, fill_plane, 0)
     if exchange:
         pl.semaphore_wait(barrier, group + groups - 2)
         near[mine] = part
@@ -123,20 +136,6 @@
         lax.fori_loop(1, group, send_near, 0)
     else:
         sum_ref[...] = part
-
-    half = height // NZB
-
-    def fill_plane(x, carry):
-        for zb in range(NZB):
-            for c in range(components):
-                xq[2 * (x + 1) + zb, c * width_y : (c + 1) * width_y, :] = a_ref[c, x, :, zb * half : (zb + 1) * half].astype(jnp.bfloat16)
-        return carry
-
-    for zb in range(NZB):
-        for c in range(components):
-            xq[zb, c * width_y : (c + 1) * width_y, :] = w_ref[c, 0, :, zb * half : (zb + 1) * half].astype(jnp.bfloat16)
-            xq[2 * (width_x + 1) + zb, c * width_y : (c + 1) * width_y, :] = e_ref[c, 0, :, zb * half : (zb + 1) * half].astype(jnp.bfloat16)
-    lax.fori_loop(0, width_x, fill_plane, 0)
 
     def eddy_block(p, carry):
         acc = jnp.zeros((components * width_y, half), jnp.float32)

time: 146 us -> 145 us (level)
  no operation moved by 1% of the time
where the time goes in v9:
time: 145 us
  Pallas kernels  39.1 us (27%)
  waiting for transfers between devices  31 us (21%)
  starting transfers between devices  29.1 us (20%)
  local copies, waits for them, and re-layouts  28.5 us (20%)
  matrix products  10.7 us (7%)
  other arithmetic  5.35 us (4%)
    pallas_call x2, Pallas kernels, advance(): pl.pallas_call(functools.partial(advance_kernel, count_y, group, exchange...  39.1 us
    all_to_all x2, waiting for transfers between devices, shards(): lax.all_to_all(packed, ('gx', 'gy'), split_axis=0, concat_axis=0, tiled=T...  31 us
    all_to_all x2, starting transfers between devices, shards(): lax.all_to_all(packed, ('gx', 'gy'), split_axis=0, concat_axis=0, tiled=T...  18 us
    convert_element_type x2, local copies, waits for them, and re-layouts, shards(): packed = jnp.einsum('drs,scb->dcrb', pack_table, stored, preferred_elemen...  9.8 us
    ppermute x4, starting transfers between devices, halo(): lax.ppermute(last, axis, forward)  8.01 us
    unnamed x42, local copies, waits for them, and re-layouts  6.64 us
    reshape x2, local copies, waits for them, and re-layouts, shards(): forward = forward.reshape(components, width_x, width_y, height)  5.16 us
    dot_general x2, matrix products, shards(): jnp.einsum('drs,scb->dcrb', pack_table, stored, preferred_element_type=jn...  4.84 us
  transfers between devices with their start and end apart: 10, of which 2 were waited for; matrix products, arithmetic and copies ran while one was open for 19% of the time, Pallas kernels for 13%

profile of v9, /device:TPU:1, one launch (start us, length us, event | category | flops | bytes accessed | tf_op | source)
XLA Modules:
  0.0 144.7 jit_solution(8884017804536395674)
XLA Ops:
  3.1 2.4 %fusion.4 = bf16[128,3,2,2048]{3,0,1,2:T(8,128)(2,1)S(1)} fusion(bf16[2,128,3,2048]{3,1,2,0:T(8,128)(2,1)} %param.16, s32[128]{0:T(128)S(1)} %add_add_fusion, s32[128,2]{0,1:T(2,128)S(1)} %multiply_add_fusion), kind=kOutput, calls=%fused_computation.8 | convolution fusion | flops 404258816 | bytes 4720128 | tf_op jit(solution)/shard_map/drs,scb->dcrb/dot_general | solution.py:333
  5.5 4.9 %copy.25 = bf16[128,3,2,2048]{3,2,1,0:T(2,128)(2,1)} copy(bf16[128,3,2,2048]{3,0,1,2:T(8,128)(2,1)S(1)} %fusion.4) | data formatting | bytes 6291456 | tf_op jit(solution)/shard_map/convert_element_type | solution.py:335
  10.4 11.5 %all-to-all-start = ((bf16[128,3,2,2048]{3,2,1,0:T(2,128)(2,1)}), bf16[128,3,2,2048]{3,2,1,0:T(2,128)(2,1)S(1)}, u32[]{:S(2)}, u32[]{:S(2)}) async-start(bf16[128,3,2,2048]{3,2,1,0:T(2,128)(2,1)} %copy.25), calls=%async_computation | async-start | bytes 6291456 | tf_op jit(solution)/shard_map/all_to_all | solution.py:336
  21.9 1.8 %fusion.54 = (f32[3,16,1,256]{3,2,1,0:T(1,128)}, f32[3,16,1,256]{3,2,1,0:T(1,128)}) fusion(f32[3,16,64,256]{3,2,1,0:T(8,128)} %refs_2_.1), kind=kLoop, calls=%fused_computation.76 | loop fusion | bytes 196608 | tf_op jit(solution)/shard_map/slice | solution.py:329
  23.7 1.5 %collective-permute-start.3 = (f32[3,16,1,256]{3,2,1,0:T(1,128)}, f32[3,16,1,256]{3,2,1,0:T(1,128)}, u32[]{:S(2)}, u32[]{:S(2)}) collective-permute-start(f32[3,16,1,256]{3,2,1,0:T(1,128)} %get-tuple-element.42), channel_id=1, source_target_pairs={{1,0},{0,1},{3,2},{2,3},{5,4},{4,5},{7,6},{6,7},{9,8},{8,9},{11,10... | collective-permute-start | bytes 147464 | tf_op jit(solution)/shard_map/ppermute | solution.py:285
  25.3 1.8 %fusion.55 = (f32[3,1,64,256]{3,2,1,0:T(8,128)}, f32[3,1,64,256]{3,2,1,0:T(8,128)}) fusion(f32[3,16,64,256]{3,2,1,0:T(8,128)} %refs_2_.1), kind=kLoop, calls=%fused_computation.77 | loop fusion | bytes 786432 | tf_op jit(solution)/shard_map/slice | solution.py:328
  27.1 1.6 %collective-permute-start.1 = (f32[3,1,64,256]{3,2,1,0:T(8,128)}, f32[3,1,64,256]{3,2,1,0:T(8,128)}, u32[]{:S(2)}, u32[]{:S(2)}) collective-permute-start(f32[3,1,64,256]{3,2,1,0:T(8,128)} %get-tuple-element.44), channel_id=1, source_target_pairs={{2,0},{4,2},{6,4},{8,6},{10,8},{12,10},{14,12},{16,14},{18,16},{20... | collective-permute-start | bytes 589832 | tf_op jit(solution)/shard_map/ppermute | solution.py:285
  28.6 2.5 %collective-permute-start = (f32[3,1,64,256]{3,2,1,0:T(8,128)}, f32[3,1,64,256]{3,2,1,0:T(8,128)}, u32[]{:S(2)}, u32[]{:S(2)}) collective-permute-start(f32[3,1,64,256]{3,2,1,0:T(8,128)} %get-tuple-element.45), channel_id=1, source_target_pairs={{0,2},{2,4},{4,6},{6,8},{8,10},{10,12},{12,14},{14,16},{16,18},{18... | collective-permute-start | bytes 589832 | tf_op jit(solution)/shard_map/ppermute | solution.py:285
  31.2 2.4 %fusion.5 = bf16[128,3,2,2048]{3,0,1,2:T(8,128)(2,1)S(1)} fusion(bf16[2,128,3,2048]{3,1,2,0:T(8,128)(2,1)} %param.16, s32[128]{0:T(128)S(1)} %add_add_fusion, s32[128,2]{0,1:T(2,128)S(1)} %multiply_add_fusion), kind=kOutput, calls=%fused_computation.9 | convolution fusion | flops 404258816 | bytes 4720128 | tf_op jit(solution)/shard_map/drs,scb->dcrb/dot_general | solution.py:333
  33.7 4.9 %copy.29 = bf16[128,3,2,2048]{3,2,1,0:T(2,128)(2,1)} copy(bf16[128,3,2,2048]{3,0,1,2:T(8,128)(2,1)S(1)} %fusion.5) | data formatting | bytes 6291456 | tf_op jit(solution)/shard_map/convert_element_type | solution.py:335
  38.6 24.9 %all-to-all-done = bf16[128,3,2,2048]{3,2,1,0:T(2,128)(2,1)S(1)} async-done(((bf16[128,3,2,2048]{3,2,1,0:T(2,128)(2,1)}), bf16[128,3,2,2048]{3,2,1,0:T(2,128)(2,1)S(1)}, u32[]{:S(2)}, u32[]{:S(2)}) %all-to-all-start) | async-done | bytes 3145760 | tf_op jit(solution)/shard_map/all_to_all | solution.py:336
  63.4 6.5 %all-to-all-start.1 = ((bf16[128,3,2,2048]{3,2,1,0:T(2,128)(2,1)}), bf16[128,3,2,2048]{3,2,1,0:T(2,128)(2,1)}, u32[]{:S(2)}, u32[]{:S(2)}) async-start(bf16[128,3,2,2048]{3,2,1,0:T(2,128)(2,1)} %copy.29), calls=%async_computation.1 | async-start | bytes 6291456 | tf_op jit(solution)/shard_map/all_to_all | solution.py:336
  73.5 1.5 %fusion.10 = bf16[3,128,2048]{1,2,0:T(8,128)(2,1)S(1)} fusion(bf16[128,3,2,2048]{3,2,1,0:T(2,128)(2,1)S(1)} %copy-done.6, s32[128,2]{0,1:T(2,128)S(1)} %copy-done.8, s32[128]{0:T(128)S(1)} %copy-done.19), kind=kOutput, calls=%fused_computation.10 | convolution fusion | flops 403472384 | bytes 4720128 | tf_op jit(solution)/shard_map/jsr,scrb->cjb/dot_general | solution.py:337
  75.0 1.6 %copy.27 = bf16[3,128,2048]{2,1,0:T(8,128)(2,1)} copy(bf16[3,128,2048]{1,2,0:T(8,128)(2,1)S(1)} %fusion.10) | data formatting | bytes 3145728 | tf_op jit(solution)/shard_map/convert_element_type | solution.py:339
  76.6 2.6 %reshape.195.refs_7_ = bf16[3,16,64,256]{3,2,1,0:T(8,128)(2,1)S(1)} reshape(bf16[3,128,2048]{2,1,0:T(8,128)(2,1)} %copy.27) | data formatting | bytes 3145728 | tf_op jit(solution)/shard_map/reshape | solution.py:340
  79.9 19.0 %shard_map.122 = (f32[3,16,64,256]{3,2,1,0:T(8,128)}, f32[8,128]{1,0:T(8,128)S(1)}, f32[3,1,64,256]{3,2,1,0:T(8,128)}, f32[3,1,64,256]{3,2,1,0:T(8,128)}, f32[3,...) custom-call(s32[32,8]{1,0:T(8,128)S(1)} %copy.32.refs_0_, f32[16]{0:T(128)S(1)} %copy-done.3, f32[3,16,64,256]{3,2,1,0:T(8,128)} %refs_2_.1, ...), custom_call_target="tpu_custom_call" | custom-call | tf_op jit(solution)/shard_map/pallas_call | solution.py:260
  99.5 1.5 %collective-permute-start.6 = (f32[3,16,1,256]{3,2,1,0:T(1,128)}, f32[3,16,1,256]{3,2,1,0:T(1,128)}, u32[]{:S(2)}, u32[]{:S(2)}) collective-permute-start(f32[3,16,1,256]{3,2,1,0:T(1,128)} %get-tuple-element.37), channel_id=1, source_target_pairs={{0,1},{1,0},{2,3},{3,2},{4,5},{5,4},{6,7},{7,6},{8,9},{9,8},{10,11... | collective-permute-start | bytes 147464 | tf_op jit(solution)/shard_map/ppermute | solution.py:285
  101.0 4.0 %collective-permute-start.4 = (f32[3,1,64,256]{3,2,1,0:T(8,128)}, f32[3,1,64,256]{3,2,1,0:T(8,128)}, u32[]{:S(2)}, u32[]{:S(2)}) collective-permute-start(f32[3,1,64,256]{3,2,1,0:T(8,128)} %get-tuple-element.35), channel_id=1, source_target_pairs={{0,2},{2,4},{4,6},{6,8},{8,10},{10,12},{12,14},{14,16},{16,18},{18... | collective-permute-start | bytes 589832 | tf_op jit(solution)/shard_map/ppermute | solution.py:285
  105.0 6.1 %all-to-all-done.1 = bf16[128,3,2,2048]{3,2,1,0:T(2,128)(2,1)} async-done(((bf16[128,3,2,2048]{3,2,1,0:T(2,128)(2,1)}), bf16[128,3,2,2048]{3,2,1,0:T(2,128)(2,1)}, u32[]{:S(2)}, u32[]{:S(2)}) %all-to-all-start.1) | async-done | bytes 3145760 | tf_op jit(solution)/shard_map/all_to_all | solution.py:336
  111.1 3.3 %fusion.13 = bf16[3,128,2048]{1,2,0:T(8,128)(2,1)S(1)} fusion(bf16[128,3,2,2048]{3,2,1,0:T(2,128)(2,1)} %all-to-all-done.1, s32[128,2]{0,1:T(2,128)} %copy-done.7, s32[128]{0:T(128)} %param.18), kind=kOutput, calls=%fused_computation.11 | convolution fusion | flops 403472384 | bytes 4720128 | tf_op jit(solution)/shard_map/jsr,scrb->cjb/dot_general | solution.py:337
  114.5 1.6 %copy.31 = bf16[3,128,2048]{2,1,0:T(8,128)(2,1)} copy(bf16[3,128,2048]{1,2,0:T(8,128)(2,1)S(1)} %fusion.13) | data formatting | bytes 3145728 | tf_op jit(solution)/shard_map/convert_element_type | solution.py:339
  116.1 2.6 %reshape.198.refs_7_ = bf16[3,16,64,256]{3,2,1,0:T(8,128)(2,1)S(1)} reshape(bf16[3,128,2048]{2,1,0:T(8,128)(2,1)} %copy.31) | data formatting | bytes 3145728 | tf_op jit(solution)/shard_map/reshape | solution.py:340
  120.1 20.1 %shard_map.123 = (f32[3,16,64,256]{3,2,1,0:T(8,128)}, f32[8,128]{1,0:T(8,128)S(1)}, f32[3,1,64,256]{3,2,1,0:T(8,128)}, f32[3,1,64,256]{3,2,1,0:T(8,128)}, f32[3,...) custom-call(s32[32,8]{1,0:T(8,128)S(1)} %copy.32.refs_0_, f32[16]{0:T(128)S(1)} %copy-done.4, ...), custom_call_target="tpu_custom_call" | custom-call | tf_op jit(solution)/shard_map/pallas_call | solution.py:260
  140.8 3.9 %copy.49 = f32[3,16,64,256]{3,2,1,0:T(8,128)} copy(f32[3,16,64,256]{3,2,1,0:T(8,128)} %get-tuple-element.57) | data formatting | bytes 6291456
  (77 shorter events, 9.3 us)
Async XLA Ops:
  0.6 30.6 %copy-start.7 = (s32[128,2]{0,1:T(2,128)}, s32[128,2]{0,1:T(2,128)S(1)}, u32[]{:S(2)}) copy-start(s32[128,2]{0,1:T(2,128)S(1)} %multiply_add_fusion) | copy-start | bytes 3076
  10.4 20.7 %copy-start.16 = (f32[80]{0:T(128)S(1)}, f32[80]{0:T(128)}, u32[]{:S(2)}) copy-start(f32[80]{0:T(128)} %param.22) | copy-start | bytes 964
  10.4 20.8 %copy-start.9 = (s32[32,8]{0,1:T(8,128)S(1)}, s32[32,8]{0,1:T(8,128)}, u32[]{:S(2)}) copy-start(s32[32,8]{0,1:T(8,128)} %param.19) | copy-start | bytes 3076
  10.4 53.0 %all-to-all-start = ((bf16[128,3,2,2048]{3,2,1,0:T(2,128)(2,1)}), bf16[128,3,2,2048]{3,2,1,0:T(2,128)(2,1)S(1)}, u32[]{:S(2)}, u32[]{:S(2)}) async-start(bf16[128,3,2,2048]{3,2,1,0:T(2,128)(2,1)} %copy.25), calls=%async_computation | async-start | bytes 6291456 | tf_op jit(solution)/shard_map/all_to_all | solution.py:336
  23.7 55.4 %collective-permute-start.3 = (f32[3,16,1,256]{3,2,1,0:T(1,128)}, f32[3,16,1,256]{3,2,1,0:T(1,128)}, u32[]{:S(2)}, u32[]{:S(2)}) collective-permute-start(f32[3,16,1,256]{3,2,1,0:T(1,128)} %get-tuple-element.42), channel_id=1, source_target_pairs={{1,0},{0,1},{3,2},{2,3},{5,4},{4,5},{7,6},{6,7},{9,8},{8,9},{11,10... | collective-permute-start | bytes 147464 | tf_op jit(solution)/shard_map/ppermute | solution.py:285
  25.2 53.9 %collective-permute-start.2 = (f32[3,16,1,256]{3,2,1,0:T(1,128)}, f32[3,16,1,256]{3,2,1,0:T(1,128)}, u32[]{:S(2)}, u32[]{:S(2)}) collective-permute-start(f32[3,16,1,256]{3,2,1,0:T(1,128)} %get-tuple-element.43), channel_id=1, source_target_pairs={{0,1},{1,0},{2,3},{3,2},{4,5},{5,4},{6,7},{7,6},{8,9},{9,8},{10,11... | collective-permute-start | bytes 147464 | tf_op jit(solution)/shard_map/ppermute | solution.py:285
  27.1 52.1 %collective-permute-start.1 = (f32[3,1,64,256]{3,2,1,0:T(8,128)}, f32[3,1,64,256]{3,2,1,0:T(8,128)}, u32[]{:S(2)}, u32[]{:S(2)}) collective-permute-start(f32[3,1,64,256]{3,2,1,0:T(8,128)} %get-tuple-element.44), channel_id=1, source_target_pairs={{2,0},{4,2},{6,4},{8,6},{10,8},{12,10},{14,12},{16,14},{18,16},{20... | collective-permute-start | bytes 589832 | tf_op jit(solution)/shard_map/ppermute | solution.py:285
  28.6 50.6 %collective-permute-start = (f32[3,1,64,256]{3,2,1,0:T(8,128)}, f32[3,1,64,256]{3,2,1,0:T(8,128)}, u32[]{:S(2)}, u32[]{:S(2)}) collective-permute-start(f32[3,1,64,256]{3,2,1,0:T(8,128)} %get-tuple-element.45), channel_id=1, source_target_pairs={{0,2},{2,4},{4,6},{6,8},{8,10},{10,12},{12,14},{14,16},{16,18},{18... | collective-permute-start | bytes 589832 | tf_op jit(solution)/shard_map/ppermute | solution.py:285
  31.2 38.8 %copy-start.12 = (f32[80]{0:T(128)}, f32[80]{0:T(128)S(1)}, u32[]{:S(2)}) copy-start(f32[80]{0:T(128)S(1)} %cos.4) | copy-start | bytes 964
  38.6 31.3 %copy-start.15 = (s32[80]{0:T(128)S(1)}, s32[80]{0:T(128)}, u32[]{:S(2)}) copy-start(s32[80]{0:T(128)} %param.24) | copy-start | bytes 964
  38.6 31.4 %copy-start.10 = (f32[80]{0:T(128)S(1)}, f32[80]{0:T(128)}, u32[]{:S(2)}) copy-start(f32[80]{0:T(128)} %param.21) | copy-start | bytes 964
  38.6 31.4 %copy-start.14 = (f32[3,80]{1,0:T(4,128)S(1)}, f32[3,80]{1,0:T(4,128)}, u32[]{:S(2)}) copy-start(f32[3,80]{1,0:T(4,128)} %param.23) | copy-start | bytes 2884
  63.4 6.5 %copy-start.5 = (bf16[128,3,2,2048]{3,2,1,0:T(2,128)(2,1)}, bf16[128,3,2,2048]{3,2,1,0:T(2,128)(2,1)S(1)}, u32[]{:S(2)}) copy-start(bf16[128,3,2,2048]{3,2,1,0:T(2,128)(2,1)S(1)} %all-to-all-done) | copy-start | bytes 9437188
  63.4 47.7 %all-to-all-start.1 = ((bf16[128,3,2,2048]{3,2,1,0:T(2,128)(2,1)}), bf16[128,3,2,2048]{3,2,1,0:T(2,128)(2,1)}, u32[]{:S(2)}, u32[]{:S(2)}) async-start(bf16[128,3,2,2048]{3,2,1,0:T(2,128)(2,1)} %copy.29), calls=%async_computation.1 | async-start | bytes 6291456 | tf_op jit(solution)/shard_map/all_to_all | solution.py:336
  69.9 3.6 %copy-start.8 = (s32[128,2]{0,1:T(2,128)S(1)}, s32[128,2]{0,1:T(2,128)}, u32[]{:S(2)}) copy-start(s32[128,2]{0,1:T(2,128)} %copy-done.7) | copy-start | bytes 3076
  69.9 3.6 %copy-start.19 = (s32[128]{0:T(128)S(1)}, s32[128]{0:T(128)}, u32[]{:S(2)}) copy-start(s32[128]{0:T(128)} %param.18) | copy-start | bytes 1540
  75.0 4.2 %copy-start = (bf16[8,128,128]{2,1,0:T(8,128)(2,1)S(1)}, bf16[8,128,128]{2,1,0:T(8,128)(2,1)}, u32[]{:S(2)}) copy-start(bf16[8,128,128]{2,1,0:T(8,128)(2,1)} %param.20) | copy-start | bytes 786436
  99.5 19.2 %collective-permute-start.6 = (f32[3,16,1,256]{3,2,1,0:T(1,128)}, f32[3,16,1,256]{3,2,1,0:T(1,128)}, u32[]{:S(2)}, u32[]{:S(2)}) collective-permute-start(f32[3,16,1,256]{3,2,1,0:T(1,128)} %get-tuple-element.37), channel_id=1, source_target_pairs={{0,1},{1,0},{2,3},{3,2},{4,5},{5,4},{6,7},{7,6},{8,9},{9,8},{10,11... | collective-permute-start | bytes 147464 | tf_op jit(solution)/shard_map/ppermute | solution.py:285
  101.0 17.7 %collective-permute-start.7 = (f32[3,16,1,256]{3,2,1,0:T(1,128)}, f32[3,16,1,256]{3,2,1,0:T(1,128)}, u32[]{:S(2)}, u32[]{:S(2)}) collective-permute-start(f32[3,16,1,256]{3,2,1,0:T(1,128)} %get-tuple-element.38), channel_id=1, source_target_pairs={{1,0},{0,1},{3,2},{2,3},{5,4},{4,5},{7,6},{6,7},{9,8},{8,9},{11,10... | collective-permute-start | bytes 147464 | tf_op jit(solution)/shard_map/ppermute | solution.py:285
  101.0 17.7 %collective-permute-start.4 = (f32[3,1,64,256]{3,2,1,0:T(8,128)}, f32[3,1,64,256]{3,2,1,0:T(8,128)}, u32[]{:S(2)}, u32[]{:S(2)}) collective-permute-start(f32[3,1,64,256]{3,2,1,0:T(8,128)} %get-tuple-element.35), channel_id=1, source_target_pairs={{0,2},{2,4},{4,6},{6,8},{8,10},{10,12},{12,14},{14,16},{16,18},{18... | collective-permute-start | bytes 589832 | tf_op jit(solution)/shard_map/ppermute | solution.py:285
  105.0 13.7 %collective-permute-start.5 = (f32[3,1,64,256]{3,2,1,0:T(8,128)}, f32[3,1,64,256]{3,2,1,0:T(8,128)}, u32[]{:S(2)}, u32[]{:S(2)}) collective-permute-start(f32[3,1,64,256]{3,2,1,0:T(8,128)} %get-tuple-element.36), channel_id=1, source_target_pairs={{2,0},{4,2},{6,4},{8,6},{10,8},{12,10},{14,12},{16,14},{18,16},{20... | collective-permute-start | bytes 589832 | tf_op jit(solution)/shard_map/ppermute | solution.py:285
  120.0 20.1 %copy-start.11 = (f32[80]{0:T(128)S(1)}, f32[80]{0:T(128)}, u32[]{:S(2)}) copy-start(f32[80]{0:T(128)} %param.21) | copy-start | bytes 964
  120.0 20.1 %copy-start.13 = (f32[80]{0:T(128)S(1)}, f32[80]{0:T(128)}, u32[]{:S(2)}) copy-start(f32[80]{0:T(128)} %copy-done.12) | copy-start | bytes 964
  120.0 20.1 %copy-start.17 = (f32[80]{0:T(128)S(1)}, f32[80]{0:T(128)}, u32[]{:S(2)}) copy-start(f32[80]{0:T(128)} %param.22) | copy-start | bytes 964
  (6 other events, 7.1 us)

commit v10 on v7

--- a/solution.py
+++ b/solution.py
@@ -336,9 +336,9 @@
         ).astype(jnp.bfloat16)
         arrived = lax.all_to_all(packed, ("gx", "gy"), split_axis=0, concat_axis=0, tiled=True)
         forward = jnp.einsum(
-            "jsr,scrb->cjb", pick_table, arrived, preferred_element_type=jnp.float32
-        ).astype(jnp.bfloat16)
-        forward = forward.reshape(components, width_x, width_y, height)
+            "scrb,jsr->cjb", arrived, pick_table, preferred_element_type=jnp.float32
+        )
+        forward = forward.reshape(components, width_x, width_y, height).astype(jnp.bfloat16)
         west, east = halo(*edges[0], "gx")
         south, north = halo(*edges[1], "gy")
         adjoint, gradient_block, first_plane, last_plane, first_row, last_row = advance(

time: 146 us -> 146 us (level)
  matrix products: 10.7 us -> 14.2 us
  local copies, waits for them, and re-layouts: 28.5 us -> 25.3 us
    reshape x2 -> x0, local copies, waits for them, and re-layouts: 5.16 us -> none  [shards(): forward = forward.reshape(components, width_x, width_y, height)]
    dot_general x2, matrix products: 4.8 us -> 8.33 us  [shards(): jnp.einsum('scrb,jsr->cjb', arrived, pick_table, preferred_element_type=j...]
    convert_element_type x2, local copies, waits for them, and re-layouts: 3.15 us -> 5.16 us  [shards(): forward.reshape(components, width_x, width_y, height).astype(jnp.bfloat16)]
where the time goes in v10:
time: 146 us; the launch traced here: 145 us
  Pallas kernels  39.1 us (27%)
  waiting for transfers between devices  30.8 us (21%)
  starting transfers between devices  29.1 us (20%)
  local copies, waits for them, and re-layouts  25.3 us (17%)
  matrix products  14.2 us (10%)
  other arithmetic  5.35 us (4%)
    pallas_call x2, Pallas kernels, advance(): pl.pallas_call(functools.partial(advance_kernel, count_y, group, exchange...  39.1 us
    all_to_all x2, waiting for transfers between devices, shards(): lax.all_to_all(packed, ('gx', 'gy'), split_axis=0, concat_axis=0, tiled=T...  30.8 us
    all_to_all x2, starting transfers between devices, shards(): lax.all_to_all(packed, ('gx', 'gy'), split_axis=0, concat_axis=0, tiled=T...  18 us
    convert_element_type x2, local copies, waits for them, and re-layouts, shards(): packed = jnp.einsum('drs,scb->dcrb', pack_table, stored, preferred_elemen...  9.8 us
    dot_general x2, matrix products, shards(): jnp.einsum('scrb,jsr->cjb', arrived, pick_table, preferred_element_type=j...  8.33 us
    ppermute x4, starting transfers between devices, halo(): lax.ppermute(last, axis, forward)  8.02 us
    unnamed x42, local copies, waits for them, and re-layouts  6.64 us
    convert_element_type x2, local copies, waits for them, and re-layouts, shards(): forward.reshape(components, width_x, width_y, height).astype(jnp.bfloat16)  5.16 us
  transfers between devices with their start and end apart: 10, of which 2 were waited for; matrix products, arithmetic and copies ran while one was open for 19% of the time, Pallas kernels for 13%

profile of v10, /device:TPU:1, one launch (start us, length us, event | category | flops | bytes accessed | tf_op | source)
XLA Modules:
  0.0 144.9 jit_solution(10561049894567290514)
XLA Ops:
  1.6 0.8 select_reduce_fusion
  3.1 2.4 %fusion.4 = bf16[128,3,2,2048]{3,0,1,2:T(8,128)(2,1)S(1)} fusion(bf16[2,128,3,2048]{3,1,2,0:T(8,128)(2,1)} %param.16, s32[128]{0:T(128)S(1)} %add_add_fusion, s32[128,2]{0,1:T(2,128)S(1)} %multiply_add_fusion), kind=kOutput, calls=%fused_computation.8 | convolution fusion | flops 404258816 | bytes 4720128 | tf_op jit(solution)/shard_map/drs,scb->dcrb/dot_general | solution.py:334
  5.5 4.9 %copy.21 = bf16[128,3,2,2048]{3,2,1,0:T(2,128)(2,1)} copy(bf16[128,3,2,2048]{3,0,1,2:T(8,128)(2,1)S(1)} %fusion.4) | data formatting | bytes 6291456 | tf_op jit(solution)/shard_map/convert_element_type | solution.py:336
  10.4 11.5 %all-to-all-start = ((bf16[128,3,2,2048]{3,2,1,0:T(2,128)(2,1)}), bf16[128,3,2,2048]{3,2,1,0:T(2,128)(2,1)S(1)}, u32[]{:S(2)}, u32[]{:S(2)}) async-start(bf16[128,3,2,2048]{3,2,1,0:T(2,128)(2,1)} %copy.21), calls=%async_computation | async-start | bytes 6291456 | tf_op jit(solution)/shard_map/all_to_all | solution.py:337
  21.9 1.8 %fusion.54 = (f32[3,16,1,256]{3,2,1,0:T(1,128)}, f32[3,16,1,256]{3,2,1,0:T(1,128)}) fusion(f32[3,16,64,256]{3,2,1,0:T(8,128)} %refs_2_.1), kind=kLoop, calls=%fused_computation.76 | loop fusion | bytes 196608 | tf_op jit(solution)/shard_map/slice | solution.py:330
  23.7 1.5 %collective-permute-start.3 = (f32[3,16,1,256]{3,2,1,0:T(1,128)}, f32[3,16,1,256]{3,2,1,0:T(1,128)}, u32[]{:S(2)}, u32[]{:S(2)}) collective-permute-start(f32[3,16,1,256]{3,2,1,0:T(1,128)} %get-tuple-element.42), channel_id=1, source_target_pairs={{1,0},{0,1},{3,2},{2,3},{5,4},{4,5},{7,6},{6,7},{9,8},{8,9},{11,10... | collective-permute-start | bytes 147464 | tf_op jit(solution)/shard_map/ppermute | solution.py:286
  25.3 1.8 %fusion.55 = (f32[3,1,64,256]{3,2,1,0:T(8,128)}, f32[3,1,64,256]{3,2,1,0:T(8,128)}) fusion(f32[3,16,64,256]{3,2,1,0:T(8,128)} %refs_2_.1), kind=kLoop, calls=%fused_computation.77 | loop fusion | bytes 786432 | tf_op jit(solution)/shard_map/slice | solution.py:329
  27.1 1.6 %collective-permute-start.1 = (f32[3,1,64,256]{3,2,1,0:T(8,128)}, f32[3,1,64,256]{3,2,1,0:T(8,128)}, u32[]{:S(2)}, u32[]{:S(2)}) collective-permute-start(f32[3,1,64,256]{3,2,1,0:T(8,128)} %get-tuple-element.44), channel_id=1, source_target_pairs={{2,0},{4,2},{6,4},{8,6},{10,8},{12,10},{14,12},{16,14},{18,16},{20... | collective-permute-start | bytes 589832 | tf_op jit(solution)/shard_map/ppermute | solution.py:286
  28.6 2.5 %collective-permute-start = (f32[3,1,64,256]{3,2,1,0:T(8,128)}, f32[3,1,64,256]{3,2,1,0:T(8,128)}, u32[]{:S(2)}, u32[]{:S(2)}) collective-permute-start(f32[3,1,64,256]{3,2,1,0:T(8,128)} %get-tuple-element.45), channel_id=1, source_target_pairs={{0,2},{2,4},{4,6},{6,8},{8,10},{10,12},{12,14},{14,16},{16,18},{18... | collective-permute-start | bytes 589832 | tf_op jit(solution)/shard_map/ppermute | solution.py:286
  31.2 2.4 %fusion.5 = bf16[128,3,2,2048]{3,0,1,2:T(8,128)(2,1)S(1)} fusion(bf16[2,128,3,2048]{3,1,2,0:T(8,128)(2,1)} %param.16, s32[128]{0:T(128)S(1)} %add_add_fusion, s32[128,2]{0,1:T(2,128)S(1)} %multiply_add_fusion), kind=kOutput, calls=%fused_computation.9 | convolution fusion | flops 404258816 | bytes 4720128 | tf_op jit(solution)/shard_map/drs,scb->dcrb/dot_general | solution.py:334
  33.7 4.9 %copy.24 = bf16[128,3,2,2048]{3,2,1,0:T(2,128)(2,1)} copy(bf16[128,3,2,2048]{3,0,1,2:T(8,128)(2,1)S(1)} %fusion.5) | data formatting | bytes 6291456 | tf_op jit(solution)/shard_map/convert_element_type | solution.py:336
  38.6 24.9 %all-to-all-done = bf16[128,3,2,2048]{3,2,1,0:T(2,128)(2,1)S(1)} async-done(((bf16[128,3,2,2048]{3,2,1,0:T(2,128)(2,1)}), bf16[128,3,2,2048]{3,2,1,0:T(2,128)(2,1)S(1)}, u32[]{:S(2)}, u32[]{:S(2)}) %all-to-all-start) | async-done | bytes 3145760 | tf_op jit(solution)/shard_map/all_to_all | solution.py:337
  63.4 6.5 %all-to-all-start.1 = ((bf16[128,3,2,2048]{3,2,1,0:T(2,128)(2,1)}), bf16[128,3,2,2048]{3,2,1,0:T(2,128)(2,1)}, u32[]{:S(2)}, u32[]{:S(2)}) async-start(bf16[128,3,2,2048]{3,2,1,0:T(2,128)(2,1)} %copy.24), calls=%async_computation.1 | async-start | bytes 6291456 | tf_op jit(solution)/shard_map/all_to_all | solution.py:337
  72.5 1.0 fusion.29.refs_8_
  73.6 3.2 %fusion.10 = bf16[3,128,2048]{2,1,0:T(8,128)(2,1)} fusion(bf16[128,3,2,2048]{3,2,1,0:T(2,128)(2,1)S(1)} %copy-done.6, s32[128,2]{0,1:T(2,128)S(1)} %copy-done.8, s32[128]{0:T(128)S(1)} %copy-done.14), kind=kOutput, calls=%fused_computation.10 | convolution fusion | flops 403472384 | bytes 4720128 | tf_op jit(solution)/shard_map/scrb,jsr->cjb/dot_general | solution.py:338
  76.7 2.6 %convert_element_type.40.refs_7_ = bf16[3,16,64,256]{3,2,1,0:T(8,128)(2,1)S(1)} reshape(bf16[3,128,2048]{2,1,0:T(8,128)(2,1)} %fusion.10) | data formatting | bytes 3145728 | tf_op jit(solution)/shard_map/convert_element_type | solution.py:341
  80.1 19.0 %shard_map.122 = (f32[3,16,64,256]{3,2,1,0:T(8,128)}, f32[8,128]{1,0:T(8,128)S(1)}, f32[3,1,64,256]{3,2,1,0:T(8,128)}, f32[3,1,64,256]{3,2,1,0:T(8,128)}, f32[3,...) custom-call(s32[32,8]{1,0:T(8,128)S(1)} %copy.26.refs_0_, f32[16]{0:T(128)S(1)} %copy-done.3, f32[3,16,64,256]{3,2,1,0:T(8,128)} %refs_2_.1, ...), custom_call_target="tpu_custom_call" | custom-call | tf_op jit(solution)/shard_map/pallas_call | solution.py:261
  99.6 1.5 %collective-permute-start.6 = (f32[3,16,1,256]{3,2,1,0:T(1,128)}, f32[3,16,1,256]{3,2,1,0:T(1,128)}, u32[]{:S(2)}, u32[]{:S(2)}) collective-permute-start(f32[3,16,1,256]{3,2,1,0:T(1,128)} %get-tuple-element.37), channel_id=1, source_target_pairs={{0,1},{1,0},{2,3},{3,2},{4,5},{5,4},{6,7},{7,6},{8,9},{9,8},{10,11... | collective-permute-start | bytes 147464 | tf_op jit(solution)/shard_map/ppermute | solution.py:286
  101.2 4.0 %collective-permute-start.4 = (f32[3,1,64,256]{3,2,1,0:T(8,128)}, f32[3,1,64,256]{3,2,1,0:T(8,128)}, u32[]{:S(2)}, u32[]{:S(2)}) collective-permute-start(f32[3,1,64,256]{3,2,1,0:T(8,128)} %get-tuple-element.35), channel_id=1, source_target_pairs={{0,2},{2,4},{4,6},{6,8},{8,10},{10,12},{12,14},{14,16},{16,18},{18... | collective-permute-start | bytes 589832 | tf_op jit(solution)/shard_map/ppermute | solution.py:286
  105.2 5.9 %all-to-all-done.1 = bf16[128,3,2,2048]{3,2,1,0:T(2,128)(2,1)} async-done(((bf16[128,3,2,2048]{3,2,1,0:T(2,128)(2,1)}), bf16[128,3,2,2048]{3,2,1,0:T(2,128)(2,1)}, u32[]{:S(2)}, u32[]{:S(2)}) %all-to-all-start.1) | async-done | bytes 3145760 | tf_op jit(solution)/shard_map/all_to_all | solution.py:337
  111.1 5.1 %fusion.13 = bf16[3,128,2048]{2,1,0:T(8,128)(2,1)} fusion(bf16[128,3,2,2048]{3,2,1,0:T(2,128)(2,1)} %all-to-all-done.1, s32[128,2]{0,1:T(2,128)} %copy-done.7, s32[128]{0:T(128)} %param.18), kind=kOutput, calls=%fused_computation.11 | convolution fusion | flops 403472384 | bytes 4720128 | tf_op jit(solution)/shard_map/scrb,jsr->cjb/dot_general | solution.py:338
  116.3 2.6 %convert_element_type.46.refs_7_ = bf16[3,16,64,256]{3,2,1,0:T(8,128)(2,1)S(1)} reshape(bf16[3,128,2048]{2,1,0:T(8,128)(2,1)} %fusion.13) | data formatting | bytes 3145728 | tf_op jit(solution)/shard_map/convert_element_type | solution.py:341
  120.3 20.1 %shard_map.123 = (f32[3,16,64,256]{3,2,1,0:T(8,128)}, f32[8,128]{1,0:T(8,128)S(1)}, f32[3,1,64,256]{3,2,1,0:T(8,128)}, f32[3,1,64,256]{3,2,1,0:T(8,128)}, f32[3,...) custom-call(s32[32,8]{1,0:T(8,128)S(1)} %copy.26.refs_0_, f32[16]{0:T(128)S(1)} %copy-done.4, ...), custom_call_target="tpu_custom_call" | custom-call | tf_op jit(solution)/shard_map/pallas_call | solution.py:261
  141.0 3.9 %copy.43 = f32[3,16,64,256]{3,2,1,0:T(8,128)} copy(f32[3,16,64,256]{3,2,1,0:T(8,128)} %get-tuple-element.57) | data formatting | bytes 6291456
  (75 shorter events, 7.4 us)
Async XLA Ops:
  0.6 30.6 %copy-start.7 = (s32[128,2]{0,1:T(2,128)}, s32[128,2]{0,1:T(2,128)S(1)}, u32[]{:S(2)}) copy-start(s32[128,2]{0,1:T(2,128)S(1)} %multiply_add_fusion) | copy-start | bytes 3076
  10.4 20.7 %copy-start.17 = (f32[80]{0:T(128)S(1)}, f32[80]{0:T(128)}, u32[]{:S(2)}) copy-start(f32[80]{0:T(128)} %param.22) | copy-start | bytes 964
  10.4 20.8 %copy-start.9 = (s32[32,8]{0,1:T(8,128)S(1)}, s32[32,8]{0,1:T(8,128)}, u32[]{:S(2)}) copy-start(s32[32,8]{0,1:T(8,128)} %param.19) | copy-start | bytes 3076
  10.4 53.0 %all-to-all-start = ((bf16[128,3,2,2048]{3,2,1,0:T(2,128)(2,1)}), bf16[128,3,2,2048]{3,2,1,0:T(2,128)(2,1)S(1)}, u32[]{:S(2)}, u32[]{:S(2)}) async-start(bf16[128,3,2,2048]{3,2,1,0:T(2,128)(2,1)} %copy.21), calls=%async_computation | async-start | bytes 6291456 | tf_op jit(solution)/shard_map/all_to_all | solution.py:337
  23.7 55.6 %collective-permute-start.3 = (f32[3,16,1,256]{3,2,1,0:T(1,128)}, f32[3,16,1,256]{3,2,1,0:T(1,128)}, u32[]{:S(2)}, u32[]{:S(2)}) collective-permute-start(f32[3,16,1,256]{3,2,1,0:T(1,128)} %get-tuple-element.42), channel_id=1, source_target_pairs={{1,0},{0,1},{3,2},{2,3},{5,4},{4,5},{7,6},{6,7},{9,8},{8,9},{11,10... | collective-permute-start | bytes 147464 | tf_op jit(solution)/shard_map/ppermute | solution.py:286
  25.2 54.1 %collective-permute-start.2 = (f32[3,16,1,256]{3,2,1,0:T(1,128)}, f32[3,16,1,256]{3,2,1,0:T(1,128)}, u32[]{:S(2)}, u32[]{:S(2)}) collective-permute-start(f32[3,16,1,256]{3,2,1,0:T(1,128)} %get-tuple-element.43), channel_id=1, source_target_pairs={{0,1},{1,0},{2,3},{3,2},{4,5},{5,4},{6,7},{7,6},{8,9},{9,8},{10,11... | collective-permute-start | bytes 147464 | tf_op jit(solution)/shard_map/ppermute | solution.py:286
  27.1 52.3 %collective-permute-start.1 = (f32[3,1,64,256]{3,2,1,0:T(8,128)}, f32[3,1,64,256]{3,2,1,0:T(8,128)}, u32[]{:S(2)}, u32[]{:S(2)}) collective-permute-start(f32[3,1,64,256]{3,2,1,0:T(8,128)} %get-tuple-element.44), channel_id=1, source_target_pairs={{2,0},{4,2},{6,4},{8,6},{10,8},{12,10},{14,12},{16,14},{18,16},{20... | collective-permute-start | bytes 589832 | tf_op jit(solution)/shard_map/ppermute | solution.py:286
  28.6 50.7 %collective-permute-start = (f32[3,1,64,256]{3,2,1,0:T(8,128)}, f32[3,1,64,256]{3,2,1,0:T(8,128)}, u32[]{:S(2)}, u32[]{:S(2)}) collective-permute-start(f32[3,1,64,256]{3,2,1,0:T(8,128)} %get-tuple-element.45), channel_id=1, source_target_pairs={{0,2},{2,4},{4,6},{6,8},{8,10},{10,12},{12,14},{14,16},{16,18},{18... | collective-permute-start | bytes 589832 | tf_op jit(solution)/shard_map/ppermute | solution.py:286
  31.2 38.8 %copy-start.12 = (f32[80]{0:T(128)}, f32[80]{0:T(128)S(1)}, u32[]{:S(2)}) copy-start(f32[80]{0:T(128)S(1)} %cos.4) | copy-start | bytes 964
  38.6 31.3 %copy-start.16 = (s32[80]{0:T(128)S(1)}, s32[80]{0:T(128)}, u32[]{:S(2)}) copy-start(s32[80]{0:T(128)} %param.24) | copy-start | bytes 964
  38.6 31.4 %copy-start.10 = (f32[80]{0:T(128)S(1)}, f32[80]{0:T(128)}, u32[]{:S(2)}) copy-start(f32[80]{0:T(128)} %param.21) | copy-start | bytes 964
  38.6 31.4 %copy-start.15 = (f32[3,80]{1,0:T(4,128)S(1)}, f32[3,80]{1,0:T(4,128)}, u32[]{:S(2)}) copy-start(f32[3,80]{1,0:T(4,128)} %param.23) | copy-start | bytes 2884
  63.4 6.5 %copy-start.5 = (bf16[128,3,2,2048]{3,2,1,0:T(2,128)(2,1)}, bf16[128,3,2,2048]{3,2,1,0:T(2,128)(2,1)S(1)}, u32[]{:S(2)}) copy-start(bf16[128,3,2,2048]{3,2,1,0:T(2,128)(2,1)S(1)} %all-to-all-done) | copy-start | bytes 9437188
  63.4 47.7 %all-to-all-start.1 = ((bf16[128,3,2,2048]{3,2,1,0:T(2,128)(2,1)}), bf16[128,3,2,2048]{3,2,1,0:T(2,128)(2,1)}, u32[]{:S(2)}, u32[]{:S(2)}) async-start(bf16[128,3,2,2048]{3,2,1,0:T(2,128)(2,1)} %copy.24), calls=%async_computation.1 | async-start | bytes 6291456 | tf_op jit(solution)/shard_map/all_to_all | solution.py:337
  69.9 3.6 %copy-start.8 = (s32[128,2]{0,1:T(2,128)S(1)}, s32[128,2]{0,1:T(2,128)}, u32[]{:S(2)}) copy-start(s32[128,2]{0,1:T(2,128)} %copy-done.7) | copy-start | bytes 3076
  69.9 3.6 %copy-start.14 = (s32[128]{0:T(128)S(1)}, s32[128]{0:T(128)}, u32[]{:S(2)}) copy-start(s32[128]{0:T(128)} %param.18) | copy-start | bytes 1540
  73.5 5.8 %copy-start = (bf16[8,128,128]{2,1,0:T(8,128)(2,1)S(1)}, bf16[8,128,128]{2,1,0:T(8,128)(2,1)}, u32[]{:S(2)}) copy-start(bf16[8,128,128]{2,1,0:T(8,128)(2,1)} %param.20) | copy-start | bytes 786436
  99.6 19.2 %collective-permute-start.6 = (f32[3,16,1,256]{3,2,1,0:T(1,128)}, f32[3,16,1,256]{3,2,1,0:T(1,128)}, u32[]{:S(2)}, u32[]{:S(2)}) collective-permute-start(f32[3,16,1,256]{3,2,1,0:T(1,128)} %get-tuple-element.37), channel_id=1, source_target_pairs={{0,1},{1,0},{2,3},{3,2},{4,5},{5,4},{6,7},{7,6},{8,9},{9,8},{10,11... | collective-permute-start | bytes 147464 | tf_op jit(solution)/shard_map/ppermute | solution.py:286
  101.1 17.7 %collective-permute-start.7 = (f32[3,16,1,256]{3,2,1,0:T(1,128)}, f32[3,16,1,256]{3,2,1,0:T(1,128)}, u32[]{:S(2)}, u32[]{:S(2)}) collective-permute-start(f32[3,16,1,256]{3,2,1,0:T(1,128)} %get-tuple-element.38), channel_id=1, source_target_pairs={{1,0},{0,1},{3,2},{2,3},{5,4},{4,5},{7,6},{6,7},{9,8},{8,9},{11,10... | collective-permute-start | bytes 147464 | tf_op jit(solution)/shard_map/ppermute | solution.py:286
  101.2 17.7 %collective-permute-start.4 = (f32[3,1,64,256]{3,2,1,0:T(8,128)}, f32[3,1,64,256]{3,2,1,0:T(8,128)}, u32[]{:S(2)}, u32[]{:S(2)}) collective-permute-start(f32[3,1,64,256]{3,2,1,0:T(8,128)} %get-tuple-element.35), channel_id=1, source_target_pairs={{0,2},{2,4},{4,6},{6,8},{8,10},{10,12},{12,14},{14,16},{16,18},{18... | collective-permute-start | bytes 589832 | tf_op jit(solution)/shard_map/ppermute | solution.py:286
  105.2 13.7 %collective-permute-start.5 = (f32[3,1,64,256]{3,2,1,0:T(8,128)}, f32[3,1,64,256]{3,2,1,0:T(8,128)}, u32[]{:S(2)}, u32[]{:S(2)}) collective-permute-start(f32[3,1,64,256]{3,2,1,0:T(8,128)} %get-tuple-element.36), channel_id=1, source_target_pairs={{2,0},{4,2},{6,4},{8,6},{10,8},{12,10},{14,12},{16,14},{18,16},{20... | collective-permute-start | bytes 589832 | tf_op jit(solution)/shard_map/ppermute | solution.py:286
  120.3 20.1 %copy-start.11 = (f32[80]{0:T(128)S(1)}, f32[80]{0:T(128)}, u32[]{:S(2)}) copy-start(f32[80]{0:T(128)} %param.21) | copy-start | bytes 964
  120.3 20.1 %copy-start.13 = (f32[80]{0:T(128)S(1)}, f32[80]{0:T(128)}, u32[]{:S(2)}) copy-start(f32[80]{0:T(128)} %copy-done.12) | copy-start | bytes 964
  120.3 20.1 %copy-start.18 = (f32[80]{0:T(128)S(1)}, f32[80]{0:T(128)}, u32[]{:S(2)}) copy-start(f32[80]{0:T(128)} %param.22) | copy-start | bytes 964
  (6 other events, 7.2 us)

commit v11 on v7

--- a/solution.py
+++ b/solution.py
@@ -201,7 +201,7 @@
             )
             if c == 0:
                 update = update - drag * center
-            final = update * scale
+            final = update if exchange else update * scale
             out_ref[c, x] = final
             first_row[c, x] = final[0:1, :]
             last_row[c, x] = final[width_y - 1 :, :]
@@ -346,6 +346,7 @@
             turbine, gradient_block, step_index == steps_total - 1,
         )
         edges = ((first_plane, last_plane), (first_row, last_row))
+    adjoint = adjoint * fringe_scale[None, :, None, None]
     gradient_sum = gradient_block[0, : thrust.shape[0]]
     cosine = jnp.cos(yaw_angle)
     sine = jnp.sin(yaw_angle)

time: 146 us -> 146 us (level)
  other arithmetic: 5.35 us -> 9.41 us
  local copies, waits for them, and re-layouts: 28.5 us -> 24.6 us
    mul x0 -> x1, other arithmetic: none -> 4.06 us  [shards(): adjoint = adjoint * fringe_scale[None, :, None, None]]
    unnamed x42 -> x41, local copies, waits for them, and re-layouts: 6.64 us -> 2.74 us
where the time goes in v11:
time: 146 us; the launch traced here: 145 us
  Pallas kernels  39 us (27%)
  waiting for transfers between devices  31 us (21%)
  starting transfers between devices  29.1 us (20%)
  local copies, waits for them, and re-layouts  24.6 us (17%)
  matrix products  10.7 us (7%)
  other arithmetic  9.41 us (6%)
    pallas_call x2, Pallas kernels, advance(): pl.pallas_call(functools.partial(advance_kernel, count_y, group, exchange...  39 us
    all_to_all x2, waiting for transfers between devices, shards(): lax.all_to_all(packed, ('gx', 'gy'), split_axis=0, concat_axis=0, tiled=T...  31 us
    all_to_all x2, starting transfers between devices, shards(): lax.all_to_all(packed, ('gx', 'gy'), split_axis=0, concat_axis=0, tiled=T...  18 us
    convert_element_type x2, local copies, waits for them, and re-layouts, shards(): packed = jnp.einsum('drs,scb->dcrb', pack_table, stored, preferred_elemen...  9.8 us
    ppermute x4, starting transfers between devices, halo(): lax.ppermute(last, axis, forward)  8.01 us
    reshape x2, local copies, waits for them, and re-layouts, shards(): forward = forward.reshape(components, width_x, width_y, height)  5.16 us
    dot_general x2, matrix products, shards(): jnp.einsum('drs,scb->dcrb', pack_table, stored, preferred_element_type=jn...  4.84 us
    dot_general x2, matrix products, shards(): jnp.einsum('jsr,scrb->cjb', pick_table, arrived, preferred_element_type=j...  4.8 us
  transfers between devices with their start and end apart: 10, of which 2 were waited for; matrix products, arithmetic and copies ran while one was open for 19% of the time, Pallas kernels for 13%

profile of v11, /device:TPU:1, one launch (start us, length us, event | category | flops | bytes accessed | tf_op | source)
XLA Modules:
  0.0 144.7 jit_solution(3672349047160740642)
XLA Ops:
  3.1 2.4 %fusion.4 = bf16[128,3,2,2048]{3,0,1,2:T(8,128)(2,1)S(1)} fusion(bf16[2,128,3,2048]{3,1,2,0:T(8,128)(2,1)} %param.16, s32[128]{0:T(128)S(1)} %add_add_fusion, s32[128,2]{0,1:T(2,128)S(1)} %multiply_add_fusion), kind=kOutput, calls=%fused_computation.8 | convolution fusion | flops 404258816 | bytes 4720128 | tf_op jit(solution)/shard_map/drs,scb->dcrb/dot_general | solution.py:334
  5.5 4.9 %copy.25 = bf16[128,3,2,2048]{3,2,1,0:T(2,128)(2,1)} copy(bf16[128,3,2,2048]{3,0,1,2:T(8,128)(2,1)S(1)} %fusion.4) | data formatting | bytes 6291456 | tf_op jit(solution)/shard_map/convert_element_type | solution.py:336
  10.4 11.5 %all-to-all-start = ((bf16[128,3,2,2048]{3,2,1,0:T(2,128)(2,1)}), bf16[128,3,2,2048]{3,2,1,0:T(2,128)(2,1)S(1)}, u32[]{:S(2)}, u32[]{:S(2)}) async-start(bf16[128,3,2,2048]{3,2,1,0:T(2,128)(2,1)} %copy.25), calls=%async_computation | async-start | bytes 6291456 | tf_op jit(solution)/shard_map/all_to_all | solution.py:337
  21.9 1.8 %fusion.54 = (f32[3,16,1,256]{3,2,1,0:T(1,128)}, f32[3,16,1,256]{3,2,1,0:T(1,128)}) fusion(f32[3,16,64,256]{3,2,1,0:T(8,128)} %refs_2_.1), kind=kLoop, calls=%fused_computation.77 | loop fusion | bytes 196608 | tf_op jit(solution)/shard_map/slice | solution.py:330
  23.7 1.5 %collective-permute-start.3 = (f32[3,16,1,256]{3,2,1,0:T(1,128)}, f32[3,16,1,256]{3,2,1,0:T(1,128)}, u32[]{:S(2)}, u32[]{:S(2)}) collective-permute-start(f32[3,16,1,256]{3,2,1,0:T(1,128)} %get-tuple-element.42), channel_id=1, source_target_pairs={{1,0},{0,1},{3,2},{2,3},{5,4},{4,5},{7,6},{6,7},{9,8},{8,9},{11,10... | collective-permute-start | bytes 147464 | tf_op jit(solution)/shard_map/ppermute | solution.py:286
  25.3 1.8 %fusion.55 = (f32[3,1,64,256]{3,2,1,0:T(8,128)}, f32[3,1,64,256]{3,2,1,0:T(8,128)}) fusion(f32[3,16,64,256]{3,2,1,0:T(8,128)} %refs_2_.1), kind=kLoop, calls=%fused_computation.78 | loop fusion | bytes 786432 | tf_op jit(solution)/shard_map/slice | solution.py:329
  27.1 1.6 %collective-permute-start.1 = (f32[3,1,64,256]{3,2,1,0:T(8,128)}, f32[3,1,64,256]{3,2,1,0:T(8,128)}, u32[]{:S(2)}, u32[]{:S(2)}) collective-permute-start(f32[3,1,64,256]{3,2,1,0:T(8,128)} %get-tuple-element.44), channel_id=1, source_target_pairs={{2,0},{4,2},{6,4},{8,6},{10,8},{12,10},{14,12},{16,14},{18,16},{20... | collective-permute-start | bytes 589832 | tf_op jit(solution)/shard_map/ppermute | solution.py:286
  28.6 2.5 %collective-permute-start = (f32[3,1,64,256]{3,2,1,0:T(8,128)}, f32[3,1,64,256]{3,2,1,0:T(8,128)}, u32[]{:S(2)}, u32[]{:S(2)}) collective-permute-start(f32[3,1,64,256]{3,2,1,0:T(8,128)} %get-tuple-element.45), channel_id=1, source_target_pairs={{0,2},{2,4},{4,6},{6,8},{8,10},{10,12},{12,14},{14,16},{16,18},{18... | collective-permute-start | bytes 589832 | tf_op jit(solution)/shard_map/ppermute | solution.py:286
  31.2 2.4 %fusion.5 = bf16[128,3,2,2048]{3,0,1,2:T(8,128)(2,1)S(1)} fusion(bf16[2,128,3,2048]{3,1,2,0:T(8,128)(2,1)} %param.16, s32[128]{0:T(128)S(1)} %add_add_fusion, s32[128,2]{0,1:T(2,128)S(1)} %multiply_add_fusion), kind=kOutput, calls=%fused_computation.9 | convolution fusion | flops 404258816 | bytes 4720128 | tf_op jit(solution)/shard_map/drs,scb->dcrb/dot_general | solution.py:334
  33.7 4.9 %copy.29 = bf16[128,3,2,2048]{3,2,1,0:T(2,128)(2,1)} copy(bf16[128,3,2,2048]{3,0,1,2:T(8,128)(2,1)S(1)} %fusion.5) | data formatting | bytes 6291456 | tf_op jit(solution)/shard_map/convert_element_type | solution.py:336
  38.6 24.9 %all-to-all-done = bf16[128,3,2,2048]{3,2,1,0:T(2,128)(2,1)S(1)} async-done(((bf16[128,3,2,2048]{3,2,1,0:T(2,128)(2,1)}), bf16[128,3,2,2048]{3,2,1,0:T(2,128)(2,1)S(1)}, u32[]{:S(2)}, u32[]{:S(2)}) %all-to-all-start) | async-done | bytes 3145760 | tf_op jit(solution)/shard_map/all_to_all | solution.py:337
  63.4 6.5 %all-to-all-start.1 = ((bf16[128,3,2,2048]{3,2,1,0:T(2,128)(2,1)}), bf16[128,3,2,2048]{3,2,1,0:T(2,128)(2,1)}, u32[]{:S(2)}, u32[]{:S(2)}) async-start(bf16[128,3,2,2048]{3,2,1,0:T(2,128)(2,1)} %copy.29), calls=%async_computation.1 | async-start | bytes 6291456 | tf_op jit(solution)/shard_map/all_to_all | solution.py:337
  73.5 1.5 %fusion.10 = bf16[3,128,2048]{1,2,0:T(8,128)(2,1)S(1)} fusion(bf16[128,3,2,2048]{3,2,1,0:T(2,128)(2,1)S(1)} %copy-done.6, s32[128,2]{0,1:T(2,128)S(1)} %copy-done.8, s32[128]{0:T(128)S(1)} %copy-done.19), kind=kOutput, calls=%fused_computation.10 | convolution fusion | flops 403472384 | bytes 4720128 | tf_op jit(solution)/shard_map/jsr,scrb->cjb/dot_general | solution.py:338
  75.0 1.6 %copy.27 = bf16[3,128,2048]{2,1,0:T(8,128)(2,1)} copy(bf16[3,128,2048]{1,2,0:T(8,128)(2,1)S(1)} %fusion.10) | data formatting | bytes 3145728 | tf_op jit(solution)/shard_map/convert_element_type | solution.py:340
  76.6 2.6 %reshape.198.refs_7_ = bf16[3,16,64,256]{3,2,1,0:T(8,128)(2,1)S(1)} reshape(bf16[3,128,2048]{2,1,0:T(8,128)(2,1)} %copy.27) | data formatting | bytes 3145728 | tf_op jit(solution)/shard_map/reshape | solution.py:341
  79.9 19.0 %shard_map.122 = (f32[3,16,64,256]{3,2,1,0:T(8,128)}, f32[8,128]{1,0:T(8,128)S(1)}, f32[3,1,64,256]{3,2,1,0:T(8,128)}, f32[3,1,64,256]{3,2,1,0:T(8,128)}, f32[3,...) custom-call(s32[32,8]{1,0:T(8,128)S(1)} %copy.32.refs_0_, f32[16]{0:T(128)S(1)} %copy-done.1, f32[3,16,64,256]{3,2,1,0:T(8,128)} %refs_2_.1, ...), custom_call_target="tpu_custom_call" | custom-call | tf_op jit(solution)/shard_map/pallas_call | solution.py:261
  99.5 1.5 %collective-permute-start.6 = (f32[3,16,1,256]{3,2,1,0:T(1,128)}, f32[3,16,1,256]{3,2,1,0:T(1,128)}, u32[]{:S(2)}, u32[]{:S(2)}) collective-permute-start(f32[3,16,1,256]{3,2,1,0:T(1,128)} %get-tuple-element.37), channel_id=1, source_target_pairs={{0,1},{1,0},{2,3},{3,2},{4,5},{5,4},{6,7},{7,6},{8,9},{9,8},{10,11... | collective-permute-start | bytes 147464 | tf_op jit(solution)/shard_map/ppermute | solution.py:286
  101.0 4.0 %collective-permute-start.4 = (f32[3,1,64,256]{3,2,1,0:T(8,128)}, f32[3,1,64,256]{3,2,1,0:T(8,128)}, u32[]{:S(2)}, u32[]{:S(2)}) collective-permute-start(f32[3,1,64,256]{3,2,1,0:T(8,128)} %get-tuple-element.35), channel_id=1, source_target_pairs={{0,2},{2,4},{4,6},{6,8},{8,10},{10,12},{12,14},{14,16},{16,18},{18... | collective-permute-start | bytes 589832 | tf_op jit(solution)/shard_map/ppermute | solution.py:286
  105.0 6.1 %all-to-all-done.1 = bf16[128,3,2,2048]{3,2,1,0:T(2,128)(2,1)} async-done(((bf16[128,3,2,2048]{3,2,1,0:T(2,128)(2,1)}), bf16[128,3,2,2048]{3,2,1,0:T(2,128)(2,1)}, u32[]{:S(2)}, u32[]{:S(2)}) %all-to-all-start.1) | async-done | bytes 3145760 | tf_op jit(solution)/shard_map/all_to_all | solution.py:337
  111.1 3.3 %fusion.13 = bf16[3,128,2048]{1,2,0:T(8,128)(2,1)S(1)} fusion(bf16[128,3,2,2048]{3,2,1,0:T(2,128)(2,1)} %all-to-all-done.1, s32[128,2]{0,1:T(2,128)} %copy-done.7, s32[128]{0:T(128)} %param.18), kind=kOutput, calls=%fused_computation.11 | convolution fusion | flops 403472384 | bytes 4720128 | tf_op jit(solution)/shard_map/jsr,scrb->cjb/dot_general | solution.py:338
  114.5 1.6 %copy.31 = bf16[3,128,2048]{2,1,0:T(8,128)(2,1)} copy(bf16[3,128,2048]{1,2,0:T(8,128)(2,1)S(1)} %fusion.13) | data formatting | bytes 3145728 | tf_op jit(solution)/shard_map/convert_element_type | solution.py:340
  116.1 2.6 %reshape.201.refs_7_ = bf16[3,16,64,256]{3,2,1,0:T(8,128)(2,1)S(1)} reshape(bf16[3,128,2048]{2,1,0:T(8,128)(2,1)} %copy.31) | data formatting | bytes 3145728 | tf_op jit(solution)/shard_map/reshape | solution.py:341
  120.0 20.0 %shard_map.123 = (f32[3,16,64,256]{3,2,1,0:T(8,128)}, f32[8,128]{1,0:T(8,128)S(1)}, f32[3,1,64,256]{3,2,1,0:T(8,128)}, f32[3,1,64,256]{3,2,1,0:T(8,128)}, f32[3,...) custom-call(s32[32,8]{1,0:T(8,128)S(1)} %copy.32.refs_0_, f32[16]{0:T(128)S(1)} %copy-done.2, ...), custom_call_target="tpu_custom_call" | custom-call | tf_op jit(solution)/shard_map/pallas_call | solution.py:261
  140.1 4.1 %broadcast_multiply_fusion = f32[3,16,64,256]{3,2,1,0:T(8,128)} fusion(f32[3,16,64,256]{3,2,1,0:T(8,128)} %get-tuple-element.40, f32[16]{0:T(128)S(1)} %copy-done.2), kind=kLoop, calls=%fused_computation.14 | loop fusion | flops 786432 | bytes 6291520 | tf_op jit(solution)/shard_map/mul | solution.py:349
  (77 shorter events, 9.3 us)
Async XLA Ops:
  0.6 30.6 %copy-start.7 = (s32[128,2]{0,1:T(2,128)}, s32[128,2]{0,1:T(2,128)S(1)}, u32[]{:S(2)}) copy-start(s32[128,2]{0,1:T(2,128)S(1)} %multiply_add_fusion) | copy-start | bytes 3076
  10.4 20.7 %copy-start.16 = (f32[80]{0:T(128)S(1)}, f32[80]{0:T(128)}, u32[]{:S(2)}) copy-start(f32[80]{0:T(128)} %param.22) | copy-start | bytes 964
  10.4 20.8 %copy-start.9 = (s32[32,8]{0,1:T(8,128)S(1)}, s32[32,8]{0,1:T(8,128)}, u32[]{:S(2)}) copy-start(s32[32,8]{0,1:T(8,128)} %param.19) | copy-start | bytes 3076
  10.4 53.0 %all-to-all-start = ((bf16[128,3,2,2048]{3,2,1,0:T(2,128)(2,1)}), bf16[128,3,2,2048]{3,2,1,0:T(2,128)(2,1)S(1)}, u32[]{:S(2)}, u32[]{:S(2)}) async-start(bf16[128,3,2,2048]{3,2,1,0:T(2,128)(2,1)} %copy.25), calls=%async_computation | async-start | bytes 6291456 | tf_op jit(solution)/shard_map/all_to_all | solution.py:337
  23.7 55.4 %collective-permute-start.3 = (f32[3,16,1,256]{3,2,1,0:T(1,128)}, f32[3,16,1,256]{3,2,1,0:T(1,128)}, u32[]{:S(2)}, u32[]{:S(2)}) collective-permute-start(f32[3,16,1,256]{3,2,1,0:T(1,128)} %get-tuple-element.42), channel_id=1, source_target_pairs={{1,0},{0,1},{3,2},{2,3},{5,4},{4,5},{7,6},{6,7},{9,8},{8,9},{11,10... | collective-permute-start | bytes 147464 | tf_op jit(solution)/shard_map/ppermute | solution.py:286
  25.2 53.9 %collective-permute-start.2 = (f32[3,16,1,256]{3,2,1,0:T(1,128)}, f32[3,16,1,256]{3,2,1,0:T(1,128)}, u32[]{:S(2)}, u32[]{:S(2)}) collective-permute-start(f32[3,16,1,256]{3,2,1,0:T(1,128)} %get-tuple-element.43), channel_id=1, source_target_pairs={{0,1},{1,0},{2,3},{3,2},{4,5},{5,4},{6,7},{7,6},{8,9},{9,8},{10,11... | collective-permute-start | bytes 147464 | tf_op jit(solution)/shard_map/ppermute | solution.py:286
  27.1 52.1 %collective-permute-start.1 = (f32[3,1,64,256]{3,2,1,0:T(8,128)}, f32[3,1,64,256]{3,2,1,0:T(8,128)}, u32[]{:S(2)}, u32[]{:S(2)}) collective-permute-start(f32[3,1,64,256]{3,2,1,0:T(8,128)} %get-tuple-element.44), channel_id=1, source_target_pairs={{2,0},{4,2},{6,4},{8,6},{10,8},{12,10},{14,12},{16,14},{18,16},{20... | collective-permute-start | bytes 589832 | tf_op jit(solution)/shard_map/ppermute | solution.py:286
  28.6 50.6 %collective-permute-start = (f32[3,1,64,256]{3,2,1,0:T(8,128)}, f32[3,1,64,256]{3,2,1,0:T(8,128)}, u32[]{:S(2)}, u32[]{:S(2)}) collective-permute-start(f32[3,1,64,256]{3,2,1,0:T(8,128)} %get-tuple-element.45), channel_id=1, source_target_pairs={{0,2},{2,4},{4,6},{6,8},{8,10},{10,12},{12,14},{14,16},{16,18},{18... | collective-permute-start | bytes 589832 | tf_op jit(solution)/shard_map/ppermute | solution.py:286
  31.2 38.8 %copy-start.12 = (f32[80]{0:T(128)}, f32[80]{0:T(128)S(1)}, u32[]{:S(2)}) copy-start(f32[80]{0:T(128)S(1)} %cos.4) | copy-start | bytes 964
  38.6 31.3 %copy-start.15 = (s32[80]{0:T(128)S(1)}, s32[80]{0:T(128)}, u32[]{:S(2)}) copy-start(s32[80]{0:T(128)} %param.24) | copy-start | bytes 964
  38.6 31.4 %copy-start.10 = (f32[80]{0:T(128)S(1)}, f32[80]{0:T(128)}, u32[]{:S(2)}) copy-start(f32[80]{0:T(128)} %param.21) | copy-start | bytes 964
  38.6 31.4 %copy-start.14 = (f32[3,80]{1,0:T(4,128)S(1)}, f32[3,80]{1,0:T(4,128)}, u32[]{:S(2)}) copy-start(f32[3,80]{1,0:T(4,128)} %param.23) | copy-start | bytes 2884
  63.4 6.5 %copy-start.5 = (bf16[128,3,2,2048]{3,2,1,0:T(2,128)(2,1)}, bf16[128,3,2,2048]{3,2,1,0:T(2,128)(2,1)S(1)}, u32[]{:S(2)}) copy-start(bf16[128,3,2,2048]{3,2,1,0:T(2,128)(2,1)S(1)} %all-to-all-done) | copy-start | bytes 9437188
  63.4 47.7 %all-to-all-start.1 = ((bf16[128,3,2,2048]{3,2,1,0:T(2,128)(2,1)}), bf16[128,3,2,2048]{3,2,1,0:T(2,128)(2,1)}, u32[]{:S(2)}, u32[]{:S(2)}) async-start(bf16[128,3,2,2048]{3,2,1,0:T(2,128)(2,1)} %copy.29), calls=%async_computation.1 | async-start | bytes 6291456 | tf_op jit(solution)/shard_map/all_to_all | solution.py:337
  69.9 3.6 %copy-start.8 = (s32[128,2]{0,1:T(2,128)S(1)}, s32[128,2]{0,1:T(2,128)}, u32[]{:S(2)}) copy-start(s32[128,2]{0,1:T(2,128)} %copy-done.7) | copy-start | bytes 3076
  69.9 3.6 %copy-start.19 = (s32[128]{0:T(128)S(1)}, s32[128]{0:T(128)}, u32[]{:S(2)}) copy-start(s32[128]{0:T(128)} %param.18) | copy-start | bytes 1540
  75.0 4.2 %copy-start = (bf16[8,128,128]{2,1,0:T(8,128)(2,1)S(1)}, bf16[8,128,128]{2,1,0:T(8,128)(2,1)}, u32[]{:S(2)}) copy-start(bf16[8,128,128]{2,1,0:T(8,128)(2,1)} %param.20) | copy-start | bytes 786436
  99.5 19.2 %collective-permute-start.6 = (f32[3,16,1,256]{3,2,1,0:T(1,128)}, f32[3,16,1,256]{3,2,1,0:T(1,128)}, u32[]{:S(2)}, u32[]{:S(2)}) collective-permute-start(f32[3,16,1,256]{3,2,1,0:T(1,128)} %get-tuple-element.37), channel_id=1, source_target_pairs={{0,1},{1,0},{2,3},{3,2},{4,5},{5,4},{6,7},{7,6},{8,9},{9,8},{10,11... | collective-permute-start | bytes 147464 | tf_op jit(solution)/shard_map/ppermute | solution.py:286
  101.0 17.7 %collective-permute-start.7 = (f32[3,16,1,256]{3,2,1,0:T(1,128)}, f32[3,16,1,256]{3,2,1,0:T(1,128)}, u32[]{:S(2)}, u32[]{:S(2)}) collective-permute-start(f32[3,16,1,256]{3,2,1,0:T(1,128)} %get-tuple-element.38), channel_id=1, source_target_pairs={{1,0},{0,1},{3,2},{2,3},{5,4},{4,5},{7,6},{6,7},{9,8},{8,9},{11,10... | collective-permute-start | bytes 147464 | tf_op jit(solution)/shard_map/ppermute | solution.py:286
  101.0 17.7 %collective-permute-start.4 = (f32[3,1,64,256]{3,2,1,0:T(8,128)}, f32[3,1,64,256]{3,2,1,0:T(8,128)}, u32[]{:S(2)}, u32[]{:S(2)}) collective-permute-start(f32[3,1,64,256]{3,2,1,0:T(8,128)} %get-tuple-element.35), channel_id=1, source_target_pairs={{0,2},{2,4},{4,6},{6,8},{8,10},{10,12},{12,14},{14,16},{16,18},{18... | collective-permute-start | bytes 589832 | tf_op jit(solution)/shard_map/ppermute | solution.py:286
  105.0 13.7 %collective-permute-start.5 = (f32[3,1,64,256]{3,2,1,0:T(8,128)}, f32[3,1,64,256]{3,2,1,0:T(8,128)}, u32[]{:S(2)}, u32[]{:S(2)}) collective-permute-start(f32[3,1,64,256]{3,2,1,0:T(8,128)} %get-tuple-element.36), channel_id=1, source_target_pairs={{2,0},{4,2},{6,4},{8,6},{10,8},{12,10},{14,12},{16,14},{18,16},{20... | collective-permute-start | bytes 589832 | tf_op jit(solution)/shard_map/ppermute | solution.py:286
  140.0 4.1 %copy-start.11 = (f32[80]{0:T(128)S(1)}, f32[80]{0:T(128)}, u32[]{:S(2)}) copy-start(f32[80]{0:T(128)} %param.21) | copy-start | bytes 964
  140.0 4.1 %copy-start.13 = (f32[80]{0:T(128)S(1)}, f32[80]{0:T(128)}, u32[]{:S(2)}) copy-start(f32[80]{0:T(128)} %copy-done.12) | copy-start | bytes 964
  140.0 4.1 %copy-start.17 = (f32[80]{0:T(128)S(1)}, f32[80]{0:T(128)}, u32[]{:S(2)}) copy-start(f32[80]{0:T(128)} %param.22) | copy-start | bytes 964
  (6 other events, 7.1 us)

commit v12 on v10

--- a/solution.py
+++ b/solution.py
@@ -201,7 +201,7 @@
             )
             if c == 0:
                 update = update - drag * center
-            final = update * scale
+            final = update if exchange else update * scale
             out_ref[c, x] = final
             first_row[c, x] = final[0:1, :]
             last_row[c, x] = final[width_y - 1 :, :]
@@ -346,6 +346,7 @@
             turbine, gradient_block, step_index == steps_total - 1,
         )
         edges = ((first_plane, last_plane), (first_row, last_row))
+    adjoint = adjoint * fringe_scale[None, :, None, None]
     gradient_sum = gradient_block[0, : thrust.shape[0]]
     cosine = jnp.cos(yaw_angle)
     sine = jnp.sin(yaw_angle)

time: 146 us -> 146 us (level)
  other arithmetic: 5.35 us -> 9.41 us
  local copies, waits for them, and re-layouts: 25.3 us -> 21.4 us
    mul x0 -> x1, other arithmetic: none -> 4.06 us  [shards(): adjoint = adjoint * fringe_scale[None, :, None, None]]
    unnamed x42 -> x41, local copies, waits for them, and re-layouts: 6.64 us -> 2.74 us
where the time goes in v12:
time: 146 us; the launch traced here: 145 us
  Pallas kernels  39 us (27%)
  waiting for transfers between devices  30.8 us (21%)
  starting transfers between devices  29.1 us (20%)
  local copies, waits for them, and re-layouts  21.4 us (15%)
  matrix products  14.2 us (10%)
  other arithmetic  9.41 us (6%)
    pallas_call x2, Pallas kernels, advance(): pl.pallas_call(functools.partial(advance_kernel, count_y, group, exchange...  39 us
    all_to_all x2, waiting for transfers between devices, shards(): lax.all_to_all(packed, ('gx', 'gy'), split_axis=0, concat_axis=0, tiled=T...  30.8 us
    all_to_all x2, starting transfers between devices, shards(): lax.all_to_all(packed, ('gx', 'gy'), split_axis=0, concat_axis=0, tiled=T...  18 us
    convert_element_type x2, local copies, waits for them, and re-layouts, shards(): packed = jnp.einsum('drs,scb->dcrb', pack_table, stored, preferred_elemen...  9.8 us
    dot_general x2, matrix products, shards(): jnp.einsum('scrb,jsr->cjb', arrived, pick_table, preferred_element_type=j...  8.33 us
    ppermute x4, starting transfers between devices, halo(): lax.ppermute(last, axis, forward)  8.02 us
    convert_element_type x2, local copies, waits for them, and re-layouts, shards(): forward.reshape(components, width_x, width_y, height).astype(jnp.bfloat16)  5.16 us
    dot_general x2, matrix products, shards(): jnp.einsum('drs,scb->dcrb', pack_table, stored, preferred_element_type=jn...  4.84 us
  transfers between devices with their start and end apart: 10, of which 2 were waited for; matrix products, arithmetic and copies ran while one was open for 19% of the time, Pallas kernels for 13%

profile of v12, /device:TPU:1, one launch (start us, length us, event | category | flops | bytes accessed | tf_op | source)
XLA Modules:
  0.0 145.0 jit_solution(7845443888377387158)
XLA Ops:
  1.6 0.8 select_reduce_fusion
  3.1 2.4 %fusion.4 = bf16[128,3,2,2048]{3,0,1,2:T(8,128)(2,1)S(1)} fusion(bf16[2,128,3,2048]{3,1,2,0:T(8,128)(2,1)} %param.16, s32[128]{0:T(128)S(1)} %add_add_fusion, s32[128,2]{0,1:T(2,128)S(1)} %multiply_add_fusion), kind=kOutput, calls=%fused_computation.8 | convolution fusion | flops 404258816 | bytes 4720128 | tf_op jit(solution)/shard_map/drs,scb->dcrb/dot_general | solution.py:334
  5.5 4.9 %copy.21 = bf16[128,3,2,2048]{3,2,1,0:T(2,128)(2,1)} copy(bf16[128,3,2,2048]{3,0,1,2:T(8,128)(2,1)S(1)} %fusion.4) | data formatting | bytes 6291456 | tf_op jit(solution)/shard_map/convert_element_type | solution.py:336
  10.4 11.5 %all-to-all-start = ((bf16[128,3,2,2048]{3,2,1,0:T(2,128)(2,1)}), bf16[128,3,2,2048]{3,2,1,0:T(2,128)(2,1)S(1)}, u32[]{:S(2)}, u32[]{:S(2)}) async-start(bf16[128,3,2,2048]{3,2,1,0:T(2,128)(2,1)} %copy.21), calls=%async_computation | async-start | bytes 6291456 | tf_op jit(solution)/shard_map/all_to_all | solution.py:337
  21.9 1.8 %fusion.54 = (f32[3,16,1,256]{3,2,1,0:T(1,128)}, f32[3,16,1,256]{3,2,1,0:T(1,128)}) fusion(f32[3,16,64,256]{3,2,1,0:T(8,128)} %refs_2_.1), kind=kLoop, calls=%fused_computation.77 | loop fusion | bytes 196608 | tf_op jit(solution)/shard_map/slice | solution.py:330
  23.7 1.5 %collective-permute-start.3 = (f32[3,16,1,256]{3,2,1,0:T(1,128)}, f32[3,16,1,256]{3,2,1,0:T(1,128)}, u32[]{:S(2)}, u32[]{:S(2)}) collective-permute-start(f32[3,16,1,256]{3,2,1,0:T(1,128)} %get-tuple-element.42), channel_id=1, source_target_pairs={{1,0},{0,1},{3,2},{2,3},{5,4},{4,5},{7,6},{6,7},{9,8},{8,9},{11,10... | collective-permute-start | bytes 147464 | tf_op jit(solution)/shard_map/ppermute | solution.py:286
  25.3 1.8 %fusion.55 = (f32[3,1,64,256]{3,2,1,0:T(8,128)}, f32[3,1,64,256]{3,2,1,0:T(8,128)}) fusion(f32[3,16,64,256]{3,2,1,0:T(8,128)} %refs_2_.1), kind=kLoop, calls=%fused_computation.78 | loop fusion | bytes 786432 | tf_op jit(solution)/shard_map/slice | solution.py:329
  27.1 1.6 %collective-permute-start.1 = (f32[3,1,64,256]{3,2,1,0:T(8,128)}, f32[3,1,64,256]{3,2,1,0:T(8,128)}, u32[]{:S(2)}, u32[]{:S(2)}) collective-permute-start(f32[3,1,64,256]{3,2,1,0:T(8,128)} %get-tuple-element.44), channel_id=1, source_target_pairs={{2,0},{4,2},{6,4},{8,6},{10,8},{12,10},{14,12},{16,14},{18,16},{20... | collective-permute-start | bytes 589832 | tf_op jit(solution)/shard_map/ppermute | solution.py:286
  28.6 2.5 %collective-permute-start = (f32[3,1,64,256]{3,2,1,0:T(8,128)}, f32[3,1,64,256]{3,2,1,0:T(8,128)}, u32[]{:S(2)}, u32[]{:S(2)}) collective-permute-start(f32[3,1,64,256]{3,2,1,0:T(8,128)} %get-tuple-element.45), channel_id=1, source_target_pairs={{0,2},{2,4},{4,6},{6,8},{8,10},{10,12},{12,14},{14,16},{16,18},{18... | collective-permute-start | bytes 589832 | tf_op jit(solution)/shard_map/ppermute | solution.py:286
  31.2 2.4 %fusion.5 = bf16[128,3,2,2048]{3,0,1,2:T(8,128)(2,1)S(1)} fusion(bf16[2,128,3,2048]{3,1,2,0:T(8,128)(2,1)} %param.16, s32[128]{0:T(128)S(1)} %add_add_fusion, s32[128,2]{0,1:T(2,128)S(1)} %multiply_add_fusion), kind=kOutput, calls=%fused_computation.9 | convolution fusion | flops 404258816 | bytes 4720128 | tf_op jit(solution)/shard_map/drs,scb->dcrb/dot_general | solution.py:334
  33.7 4.9 %copy.24 = bf16[128,3,2,2048]{3,2,1,0:T(2,128)(2,1)} copy(bf16[128,3,2,2048]{3,0,1,2:T(8,128)(2,1)S(1)} %fusion.5) | data formatting | bytes 6291456 | tf_op jit(solution)/shard_map/convert_element_type | solution.py:336
  38.6 24.9 %all-to-all-done = bf16[128,3,2,2048]{3,2,1,0:T(2,128)(2,1)S(1)} async-done(((bf16[128,3,2,2048]{3,2,1,0:T(2,128)(2,1)}), bf16[128,3,2,2048]{3,2,1,0:T(2,128)(2,1)S(1)}, u32[]{:S(2)}, u32[]{:S(2)}) %all-to-all-start) | async-done | bytes 3145760 | tf_op jit(solution)/shard_map/all_to_all | solution.py:337
  63.4 6.5 %all-to-all-start.1 = ((bf16[128,3,2,2048]{3,2,1,0:T(2,128)(2,1)}), bf16[128,3,2,2048]{3,2,1,0:T(2,128)(2,1)}, u32[]{:S(2)}, u32[]{:S(2)}) async-start(bf16[128,3,2,2048]{3,2,1,0:T(2,128)(2,1)} %copy.24), calls=%async_computation.1 | async-start | bytes 6291456 | tf_op jit(solution)/shard_map/all_to_all | solution.py:337
  72.5 1.0 fusion.29.refs_8_
  73.6 3.2 %fusion.10 = bf16[3,128,2048]{2,1,0:T(8,128)(2,1)} fusion(bf16[128,3,2,2048]{3,2,1,0:T(2,128)(2,1)S(1)} %copy-done.6, s32[128,2]{0,1:T(2,128)S(1)} %copy-done.8, s32[128]{0:T(128)S(1)} %copy-done.14), kind=kOutput, calls=%fused_computation.10 | convolution fusion | flops 403472384 | bytes 4720128 | tf_op jit(solution)/shard_map/scrb,jsr->cjb/dot_general | solution.py:338
  76.7 2.6 %convert_element_type.40.refs_7_ = bf16[3,16,64,256]{3,2,1,0:T(8,128)(2,1)S(1)} reshape(bf16[3,128,2048]{2,1,0:T(8,128)(2,1)} %fusion.10) | data formatting | bytes 3145728 | tf_op jit(solution)/shard_map/convert_element_type | solution.py:341
  80.1 19.0 %shard_map.122 = (f32[3,16,64,256]{3,2,1,0:T(8,128)}, f32[8,128]{1,0:T(8,128)S(1)}, f32[3,1,64,256]{3,2,1,0:T(8,128)}, f32[3,1,64,256]{3,2,1,0:T(8,128)}, f32[3,...) custom-call(s32[32,8]{1,0:T(8,128)S(1)} %copy.26.refs_0_, f32[16]{0:T(128)S(1)} %copy-done.1, f32[3,16,64,256]{3,2,1,0:T(8,128)} %refs_2_.1, ...), custom_call_target="tpu_custom_call" | custom-call | tf_op jit(solution)/shard_map/pallas_call | solution.py:261
  99.6 1.5 %collective-permute-start.6 = (f32[3,16,1,256]{3,2,1,0:T(1,128)}, f32[3,16,1,256]{3,2,1,0:T(1,128)}, u32[]{:S(2)}, u32[]{:S(2)}) collective-permute-start(f32[3,16,1,256]{3,2,1,0:T(1,128)} %get-tuple-element.37), channel_id=1, source_target_pairs={{0,1},{1,0},{2,3},{3,2},{4,5},{5,4},{6,7},{7,6},{8,9},{9,8},{10,11... | collective-permute-start | bytes 147464 | tf_op jit(solution)/shard_map/ppermute | solution.py:286
  101.2 4.0 %collective-permute-start.4 = (f32[3,1,64,256]{3,2,1,0:T(8,128)}, f32[3,1,64,256]{3,2,1,0:T(8,128)}, u32[]{:S(2)}, u32[]{:S(2)}) collective-permute-start(f32[3,1,64,256]{3,2,1,0:T(8,128)} %get-tuple-element.35), channel_id=1, source_target_pairs={{0,2},{2,4},{4,6},{6,8},{8,10},{10,12},{12,14},{14,16},{16,18},{18... | collective-permute-start | bytes 589832 | tf_op jit(solution)/shard_map/ppermute | solution.py:286
  105.2 5.9 %all-to-all-done.1 = bf16[128,3,2,2048]{3,2,1,0:T(2,128)(2,1)} async-done(((bf16[128,3,2,2048]{3,2,1,0:T(2,128)(2,1)}), bf16[128,3,2,2048]{3,2,1,0:T(2,128)(2,1)}, u32[]{:S(2)}, u32[]{:S(2)}) %all-to-all-start.1) | async-done | bytes 3145760 | tf_op jit(solution)/shard_map/all_to_all | solution.py:337
  111.1 5.1 %fusion.13 = bf16[3,128,2048]{2,1,0:T(8,128)(2,1)} fusion(bf16[128,3,2,2048]{3,2,1,0:T(2,128)(2,1)} %all-to-all-done.1, s32[128,2]{0,1:T(2,128)} %copy-done.7, s32[128]{0:T(128)} %param.18), kind=kOutput, calls=%fused_computation.11 | convolution fusion | flops 403472384 | bytes 4720128 | tf_op jit(solution)/shard_map/scrb,jsr->cjb/dot_general | solution.py:338
  116.3 2.6 %convert_element_type.46.refs_7_ = bf16[3,16,64,256]{3,2,1,0:T(8,128)(2,1)S(1)} reshape(bf16[3,128,2048]{2,1,0:T(8,128)(2,1)} %fusion.13) | data formatting | bytes 3145728 | tf_op jit(solution)/shard_map/convert_element_type | solution.py:341
  120.3 20.0 %shard_map.123 = (f32[3,16,64,256]{3,2,1,0:T(8,128)}, f32[8,128]{1,0:T(8,128)S(1)}, f32[3,1,64,256]{3,2,1,0:T(8,128)}, f32[3,1,64,256]{3,2,1,0:T(8,128)}, f32[3,...) custom-call(s32[32,8]{1,0:T(8,128)S(1)} %copy.26.refs_0_, f32[16]{0:T(128)S(1)} %copy-done.2, ...), custom_call_target="tpu_custom_call" | custom-call | tf_op jit(solution)/shard_map/pallas_call | solution.py:261
  140.3 4.1 %broadcast_multiply_fusion = f32[3,16,64,256]{3,2,1,0:T(8,128)} fusion(f32[3,16,64,256]{3,2,1,0:T(8,128)} %get-tuple-element.40, f32[16]{0:T(128)S(1)} %copy-done.2), kind=kLoop, calls=%fused_computation.14 | loop fusion | flops 786432 | bytes 6291520 | tf_op jit(solution)/shard_map/mul | solution.py:349
  (75 shorter events, 7.4 us)
Async XLA Ops:
  0.6 30.6 %copy-start.7 = (s32[128,2]{0,1:T(2,128)}, s32[128,2]{0,1:T(2,128)S(1)}, u32[]{:S(2)}) copy-start(s32[128,2]{0,1:T(2,128)S(1)} %multiply_add_fusion) | copy-start | bytes 3076
  10.4 20.7 %copy-start.17 = (f32[80]{0:T(128)S(1)}, f32[80]{0:T(128)}, u32[]{:S(2)}) copy-start(f32[80]{0:T(128)} %param.22) | copy-start | bytes 964
  10.4 20.8 %copy-start.9 = (s32[32,8]{0,1:T(8,128)S(1)}, s32[32,8]{0,1:T(8,128)}, u32[]{:S(2)}) copy-start(s32[32,8]{0,1:T(8,128)} %param.19) | copy-start | bytes 3076
  10.4 53.0 %all-to-all-start = ((bf16[128,3,2,2048]{3,2,1,0:T(2,128)(2,1)}), bf16[128,3,2,2048]{3,2,1,0:T(2,128)(2,1)S(1)}, u32[]{:S(2)}, u32[]{:S(2)}) async-start(bf16[128,3,2,2048]{3,2,1,0:T(2,128)(2,1)} %copy.21), calls=%async_computation | async-start | bytes 6291456 | tf_op jit(solution)/shard_map/all_to_all | solution.py:337
  23.7 55.6 %collective-permute-start.3 = (f32[3,16,1,256]{3,2,1,0:T(1,128)}, f32[3,16,1,256]{3,2,1,0:T(1,128)}, u32[]{:S(2)}, u32[]{:S(2)}) collective-permute-start(f32[3,16,1,256]{3,2,1,0:T(1,128)} %get-tuple-element.42), channel_id=1, source_target_pairs={{1,0},{0,1},{3,2},{2,3},{5,4},{4,5},{7,6},{6,7},{9,8},{8,9},{11,10... | collective-permute-start | bytes 147464 | tf_op jit(solution)/shard_map/ppermute | solution.py:286
  25.2 54.1 %collective-permute-start.2 = (f32[3,16,1,256]{3,2,1,0:T(1,128)}, f32[3,16,1,256]{3,2,1,0:T(1,128)}, u32[]{:S(2)}, u32[]{:S(2)}) collective-permute-start(f32[3,16,1,256]{3,2,1,0:T(1,128)} %get-tuple-element.43), channel_id=1, source_target_pairs={{0,1},{1,0},{2,3},{3,2},{4,5},{5,4},{6,7},{7,6},{8,9},{9,8},{10,11... | collective-permute-start | bytes 147464 | tf_op jit(solution)/shard_map/ppermute | solution.py:286
  27.1 52.3 %collective-permute-start.1 = (f32[3,1,64,256]{3,2,1,0:T(8,128)}, f32[3,1,64,256]{3,2,1,0:T(8,128)}, u32[]{:S(2)}, u32[]{:S(2)}) collective-permute-start(f32[3,1,64,256]{3,2,1,0:T(8,128)} %get-tuple-element.44), channel_id=1, source_target_pairs={{2,0},{4,2},{6,4},{8,6},{10,8},{12,10},{14,12},{16,14},{18,16},{20... | collective-permute-start | bytes 589832 | tf_op jit(solution)/shard_map/ppermute | solution.py:286
  28.6 50.7 %collective-permute-start = (f32[3,1,64,256]{3,2,1,0:T(8,128)}, f32[3,1,64,256]{3,2,1,0:T(8,128)}, u32[]{:S(2)}, u32[]{:S(2)}) collective-permute-start(f32[3,1,64,256]{3,2,1,0:T(8,128)} %get-tuple-element.45), channel_id=1, source_target_pairs={{0,2},{2,4},{4,6},{6,8},{8,10},{10,12},{12,14},{14,16},{16,18},{18... | collective-permute-start | bytes 589832 | tf_op jit(solution)/shard_map/ppermute | solution.py:286
  31.2 38.8 %copy-start.12 = (f32[80]{0:T(128)}, f32[80]{0:T(128)S(1)}, u32[]{:S(2)}) copy-start(f32[80]{0:T(128)S(1)} %cos.4) | copy-start | bytes 964
  38.6 31.3 %copy-start.16 = (s32[80]{0:T(128)S(1)}, s32[80]{0:T(128)}, u32[]{:S(2)}) copy-start(s32[80]{0:T(128)} %param.24) | copy-start | bytes 964
  38.6 31.4 %copy-start.10 = (f32[80]{0:T(128)S(1)}, f32[80]{0:T(128)}, u32[]{:S(2)}) copy-start(f32[80]{0:T(128)} %param.21) | copy-start | bytes 964
  38.6 31.4 %copy-start.15 = (f32[3,80]{1,0:T(4,128)S(1)}, f32[3,80]{1,0:T(4,128)}, u32[]{:S(2)}) copy-start(f32[3,80]{1,0:T(4,128)} %param.23) | copy-start | bytes 2884
  63.4 6.5 %copy-start.5 = (bf16[128,3,2,2048]{3,2,1,0:T(2,128)(2,1)}, bf16[128,3,2,2048]{3,2,1,0:T(2,128)(2,1)S(1)}, u32[]{:S(2)}) copy-start(bf16[128,3,2,2048]{3,2,1,0:T(2,128)(2,1)S(1)} %all-to-all-done) | copy-start | bytes 9437188
  63.4 47.7 %all-to-all-start.1 = ((bf16[128,3,2,2048]{3,2,1,0:T(2,128)(2,1)}), bf16[128,3,2,2048]{3,2,1,0:T(2,128)(2,1)}, u32[]{:S(2)}, u32[]{:S(2)}) async-start(bf16[128,3,2,2048]{3,2,1,0:T(2,128)(2,1)} %copy.24), calls=%async_computation.1 | async-start | bytes 6291456 | tf_op jit(solution)/shard_map/all_to_all | solution.py:337
  69.9 3.6 %copy-start.8 = (s32[128,2]{0,1:T(2,128)S(1)}, s32[128,2]{0,1:T(2,128)}, u32[]{:S(2)}) copy-start(s32[128,2]{0,1:T(2,128)} %copy-done.7) | copy-start | bytes 3076
  69.9 3.6 %copy-start.14 = (s32[128]{0:T(128)S(1)}, s32[128]{0:T(128)}, u32[]{:S(2)}) copy-start(s32[128]{0:T(128)} %param.18) | copy-start | bytes 1540
  73.5 5.8 %copy-start = (bf16[8,128,128]{2,1,0:T(8,128)(2,1)S(1)}, bf16[8,128,128]{2,1,0:T(8,128)(2,1)}, u32[]{:S(2)}) copy-start(bf16[8,128,128]{2,1,0:T(8,128)(2,1)} %param.20) | copy-start | bytes 786436
  99.6 19.2 %collective-permute-start.6 = (f32[3,16,1,256]{3,2,1,0:T(1,128)}, f32[3,16,1,256]{3,2,1,0:T(1,128)}, u32[]{:S(2)}, u32[]{:S(2)}) collective-permute-start(f32[3,16,1,256]{3,2,1,0:T(1,128)} %get-tuple-element.37), channel_id=1, source_target_pairs={{0,1},{1,0},{2,3},{3,2},{4,5},{5,4},{6,7},{7,6},{8,9},{9,8},{10,11... | collective-permute-start | bytes 147464 | tf_op jit(solution)/shard_map/ppermute | solution.py:286
  101.1 17.7 %collective-permute-start.7 = (f32[3,16,1,256]{3,2,1,0:T(1,128)}, f32[3,16,1,256]{3,2,1,0:T(1,128)}, u32[]{:S(2)}, u32[]{:S(2)}) collective-permute-start(f32[3,16,1,256]{3,2,1,0:T(1,128)} %get-tuple-element.38), channel_id=1, source_target_pairs={{1,0},{0,1},{3,2},{2,3},{5,4},{4,5},{7,6},{6,7},{9,8},{8,9},{11,10... | collective-permute-start | bytes 147464 | tf_op jit(solution)/shard_map/ppermute | solution.py:286
  101.2 17.7 %collective-permute-start.4 = (f32[3,1,64,256]{3,2,1,0:T(8,128)}, f32[3,1,64,256]{3,2,1,0:T(8,128)}, u32[]{:S(2)}, u32[]{:S(2)}) collective-permute-start(f32[3,1,64,256]{3,2,1,0:T(8,128)} %get-tuple-element.35), channel_id=1, source_target_pairs={{0,2},{2,4},{4,6},{6,8},{8,10},{10,12},{12,14},{14,16},{16,18},{18... | collective-permute-start | bytes 589832 | tf_op jit(solution)/shard_map/ppermute | solution.py:286
  105.2 13.7 %collective-permute-start.5 = (f32[3,1,64,256]{3,2,1,0:T(8,128)}, f32[3,1,64,256]{3,2,1,0:T(8,128)}, u32[]{:S(2)}, u32[]{:S(2)}) collective-permute-start(f32[3,1,64,256]{3,2,1,0:T(8,128)} %get-tuple-element.36), channel_id=1, source_target_pairs={{2,0},{4,2},{6,4},{8,6},{10,8},{12,10},{14,12},{16,14},{18,16},{20... | collective-permute-start | bytes 589832 | tf_op jit(solution)/shard_map/ppermute | solution.py:286
  140.2 4.1 %copy-start.11 = (f32[80]{0:T(128)S(1)}, f32[80]{0:T(128)}, u32[]{:S(2)}) copy-start(f32[80]{0:T(128)} %param.21) | copy-start | bytes 964
  140.3 4.1 %copy-start.13 = (f32[80]{0:T(128)S(1)}, f32[80]{0:T(128)}, u32[]{:S(2)}) copy-start(f32[80]{0:T(128)} %copy-done.12) | copy-start | bytes 964
  140.3 4.1 %copy-start.18 = (f32[80]{0:T(128)S(1)}, f32[80]{0:T(128)}, u32[]{:S(2)}) copy-start(f32[80]{0:T(128)} %param.22) | copy-start | bytes 964
  (6 other events, 7.2 us)
